TPU v7x, 128 devices: a whole 4x4x4 slice. The times are simulated.
128 devices in a mesh: grp: 32 (over y, z, core), feat: 4 (over x).
Axes of the slice: x: 4, y: 4, z: 4, core: 2. Of those that a mesh axis runs over, the one named last changes fastest.
Arguments:
- hot_table: bfloat16 [16384, 1024], P(None, 'feat'), may hold values from -6 to 6
- cold_table: bfloat16 [131072, 1024], P('grp', 'feat'), may hold values from -6 to 6
- send_blocks: int32 [32, 32, 6], P('grp'), may hold values from 0 to 31
- block_counts: int32 [32, 32], P('grp'), may hold values from 1 to 6
- self_ref: int32 [90112], P('grp'), may hold values from 0 to 40959
- neigh_ref: int32 [90112, 10], P('grp'), may hold values from 0 to 40959
- route_owner: int32 [81920, 1], P('grp'), may hold values from 0 to 31; in each aligned block of 2560 rows (0 to 2559, 2560 to 5119, ...) at most 160 rows name the same one
- route_slot: int32 [81920], P('grp'), may hold values from 0 to 255
- w1_self: bfloat16 [1024, 512], P('feat'), may hold values from -0.1875 to 0.1875
- w1_neigh: bfloat16 [1024, 512], P('feat'), may hold values from -0.1875 to 0.1875
- b1_bias: float32 [512], P('feat'), may hold values from -3 to 3
- w2_self: bfloat16 [512, 512], P('feat'), may hold values from -0.25 to 0.25
- w2_neigh: bfloat16 [512, 512], P('feat'), may hold values from -0.25 to 0.25
- b2_bias: float32 [512], P('feat'), may hold values from -3 to 3
Outputs:
- embedding: bfloat16 [8192, 512], P('grp', 'feat')
Inputs may be any that keep to these rules, and one draw needn't show every extreme that they name: `route_owner`: in every draw some index of grp sends exactly 160 routed rows to one owner.
All inputs are finite; a program needn't handle non-finite values.
Results may differ from a plain program's by a relative error of at most 0.0047.
Values may be sent and summed in bfloat16 or wider, within the bound.
No kernel may reach another device: no remote copies, remote signals or barrier semaphores. Data moves between devices by JAX's collectives and lax.ppermute only.
A program may use at most 192 MiB of HBM per device.

v0:
```python
import jax
import jax.numpy as jnp
from jax import lax
from jax.sharding import PartitionSpec as P

BLK = 128
S1 = 10


def per_device(
    hot_table,
    cold_table,
    send_blocks,
    block_counts,
    self_ref,
    neigh_ref,
    route_owner,
    route_slot,
    w1_self,
    w1_neigh,
    b1_bias,
    w2_self,
    w2_neigh,
    b2_bias,
):
    groups = lax.axis_size("grp")
    feat_cols = cold_table.shape[1]
    slot_count = send_blocks.shape[2]
    cold_local = cold_table.reshape(-1, BLK, feat_cols)
    outgoing = cold_local[send_blocks[0]]
    valid = jnp.arange(slot_count, dtype=jnp.int32)[None, :] < block_counts[0][:, None]
    outgoing = jnp.where(valid[:, :, None, None], outgoing, jnp.zeros_like(outgoing))
    fetched = lax.all_to_all(outgoing, "grp", split_axis=0, concat_axis=0, tiled=True)
    cold_rows = fetched.reshape(-1, feat_cols)
    table = jnp.concatenate([hot_table, cold_rows], axis=0)
    self_x = table[self_ref]
    neigh_total = jnp.sum(table[neigh_ref], axis=1, dtype=jnp.float32)
    neigh_x = (neigh_total / S1).astype(jnp.bfloat16)
    hidden_cols = b1_bias.shape[0]
    partial_value = jnp.dot(self_x, w1_self, preferred_element_type=jnp.float32) + jnp.dot(
        neigh_x, w1_neigh, preferred_element_type=jnp.float32
    )
    summed = lax.psum(partial_value, "feat")
    pre = lax.dynamic_slice_in_dim(summed, lax.axis_index("feat") * hidden_cols, hidden_cols, 1)
    h1 = jnp.maximum(pre + b1_bias, 0.0).astype(jnp.bfloat16)
    targets = h1.shape[0] - route_slot.shape[0]
    own_rows = h1[:targets]
    routed = h1[targets:]
    owner = route_owner[:, 0]
    capacity = 2 * routed.shape[0] // groups
    onehot_owner = (owner[:, None] == jnp.arange(groups, dtype=jnp.int32)[None, :]).astype(
        jnp.int32
    )
    position = jnp.sum((jnp.cumsum(onehot_owner, axis=0) - 1) * onehot_owner, axis=1)
    place = owner * capacity + position
    send_rows = jnp.zeros((groups * capacity, hidden_cols), jnp.bfloat16).at[place].set(routed)
    send_slots = jnp.full((groups * capacity,), -1, jnp.int32).at[place].set(route_slot)
    recv_rows, recv_slots = (
        lax.all_to_all(
            send_rows.reshape(groups, capacity, hidden_cols),
            "grp",
            split_axis=0,
            concat_axis=0,
            tiled=True,
        ),
        lax.all_to_all(
            send_slots.reshape(groups, capacity), "grp", split_axis=0, concat_axis=0, tiled=True
        ),
    )
    recv_rows = recv_rows.reshape(groups * capacity, hidden_cols)
    recv_slots = recv_slots.reshape(groups * capacity)
    member = jnp.arange(targets, dtype=jnp.int32)[:, None] == recv_slots[None, :]
    total = jnp.dot(member.astype(jnp.bfloat16), recv_rows, preferred_element_type=jnp.float32)
    count = jnp.sum(member.astype(jnp.float32), axis=1)
    neigh_h = (total / jnp.maximum(count, 1.0)[:, None]).astype(jnp.bfloat16)
    partial_two = jnp.dot(own_rows, w2_self, preferred_element_type=jnp.float32) + jnp.dot(
        neigh_h, w2_neigh, preferred_element_type=jnp.float32
    )
    shared = lax.psum_scatter(partial_two, "feat", scatter_dimension=1, tiled=True)
    return (shared + b2_bias).astype(jnp.bfloat16)


def solution(mesh):
    in_specs = (
        P(None, "feat"),
        P("grp", "feat"),
        P("grp", None, None),
        P("grp", None),
        P("grp"),
        P("grp", None),
        P("grp", None),
        P("grp"),
        P("feat", None),
        P("feat", None),
        P("feat"),
        P("feat", None),
        P("feat", None),
        P("feat"),
    )
    out_specs = P("grp", "feat")
    return jax.shard_map(
        per_device, mesh=mesh, in_specs=in_specs, out_specs=out_specs, check_vma=False
    )
```

profile of v0, /device:TPU:0, one launch (start us, length us, event | category | flops | bytes accessed | tf_op | source)
XLA Modules:
  0.0 589.9 jit_solution(16499131093047876776)
XLA Ops:
  6.5 0.8 compare_select_fusion.3
  7.6 0.7 iota_compare_fusion.10
  8.3 8.2 %gather_fusion = bf16[192,128,256]{2,1,0:T(8,128)(2,1)} fusion(bf16[32,128,256]{2,1,0:T(8,128)(2,1)S(1)} %bitcast.33, s32[1024]{0:T(1024)S(1)} %pad_clamp_fusion.2), kind=kCustom, calls=%fused_computation | custom fusion | bytes 25166592 | tf_op jit(solution)/shard_map/gather | solution.py:30
  16.5 10.6 %broadcast_select_fusion = bf16[32,6,128,256]{3,2,1,0:T(8,128)(2,1)} fusion(bf16[32,6,128,256]{3,2,1,0:T(8,128)(2,1)} %bitcast.34, pred[32,6]{1,0:T(8,128)(4,1)S(1)} %iota_compare_fusion.10), kind=kLoop, calls=%fused_computation.6 | loop fusion | flops 6291456 | bytes 25166016 | tf_op jit(solution)/shard_map/jit(_where)/select_n | solution.py:32
  27.1 8.7 %all-to-all-start = ((bf16[32,6,128,256]{3,2,1,0:T(8,128)(2,1)}), bf16[32,6,128,256]{3,2,1,0:T(8,128)(2,1)}, u32[]{:S(2)}, u32[]{:S(2)}) async-start(bf16[32,6,128,256]{3,2,1,0:T(8,128)(2,1)} %broadcast_select_fusion), calls=%async_computation | async-start | bytes 25165824 | tf_op jit(solution)/shard_map/all_to_all | solution.py:33
  35.9 0.5 copy.20
  36.4 1.1 reshape.117
  37.5 175.6 %all-to-all-done = bf16[32,6,128,256]{3,2,1,0:T(8,128)(2,1)} async-done(((bf16[32,6,128,256]{3,2,1,0:T(8,128)(2,1)}), bf16[32,6,128,256]{3,2,1,0:T(8,128)(2,1)}, u32[]{:S(2)}, u32[]{:S(2)}) %all-to-all-start) | async-done | bytes 12582944 | tf_op jit(solution)/shard_map/all_to_all | solution.py:33
  213.1 21.5 %pad_maximum_fusion = bf16[40960,256]{1,0:T(8,128)(2,1)} fusion(bf16[24576,256]{1,0:T(8,128)(2,1)} %bitcast.4, bf16[16384,256]{1,0:T(8,128)(2,1)} %param.14), kind=kLoop, calls=%fused_computation.5 | loop fusion | flops 41943040 | bytes 41943040 | tf_op jit(solution)/shard_map/concatenate | solution.py:35
  234.6 15.9 %gather_fusion.1 = bf16[2816,256]{1,0:T(8,128)(2,1)S(1)} fusion(bf16[40960,256]{1,0:T(8,128)(2,1)} %pad_maximum_fusion, s32[3072]{0:T(1024)S(1)} %pad_clamp_fusion.1), kind=kCustom, calls=%fused_computation.1 | custom fusion | bytes 2894848 | tf_op jit(solution)/shard_map/gather | solution.py:36
  250.5 73.4 %gather_fusion.2 = bf16[28160,256]{1,0:T(8,128)(2,1)} fusion(bf16[40960,256]{1,0:T(8,128)(2,1)} %pad_maximum_fusion, s32[28672]{0:T(1024)S(1)} %pad_clamp_fusion), kind=kCustom, calls=%fused_computation.2 | custom fusion | bytes 28948480 | tf_op jit(solution)/shard_map/gather | solution.py:37
  323.9 28.8 %reshape.143 = f32[2816,10,256]{2,1,0:T(8,128)} reshape(bf16[28160,256]{1,0:T(8,128)(2,1)} %gather_fusion.2) | data formatting | bytes 43253760 | tf_op jit(solution)/shard_map/convert_element_type | solution.py:37
  352.8 3.4 fusion.18
  356.1 22.0 %reduce_sum.29 = f32[2816,256]{1,0:T(8,128)} reduce(f32[2816,10,256]{2,1,0:T(8,128)} %reshape.143, f32[]{:T(128)} %constant.17.clone.1), dimensions={1}, to_apply=%region_0.1 | reduce | flops 6488064 | bytes 31719428 | tf_op jit(solution)/shard_map/reduce_sum | solution.py:37
  378.1 6.9 %convolution_add_fusion = f32[2816,512]{1,0:T(8,128)} fusion(f32[2816,512]{1,0:T(8,128)} %fusion.18, bf16[256,512]{1,0:T(8,128)(2,1)S(1)} %copy-done.2, f32[2816,256]{1,0:T(8,128)} %reduce_sum.29), kind=kOutput, calls=%fused_computation.10 | convolution fusion | flops 741081088 | bytes 14680064 | tf_op jit(solution)/shard_map/dot_general | solution.py:40
  385.0 0.7 copy-done.6
  385.8 9.4 %reduce-window.6 = s32[32,20,128]{2,1,0:T(8,128)S(1)} reduce-window(s32[32,20,128]{2,1,0:T(8,128)S(1)} %fusion.8, s32[]{:T(128)} %constant.13.clone.1), window={size=1x1x128 pad=0_0x0_0x127_0}, to_apply=%region_2.3 | reduce-window | flops 10403840 | bytes 655364 | tf_op jit(solution)/shard_map/reduce-window
  395.3 0.3 copy.23
  395.8 0.2 add_add_fusion
  396.1 10.1 %scatter_custom_fusion = s32[5120]{0:T(1024)S(1)} fusion(s32[2560]{0:T(1024)S(1)} %fusion.14, s32[2560]{0:T(1024)} %param.21, s32[]{:T(128)} %constant.22.clone.1), kind=kCustom, calls=%fused_computation.40 | custom fusion | bytes 20992 | tf_op jit(solution)/shard_map/scatter | solution.py:57
  406.2 0.7 all_to_all.13
  407.0 25.4 %all-to-all-start.1 = ((s32[32,1,160]{2,1,0:T(1,128)}), s32[32,1,160]{2,1,0:T(1,128)S(1)}, u32[]{:S(2)}, u32[]{:S(2)}) async-start(s32[32,1,160]{2,1,0:T(1,128)} %all_to_all.13), calls=%async_computation.1 | async-start | bytes 65536 | tf_op jit(solution)/shard_map/all_to_all | solution.py:66
  432.3 90.5 %all-reduce.2.cloned.1.call-done = f32[2816,512]{1,0:T(8,128)} async-done(((f32[2816,512]{1,0:T(8,128)}), f32[2816,512]{1,0:T(8,128)}) %all-reduce.2.cloned.1.call-update) | async-done | bytes 5767184 | tf_op jit(solution)/shard_map/psum | solution.py:43
  522.9 1.7 maximum_convert_fusion
  524.5 8.2 %scatter_custom_fusion.1 = bf16[5120,128]{1,0:T(8,128)(2,1)} fusion(s32[2560]{0:T(1024)S(1)} %fusion.14, bf16[2816,128]{1,0:T(8,128)(2,1)S(1)} %maximum_convert_fusion, bf16[]{:T(256)} %constant.15.clone.1), kind=kCustom, calls=%fused_computation.18 | custom fusion | bytes 1966082 | tf_op jit(solution)/shard_map/scatter | solution.py:56
  532.8 7.4 %all-to-all-start.2 = ((bf16[32,160,128]{2,1,0:T(8,128)(2,1)}), bf16[32,160,128]{2,1,0:T(8,128)(2,1)}, u32[]{:S(2)}, u32[]{:S(2)}) async-start(bf16[32,160,128]{2,1,0:T(8,128)(2,1)} %bitcast.8), calls=%async_computation.2 | async-start | bytes 2621440 | tf_op jit(solution)/shard_map/all_to_all | solution.py:59
  540.4 0.6 convert_reduce_fusion
  541.0 0.2 fusion.11
  541.2 18.7 %all-to-all-done.2 = bf16[32,160,128]{2,1,0:T(8,128)(2,1)} async-done(((bf16[32,160,128]{2,1,0:T(8,128)(2,1)}), bf16[32,160,128]{2,1,0:T(8,128)(2,1)}, u32[]{:S(2)}, u32[]{:S(2)}) %all-to-all-start.2) | async-done | bytes 1310752 | tf_op jit(solution)/shard_map/all_to_all | solution.py:59
  559.9 3.3 convolution_add_fusion.1
  563.2 18.3 %reduce-scatter.2.cloned.1.call-done = f32[256,128]{1,0:T(8,128)} async-done(((f32[256,512]{1,0:T(8,128)}), f32[256,128]{1,0:T(8,128)}) %reduce-scatter.2.cloned.1.call-update) | async-done | bytes 131088 | tf_op jit(solution)/shard_map/reduce_scatter | solution.py:79
  581.5 1.5 add_convert_fusion
  (40 shorter events, 1.1 us)
Async XLA Ops:
  6.5 1.8 copy-start
  27.1 8.7 %copy-start.4 = (s32[2816,10]{0,1:T(8,128)S(1)}, s32[2816,10]{0,1:T(8,128)}, u32[]{:S(2)}) copy-start(s32[2816,10]{0,1:T(8,128)} %param.19) | copy-start | bytes 337924
  27.1 10.4 %copy-start.7 = (s32[2816]{0:T(1024)S(1)}, s32[2816]{0:T(1024)}, u32[]{:S(2)}) copy-start(s32[2816]{0:T(1024)} %param.18) | copy-start | bytes 33796
  27.1 186.0 %all-to-all-start = ((bf16[32,6,128,256]{3,2,1,0:T(8,128)(2,1)}), bf16[32,6,128,256]{3,2,1,0:T(8,128)(2,1)}, u32[]{:S(2)}, u32[]{:S(2)}) async-start(bf16[32,6,128,256]{3,2,1,0:T(8,128)(2,1)} %broadcast_select_fusion), calls=%async_computation | async-start | bytes 25165824 | tf_op jit(solution)/shard_map/all_to_all | solution.py:33
  35.8 487.1 %all-reduce.2.cloned.1.call-start = ((), (), s32[]{:S(2)}) async-start(), calls=%async_computation.4 | async-start | bytes 11534336 | tf_op jit(solution)/shard_map/psum | solution.py:43
  323.9 28.8 %copy-start.3 = (bf16[256,512]{1,0:T(8,128)(2,1)S(1)}, bf16[256,512]{1,0:T(8,128)(2,1)}, u32[]{:S(2)}) copy-start(bf16[256,512]{1,0:T(8,128)(2,1)} %param.22) | copy-start | bytes 786436
  356.1 22.0 %copy-start.2 = (bf16[256,512]{1,0:T(8,128)(2,1)S(1)}, bf16[256,512]{1,0:T(8,128)(2,1)}, u32[]{:S(2)}) copy-start(bf16[256,512]{1,0:T(8,128)(2,1)} %param.23) | copy-start | bytes 786436
  385.0 0.7 copy-start.6
  385.0 137.9 %copy-start.9 = (f32[128]{0:T(128)S(1)}, f32[128]{0:T(128)}, u32[]{:S(2)}) copy-start(f32[128]{0:T(128)} %param.24) | copy-start | bytes 1540
  385.8 155.2 %copy-start.5 = (bf16[128,512]{1,0:T(8,128)(2,1)S(1)}, bf16[128,512]{1,0:T(8,128)(2,1)}, u32[]{:S(2)}) copy-start(bf16[128,512]{1,0:T(8,128)(2,1)} %param.25) | copy-start | bytes 393220
  407.0 125.8 %all-to-all-start.1 = ((s32[32,1,160]{2,1,0:T(1,128)}), s32[32,1,160]{2,1,0:T(1,128)S(1)}, u32[]{:S(2)}, u32[]{:S(2)}) async-start(s32[32,1,160]{2,1,0:T(1,128)} %all_to_all.13), calls=%async_computation.1 | async-start | bytes 65536 | tf_op jit(solution)/shard_map/all_to_all | solution.py:66
  522.9 60.2 %copy-start.1 = (bf16[4096,256]{1,0:T(8,128)(2,1)S(1)}, bf16[4096,256]{1,0:T(8,128)(2,1)}, u32[]{:S(2)}) copy-start(bf16[4096,256]{1,0:T(8,128)(2,1)} %param.15) | copy-start | bytes 6291460
  524.5 57.0 %copy-start.8 = (f32[128]{0:T(128)S(1)}, f32[128]{0:T(128)}, u32[]{:S(2)}) copy-start(f32[128]{0:T(128)} %param.27) | copy-start | bytes 1540
  532.8 27.2 %all-to-all-start.2 = ((bf16[32,160,128]{2,1,0:T(8,128)(2,1)}), bf16[32,160,128]{2,1,0:T(8,128)(2,1)}, u32[]{:S(2)}, u32[]{:S(2)}) async-start(bf16[32,160,128]{2,1,0:T(8,128)(2,1)} %bitcast.8), calls=%async_computation.2 | async-start | bytes 2621440 | tf_op jit(solution)/shard_map/all_to_all | solution.py:59
  540.2 41.4 %reduce-scatter.2.cloned.1.call-start = ((), (), s32[]{:S(2)}) async-start(), calls=%async_computation.5 | async-start | bytes 655360 | tf_op jit(solution)/shard_map/reduce_scatter | solution.py:79
Sparse Core Ops, SparseCore 0:
  385.2 137.6 all-reduce.1
  563.3 18.1 reduce-scatter.1
where the time goes:
time: 592 us; the launch traced here: 590 us
  waiting for transfers between devices  303 us (51%)
  local copies, waits for them, and re-layouts  148 us (25%)
  other arithmetic  69.5 us (12%)
  starting transfers between devices  41.5 us (7%)
  matrix products  13.7 us (2%)
  between operations  13.6 us (2%)
    all_to_all x1, waiting for transfers between devices, per_device(): lax.all_to_all(outgoing, 'grp', split_axis=0, concat_axis=0, tiled=True)  176 us
    psum x1, waiting for transfers between devices, per_device(): summed = lax.psum(partial_value, 'feat')  90.5 us
    gather x1, local copies, waits for them, and re-layouts, per_device(): neigh_total = jnp.sum(table[neigh_ref], axis=1, dtype=jnp.float32)  73.4 us
    convert_element_type x1, local copies, waits for them, and re-layouts, per_device(): neigh_total = jnp.sum(table[neigh_ref], axis=1, dtype=jnp.float32)  28.8 us
    all_to_all x1, starting transfers between devices, per_device(): lax.all_to_all(send_slots.reshape(groups, capacity), 'grp', split_axis=0,...  25.4 us
    reduce_sum x1, other arithmetic, per_device(): neigh_total = jnp.sum(table[neigh_ref], axis=1, dtype=jnp.float32)  22 us
    concatenate x1, other arithmetic, per_device(): table = jnp.concatenate([hot_table, cold_rows], axis=0)  21.5 us
    all_to_all x1, waiting for transfers between devices, per_device(): lax.all_to_all(send_rows.reshape(groups, capacity, hidden_cols), 'grp', s...  18.7 us
  transfers between devices with their start and end apart: 5, of which 4 were waited for; matrix products, arithmetic and copies ran while one was open for 6% of the time, Pallas kernels for 0%

commit v1 on v0

v1 whole, which is shorter than its diff:
```python
import functools

import jax
import jax.numpy as jnp
from jax import lax
from jax.experimental import pallas as pl
from jax.experimental.pallas import tpu as pltpu
from jax.sharding import PartitionSpec as P

BLK = 128
S1 = 10
LANES = 128


def pack_kernel(blocks, counts, cold, out, zeros, sems):
    zeros[...] = jnp.zeros_like(zeros)
    total = blocks.shape[0]
    slots = total // counts.shape[0]

    def start(i, carry):
        valid = lax.rem(i, slots) < counts[i // slots]
        rows = pl.ds(pl.multiple_of(i * BLK, BLK), BLK)
        origin = pl.ds(pl.multiple_of(blocks[i] * BLK, BLK), BLK)

        @pl.when(valid)
        def _():
            pltpu.make_async_copy(cold.at[origin], out.at[rows], sems.at[i]).start()

        @pl.when(jnp.logical_not(valid))
        def _():
            pltpu.make_async_copy(zeros, out.at[rows], sems.at[i]).start()

        return carry

    def wait(i, carry):
        rows = pl.ds(pl.multiple_of(i * BLK, BLK), BLK)
        pltpu.make_async_copy(zeros, out.at[rows], sems.at[i]).wait()
        return carry

    lax.fori_loop(0, total, start, 0)
    lax.fori_loop(0, total, wait, 0)


def pack_blocks(blocks, counts, cold):
    total = blocks.shape[0]
    cols = cold.shape[1]
    return pl.pallas_call(
        pack_kernel,
        out_shape=jax.ShapeDtypeStruct((total * BLK, cols), cold.dtype),
        in_specs=[
            pl.BlockSpec(memory_space=pltpu.SMEM),
            pl.BlockSpec(memory_space=pltpu.SMEM),
            pl.BlockSpec(memory_space=pltpu.VMEM),
        ],
        out_specs=pl.BlockSpec(memory_space=pl.ANY),
        scratch_shapes=[pltpu.VMEM((BLK, cols), cold.dtype), pltpu.SemaphoreType.DMA((total,))],
        name="pack_blocks",
    )(blocks, counts, cold)


CHUNK = 1024
DEPTH = 4


def gather_kernel(index, dest, hot, fetched, out, table, stage, acc, sems):
    hot_chunks = hot.shape[0] // CHUNK
    chunks = hot_chunks + fetched.shape[0] // CHUNK
    nodes = dest.shape[0]

    def copy(c, slot):
        @pl.when(c < hot_chunks)
        def _():
            rows = pl.ds(pl.multiple_of(c * CHUNK, CHUNK), CHUNK)
            pltpu.make_async_copy(hot.at[rows], stage.at[slot], sems.at[slot]).start()

        @pl.when(c >= hot_chunks)
        def _():
            rows = pl.ds(pl.multiple_of((c - hot_chunks) * CHUNK, CHUNK), CHUNK)
            pltpu.make_async_copy(fetched.at[rows], stage.at[slot], sems.at[slot]).start()

    for c in range(DEPTH):
        copy(c, c)

    def fill(i, carry):
        acc[pl.ds(pl.multiple_of(i * 8, 8), 8), :] = jnp.zeros((8, LANES), jnp.float32)
        return carry

    lax.fori_loop(0, acc.shape[0] // 8, fill, 0, unroll=8)

    def load(c, carry):
        slot = lax.rem(c, DEPTH)
        pltpu.make_async_copy(hot.at[pl.ds(0, CHUNK)], stage.at[slot], sems.at[slot]).wait()

        def widen(g, inner):
            value = stage[slot, pl.ds(pl.multiple_of(g * 16, 16), 16), :].astype(jnp.float32)
            row = pl.multiple_of(c * (2 * CHUNK) + g * 32, 32)
            table[pl.ds(row, 16, stride=2), :] = value[:, :LANES]
            table[pl.ds(row + 1, 16, stride=2), :] = value[:, LANES:]
            return inner

        lax.fori_loop(0, CHUNK // 16, widen, 0, unroll=4)

        @pl.when(c + DEPTH < chunks)
        def _():
            copy(c + DEPTH, slot)

        return carry

    lax.fori_loop(0, chunks, load, 0)

    total = acc.shape[0] // 2

    def node(i, carry):
        place = pl.multiple_of(dest[i], 2)
        acc[pl.ds(place, 2), :] = table[pl.ds(pl.multiple_of(index[i], 2), 2), :]
        rows = [
            table[pl.ds(pl.multiple_of(index[(k + 1) * nodes + i], 2), 2), :] for k in range(S1)
        ]
        while len(rows) > 1:
            rows = [a + b for a, b in zip(rows[::2], rows[1::2])] + rows[len(rows) // 2 * 2 :]
        acc[pl.ds(total + place, 2), :] = rows[0]
        return carry

    lax.fori_loop(0, nodes, node, 0, unroll=8)

    def finish(g, carry):
        row = pl.multiple_of(g * 32, 32)
        own = [acc[pl.ds(row + j, 16, stride=2), :] for j in range(2)]
        mean = [acc[pl.ds(total + row + j, 16, stride=2), :] / S1 for j in range(2)]
        out[pl.ds(pl.multiple_of(g * 16, 16), 16), :] = jnp.concatenate(own + mean, axis=1).astype(
            jnp.bfloat16
        )
        return carry

    lax.fori_loop(0, out.shape[0] // 16, finish, 0, unroll=2)


def gather_rows(index, dest, hot, fetched, rows):
    cols = hot.shape[1]
    table_rows = hot.shape[0] + fetched.shape[0]
    return pl.pallas_call(
        gather_kernel,
        out_shape=jax.ShapeDtypeStruct((rows, 2 * cols), jnp.bfloat16),
        in_specs=[
            pl.BlockSpec(memory_space=pltpu.SMEM),
            pl.BlockSpec(memory_space=pltpu.SMEM),
            pl.BlockSpec(memory_space=pl.ANY),
            pl.BlockSpec(memory_space=pl.ANY),
        ],
        out_specs=pl.BlockSpec(memory_space=pltpu.VMEM),
        scratch_shapes=[
            pltpu.VMEM((2 * table_rows, LANES), jnp.float32),
            pltpu.VMEM((DEPTH, CHUNK, cols), jnp.bfloat16),
            pltpu.VMEM((4 * rows, LANES), jnp.float32),
            pltpu.SemaphoreType.DMA((DEPTH,)),
        ],
        compiler_params=pltpu.CompilerParams(vmem_limit_bytes=60 * 1024 * 1024),
        name="gather_rows",
    )(index, dest, hot, fetched)


def per_device(
    hot_table,
    cold_table,
    send_blocks,
    block_counts,
    self_ref,
    neigh_ref,
    route_owner,
    route_slot,
    w1_self,
    w1_neigh,
    b1_bias,
    w2_self,
    w2_neigh,
    b2_bias,
):
    groups = lax.axis_size("grp")
    parts = lax.axis_size("feat")
    me = lax.axis_index("feat")
    routed = route_slot.shape[0]
    nodes = self_ref.shape[0]
    targets = nodes - routed
    own_part = targets // parts
    hidden = w1_self.shape[1]
    hidden_part = b1_bias.shape[0]
    capacity = 2 * routed // groups
    slots = capacity // parts
    part_rows = own_part + (routed + (parts - 1) * groups) // parts
    part_rows = (part_rows + 15) // 16 * 16

    outgoing = pack_blocks(send_blocks.reshape(-1), block_counts.reshape(-1), cold_table)
    outgoing = outgoing.reshape(groups, -1, cold_table.shape[1])
    fetched = lax.all_to_all(outgoing, "grp", split_axis=0, concat_axis=0, tiled=True)
    fetched = fetched.reshape(-1, cold_table.shape[1])

    w1 = jnp.concatenate([w1_self, w1_neigh], axis=0)
    w1_all, w2s_all, b1_all = [w1], [w2_self], [b1_bias]
    for step in range(1, parts):
        ring = [(s, (s + step) % parts) for s in range(parts)]
        w1_all.append(lax.ppermute(w1, "feat", ring))
        w2s_all.append(lax.ppermute(w2_self, "feat", ring))
        b1_all.append(lax.ppermute(b1_bias, "feat", ring))
    order = lax.rem(me - jnp.arange(parts) + parts, parts)
    w1_all = jnp.stack(w1_all)[order]
    w2s_all = jnp.stack(w2s_all)[order].reshape(hidden, hidden)
    b1_all = jnp.stack(b1_all)[order].reshape(hidden)

    owner = route_owner[:, 0]
    onehot = (owner[:, None] == jnp.arange(groups, dtype=jnp.int32)[None, :]).astype(jnp.int32)
    ranks = jnp.cumsum(onehot, axis=0)
    position = jnp.sum((ranks - 1) * onehot, axis=1)
    quarter, depth = position % parts, position // parts
    totals = ranks[-1]
    held = (totals[None, :] - jnp.arange(parts)[:, None] + parts - 1) // parts
    base = jnp.cumsum(held, axis=1) - held + own_part
    owner_base = jnp.sum(onehot[:, :, None] * base.T[None, :, :], axis=1)
    mine = quarter[:, None] == jnp.arange(parts)[None, :]
    row_base = jnp.sum(jnp.where(mine, owner_base, 0), axis=1)
    routed_dest = quarter * part_rows + row_base + depth
    own = jnp.arange(targets, dtype=jnp.int32)
    own_dest = own // own_part * part_rows + own % own_part
    dest = jnp.concatenate([own_dest, routed_dest]) * 2
    index = jnp.concatenate([self_ref, neigh_ref.T.reshape(-1)]) * 2

    column = quarter * slots + depth
    named = (column[:, None] == jnp.arange(capacity, dtype=jnp.int32)[None, :]).astype(jnp.bfloat16)
    send_slots = lax.dot_general(
        onehot.astype(jnp.bfloat16),
        named * (route_slot + 1).astype(jnp.bfloat16)[:, None],
        (((0,), (0,)), ((), ())),
        preferred_element_type=jnp.float32,
    )
    send_slots = send_slots.astype(jnp.int32) - 1
    recv_slots = lax.all_to_all(send_slots, "grp", split_axis=0, concat_axis=0, tiled=True)
    recv_slots = recv_slots.reshape(groups * capacity)

    my_base = lax.dynamic_index_in_dim(base, me, 0, keepdims=False)
    my_held = lax.dynamic_index_in_dim(held, me, 0, keepdims=False)
    place = jnp.arange(slots, dtype=jnp.int32)[None, :]
    source = jnp.where(place < my_held[:, None], my_base[:, None] + place, -1).reshape(-1)
    spread = (source[:, None] == jnp.arange(part_rows, dtype=jnp.int32)[None, :]).astype(
        jnp.bfloat16
    )

    rows = gather_rows(index, dest, hot_table, fetched, parts * part_rows)
    rows = rows.reshape(parts, part_rows, -1)
    rows = lax.all_to_all(rows, "feat", split_axis=0, concat_axis=0, tiled=True)
    pre = b1_all[None, :]
    for s in range(parts):
        pre = pre + jnp.dot(rows[s], w1_all[s], preferred_element_type=jnp.float32)
    h1 = jnp.maximum(pre, 0.0).astype(jnp.bfloat16)

    send_rows = jnp.dot(spread, h1, preferred_element_type=jnp.float32).astype(jnp.bfloat16)
    send_rows = send_rows.reshape(groups, slots, parts, hidden_part).transpose(0, 2, 1, 3)
    send_rows = send_rows.reshape(groups * parts, slots, hidden_part)
    recv_rows = lax.all_to_all(send_rows, ("grp", "feat"), split_axis=0, concat_axis=0, tiled=True)
    recv_rows = recv_rows.reshape(groups * capacity, hidden_part)

    own_two = jnp.dot(h1[:own_part], w2s_all, preferred_element_type=jnp.float32)
    member = jnp.arange(targets, dtype=jnp.int32)[:, None] == recv_slots[None, :]
    total = jnp.dot(member.astype(jnp.bfloat16), recv_rows, preferred_element_type=jnp.float32)
    count = jnp.sum(member.astype(jnp.float32), axis=1)
    neigh_h = (total / jnp.maximum(count, 1.0)[:, None]).astype(jnp.bfloat16)
    partial_two = jnp.dot(neigh_h, w2_neigh, preferred_element_type=jnp.float32)
    holds = (jnp.arange(parts) == me)[:, None, None]
    partial_two = partial_two.reshape(parts, own_part, hidden) + jnp.where(holds, own_two[None], 0.0)
    partial_two = partial_two.reshape(targets, parts, hidden_part).transpose(1, 0, 2)
    shared = lax.all_to_all(partial_two, "feat", split_axis=0, concat_axis=0, tiled=True)
    return (jnp.sum(shared, axis=0) + b2_bias).astype(jnp.bfloat16)


def solution(mesh):
    in_specs = (
        P(None, "feat"),
        P("grp", "feat"),
        P("grp", None, None),
        P("grp", None),
        P("grp"),
        P("grp", None),
        P("grp", None),
        P("grp"),
        P("feat", None),
        P("feat", None),
        P("feat"),
        P("feat", None),
        P("feat", None),
        P("feat"),
    )
    out_specs = P("grp", "feat")
    return jax.shard_map(
        per_device, mesh=mesh, in_specs=in_specs, out_specs=out_specs, check_vma=False
    )
```

time: 592 us -> 398 us (0.67)
  local copies, waits for them, and re-layouts: 148 us -> 13.2 us
  waiting for transfers between devices: 303 us -> 224 us
  Pallas kernels: 0 us -> 55.5 us
  other arithmetic: 69.5 us -> 16.6 us
  starting transfers between devices: 41.5 us -> 67.2 us
  between operations: 13.6 us -> 0.43 us
  blocking collectives: 0 us -> 11.9 us
  matrix products: 13.7 us -> 7.71 us
    gather x3, local copies, waits for them, and re-layouts: 97.5 us -> 4.7 us  [the longest x1 3.56 us: per_device(): w1_all = jnp.stack(w1_all)[order]]
    psum x1 -> x0, waiting for transfers between devices: 90.5 us -> none  [per_device(): summed = lax.psum(partial_value, 'feat')]
    ppermute x0 -> x9, waiting for transfers between devices: none -> 59.2 us  [the longest x3 42.9 us: per_device(): b1_all.append(lax.ppermute(b1_bias, 'feat', ring))]
    pallas_call x0 -> x2, Pallas kernels: none -> 55.5 us  [the longest x1 47.7 us: gather_rows(): pl.pallas_call(gather_kernel, out_shape=jax.ShapeDtypeStruct((rows, 2 * c...]
    convert_element_type x1 -> x0, local copies, waits for them, and re-layouts: 28.8 us -> none  [per_device(): neigh_total = jnp.sum(table[neigh_ref], axis=1, dtype=jnp.float32)]
    reduce_sum x2 -> x4, other arithmetic: 22.1 us -> 0.41 us  [the longest x1 0.25 us: per_device(): owner_base = jnp.sum(onehot[:, :, None] * base.T[None, :, :], axis=1)]
    concatenate x1 -> x0, other arithmetic: 21.5 us -> none  [per_device(): table = jnp.concatenate([hot_table, cold_rows], axis=0)]
    all_to_all x2 -> x3, waiting for transfers between devices: 18.7 us -> 0.17 us  [the longest x1 0.16 us: per_device(): lax.all_to_all(send_slots, 'grp', split_axis=0, concat_axis=0, tiled=True)]
  transfers between devices with their start and end apart: 5 -> 13, of which waited for: 4 -> 6; matrix products, arithmetic and copies ran while one was open for 6% -> 8% of each run, Pallas kernels for 0% -> 0%
where the time goes in v1:
time: 398 us; the launch traced here: 397 us
  waiting for transfers between devices  224 us (56%)
  starting transfers between devices  67.2 us (17%)
  Pallas kernels  55.5 us (14%)
  other arithmetic  16.6 us (4%)
  local copies, waits for them, and re-layouts  13.2 us (3%)
  blocking collectives  11.9 us (3%)
  matrix products  7.71 us (2%)
    all_to_all x1, waiting for transfers between devices, per_device(): lax.all_to_all(outgoing, 'grp', split_axis=0, concat_axis=0, tiled=True)  165 us
    pallas_call x1, Pallas kernels, gather_rows(): pl.pallas_call(gather_kernel, out_shape=jax.ShapeDtypeStruct((rows, 2 * c...  47.7 us
    ppermute x3, waiting for transfers between devices, per_device(): b1_all.append(lax.ppermute(b1_bias, 'feat', ring))  42.9 us
    all_to_all x1, starting transfers between devices, per_device(): lax.all_to_all(send_slots, 'grp', split_axis=0, concat_axis=0, tiled=True)  26.9 us
    ppermute x3, waiting for transfers between devices, per_device(): w2s_all.append(lax.ppermute(w2_self, 'feat', ring))  16.3 us
    all_to_all x1, blocking collectives, per_device(): lax.all_to_all(partial_two, 'feat', split_axis=0, concat_axis=0, tiled=True)  11.9 us
    all_to_all x1, starting transfers between devices, per_device(): lax.all_to_all(send_rows, ('grp', 'feat'), split_axis=0, concat_axis=0, t...  10.4 us
    another operation x3, other arithmetic  9.53 us
  transfers between devices with their start and end apart: 13, of which 6 were waited for; matrix products, arithmetic and copies ran while one was open for 8% of the time, Pallas kernels for 0%

profile of v1, /device:TPU:0, one launch (start us, length us, event | category | flops | bytes accessed | tf_op | source)
XLA Modules:
  0.0 396.8 jit_solution(646091459856752888)
XLA Ops:
  0.0 0.8 copy.48
  1.5 7.8 %pack_blocks.1 = bf16[24576,256]{1,0:T(8,128)(2,1)} custom-call(s32[192]{0:T(256)} %reshape.198.blocks, s32[32]{0:T(128)} %bitcast.88, bf16[4096,256]{1,0:T(8,128)(2,1)} %cold.1), custom_call_target="tpu_custom_call" | custom-call | tf_op jit(solution)/shard_map/pack_blocks/pallas_call | solution.py:47
  9.3 8.6 %all-to-all-start.1 = ((bf16[32,768,256]{2,1,0:T(8,128)(2,1)}), bf16[32,768,256]{2,1,0:T(8,128)(2,1)}, u32[]{:S(2)}, u32[]{:S(2)}) async-start(bf16[32,768,256]{2,1,0:T(8,128)(2,1)} %bitcast.74), calls=%async_computation.1 | async-start | bytes 25165824 | tf_op jit(solution)/shard_map/all_to_all | solution.py:194
  18.0 9.2 %reduce-window.6 = s32[32,20,128]{2,1,0:T(8,128)S(1)} reduce-window(s32[32,20,128]{2,1,0:T(8,128)S(1)} %fusion.26, s32[]{:T(128)} %constant.100.clone.1), window={size=1x1x128 pad=0_0x0_0x127_0}, to_apply=%region_0.0 | reduce-window | flops 10403840 | bytes 655364 | tf_op jit(solution)/shard_map/reduce-window
  30.2 165.0 %all-to-all-done.1 = bf16[32,768,256]{2,1,0:T(8,128)(2,1)} async-done(((bf16[32,768,256]{2,1,0:T(8,128)(2,1)}), bf16[32,768,256]{2,1,0:T(8,128)(2,1)}, u32[]{:S(2)}, u32[]{:S(2)}) %all-to-all-start.1) | async-done | bytes 12582944 | tf_op jit(solution)/shard_map/all_to_all | solution.py:194
  195.2 47.7 %gather_rows.1 = bf16[2944,512]{1,0:T(8,128)(2,1)} custom-call(s32[30976]{0:T(1024)} %add_multiply_fusion.index, s32[2816]{0:T(1024)} %add_multiply_fusion.1.dest, bf16[16384,256]{1,0:T(8,128)(2,1)} %hot.1, bf16[24576,256]{1,0:T(8,128)(2,1)} %bitcast.16.fetched), custom_call_target="tpu_custom_call" | custom-call | tf_op jit(solution)/shard_map/gather_rows/pallas_call | solution.py:141
  242.9 4.4 %all-to-all-start.2 = ((bf16[4,736,512]{2,1,0:T(8,128)(2,1)}), bf16[4,736,512]{2,1,0:T(8,128)(2,1)S(1)}, u32[]{:S(2)}, u32[]{:S(2)}) async-start(bf16[4,736,512]{2,1,0:T(8,128)(2,1)} %bitcast.75), calls=%async_computation.2 | async-start | bytes 6029312 | tf_op jit(solution)/shard_map/all_to_all | solution.py:248
  247.4 0.7 constant_dynamic-update-slice_fusion.1
  248.1 1.7 constant_dynamic-update-slice_fusion
  249.8 2.0 collective-permute-start.3
  251.8 2.7 collective-permute-start.4
  254.5 1.5 collective-permute-start.5
  256.5 0.9 collective-permute-start.1
  257.5 0.9 fusion.18
  258.4 42.3 %collective-permute-done = f32[128]{0:T(128)S(1)} collective-permute-done((f32[128]{0:T(128)S(1)}, f32[128]{0:T(128)S(1)}, u32[]{:S(2)}, u32[]{:S(2)}) %collective-permute-start) | collective-permute-done | bytes 544 | tf_op jit(solution)/shard_map/ppermute | solution.py:203
  300.7 4.1 %collective-permute-start.2 = (f32[128]{0:T(128)S(1)}, f32[128]{0:T(128)S(1)}, u32[]{:S(2)}, u32[]{:S(2)}) collective-permute-start(f32[128]{0:T(128)S(1)} %copy-done.10), channel_id=1, source_target_pairs={{0,3},{1,0},{2,1},{3,2},{4,7},{5,4},{6,5},{7,6},{8,11},{9,8},{10,9... | collective-permute-start | bytes 1544 | tf_op jit(solution)/shard_map/ppermute | solution.py:203
  306.7 3.1 pad_maximum_fusion
  309.9 3.6 gather_fusion.1
  313.4 26.9 %all-to-all-start = ((s32[32,1,160]{2,1,0:T(1,128)}), s32[32,1,160]{2,1,0:T(1,128)S(1)}, u32[]{:S(2)}, u32[]{:S(2)}) async-start(s32[32,1,160]{2,1,0:T(1,128)} %copy.47), calls=%async_computation | async-start | bytes 65536 | tf_op jit(solution)/shard_map/all_to_all | solution.py:235
  340.3 1.7 fusion.23
  343.8 0.9 copy-done.2
  344.7 1.2 fusion.2
  346.3 1.2 copy.49
  347.7 10.4 %all-to-all-start.3 = ((bf16[128,40,128]{2,1,0:T(8,128)(2,1)}), bf16[128,40,128]{2,1,0:T(8,128)(2,1)S(1)}, u32[]{:S(2)}, u32[]{:S(2)}) async-start(bf16[128,40,128]{2,1,0:T(8,128)(2,1)} %bitcast.31), calls=%async_computation.3 | async-start | bytes 2621440 | tf_op jit(solution)/shard_map/all_to_all | solution.py:257
  358.2 1.0 collective-permute-start.6
  359.2 2.7 collective-permute-start.7
  361.9 1.5 collective-permute-start.8
  364.3 13.5 %collective-permute-done.6 = bf16[128,512]{1,0:T(8,128)(2,1)S(1)} collective-permute-done((bf16[128,512]{1,0:T(8,128)(2,1)S(1)}, bf16[128,512]{1,0:T(8,128)(2,1)S(1)}, u32[]{:S(2)}, u32[]{:S(2)}) %collective-permute-start.6) | collective-permute-done | bytes 131104 | tf_op jit(solution)/shard_map/ppermute | solution.py:202
  377.8 2.8 collective-permute-done.7
  381.2 1.0 fusion.30
  382.6 1.1 fusion.11
  384.3 11.9 %all_to_all.29 = f32[4,256,128]{2,1,0:T(8,128)S(1)} all-to-all(f32[4,256,128]{2,1,0:T(8,128)S(1)} %copy.50), channel_id=1, replica_groups=mesh['grp'=32,'feat'=4] {'feat'}, dimensions={0} | all-to-all | bytes 1048576 | tf_op jit(solution)/shard_map/all_to_all | solution.py:269
  (81 shorter events, 11.6 us)
Async XLA Ops:
  0.0 382.6 %copy-start = (bf16[128,512]{1,0:T(8,128)(2,1)S(1)}, bf16[128,512]{1,0:T(8,128)(2,1)}, u32[]{:S(2)}) copy-start(bf16[128,512]{1,0:T(8,128)(2,1)} %param.26) | copy-start | bytes 393220
  9.3 8.6 %copy-start.8 = (s32[2560,1]{0,1:T(1,128)S(1)}, s32[2560,1]{0,1:T(1,128)}, u32[]{:S(2)}) copy-start(s32[2560,1]{0,1:T(1,128)} %param.20) | copy-start | bytes 30724
  9.3 185.9 %all-to-all-start.1 = ((bf16[32,768,256]{2,1,0:T(8,128)(2,1)}), bf16[32,768,256]{2,1,0:T(8,128)(2,1)}, u32[]{:S(2)}, u32[]{:S(2)}) async-start(bf16[32,768,256]{2,1,0:T(8,128)(2,1)} %bitcast.74), calls=%async_computation.1 | async-start | bytes 25165824 | tf_op jit(solution)/shard_map/all_to_all | solution.py:194
  17.9 10.6 %copy-start.4 = (s32[2816,10]{0,1:T(8,128)S(1)}, s32[2816,10]{0,1:T(8,128)}, u32[]{:S(2)}) copy-start(s32[2816,10]{0,1:T(8,128)} %param.19) | copy-start | bytes 337924
  27.2 1.7 copy-start.7
  27.2 2.4 copy-start.6
  242.9 4.5 %copy-start.3 = (bf16[256,512]{1,0:T(8,128)(2,1)S(1)}, bf16[256,512]{1,0:T(8,128)(2,1)}, u32[]{:S(2)}) copy-start(bf16[256,512]{1,0:T(8,128)(2,1)} %param.22) | copy-start | bytes 786436
  242.9 13.0 %copy-start.10 = (f32[128]{0:T(128)S(1)}, f32[128]{0:T(128)}, u32[]{:S(2)}) copy-start(f32[128]{0:T(128)} %param.24) | copy-start | bytes 1540
  242.9 70.5 %all-to-all-start.2 = ((bf16[4,736,512]{2,1,0:T(8,128)(2,1)}), bf16[4,736,512]{2,1,0:T(8,128)(2,1)S(1)}, u32[]{:S(2)}, u32[]{:S(2)}) async-start(bf16[4,736,512]{2,1,0:T(8,128)(2,1)} %bitcast.75), calls=%async_computation.2 | async-start | bytes 6029312 | tf_op jit(solution)/shard_map/all_to_all | solution.py:248
  249.8 56.9 %collective-permute-start.3 = (bf16[512,512]{1,0:T(8,128)(2,1)}, bf16[512,512]{1,0:T(8,128)(2,1)}, u32[]{:S(2)}, u32[]{:S(2)}) collective-permute-start(bf16[512,512]{1,0:T(8,128)(2,1)} %constant_dynamic-update-slice_fusion), channel_id=1, source_target_pairs={{0,1},{1,2},{2,3},{3,0},{4,5},{5,6},{6,7},{7,4},{8,9},{9,10},{10,1... | collective-permute-start | bytes 1572872 | tf_op jit(solution)/shard_map/ppermute | solution.py:201
  251.8 54.9 %collective-permute-start.4 = (bf16[512,512]{1,0:T(8,128)(2,1)}, bf16[512,512]{1,0:T(8,128)(2,1)}, u32[]{:S(2)}, u32[]{:S(2)}) collective-permute-start(bf16[512,512]{1,0:T(8,128)(2,1)} %constant_dynamic-update-slice_fusion), channel_id=1, source_target_pairs={{0,2},{1,3},{2,0},{3,1},{4,6},{5,7},{6,4},{7,5},{8,10},{9,11},{10,... | collective-permute-start | bytes 1572872 | tf_op jit(solution)/shard_map/ppermute | solution.py:201
  254.5 52.3 %collective-permute-start.5 = (bf16[512,512]{1,0:T(8,128)(2,1)}, bf16[512,512]{1,0:T(8,128)(2,1)}, u32[]{:S(2)}, u32[]{:S(2)}) collective-permute-start(bf16[512,512]{1,0:T(8,128)(2,1)} %constant_dynamic-update-slice_fusion), channel_id=1, source_target_pairs={{0,3},{1,0},{2,1},{3,2},{4,7},{5,4},{6,5},{7,6},{8,11},{9,8},{10,9... | collective-permute-start | bytes 1572872 | tf_op jit(solution)/shard_map/ppermute | solution.py:201
  255.9 44.8 %collective-permute-start = (f32[128]{0:T(128)S(1)}, f32[128]{0:T(128)S(1)}, u32[]{:S(2)}, u32[]{:S(2)}) collective-permute-start(f32[128]{0:T(128)S(1)} %copy-done.10), channel_id=1, source_target_pairs={{0,1},{1,2},{2,3},{3,0},{4,5},{5,6},{6,7},{7,4},{8,9},{9,10},{10,1... | collective-permute-start | bytes 1544 | tf_op jit(solution)/shard_map/ppermute | solution.py:203
  256.5 49.1 %collective-permute-start.1 = (f32[128]{0:T(128)S(1)}, f32[128]{0:T(128)S(1)}, u32[]{:S(2)}, u32[]{:S(2)}) collective-permute-start(f32[128]{0:T(128)S(1)} %copy-done.10), channel_id=1, source_target_pairs={{0,2},{1,3},{2,0},{3,1},{4,6},{5,7},{6,4},{7,5},{8,10},{9,11},{10,... | collective-permute-start | bytes 1544 | tf_op jit(solution)/shard_map/ppermute | solution.py:203
  300.7 5.4 %collective-permute-start.2 = (f32[128]{0:T(128)S(1)}, f32[128]{0:T(128)S(1)}, u32[]{:S(2)}, u32[]{:S(2)}) collective-permute-start(f32[128]{0:T(128)S(1)} %copy-done.10), channel_id=1, source_target_pairs={{0,3},{1,0},{2,1},{3,2},{4,7},{5,4},{6,5},{7,6},{8,11},{9,8},{10,9... | collective-permute-start | bytes 1544 | tf_op jit(solution)/shard_map/ppermute | solution.py:203
  313.4 34.3 %all-to-all-start = ((s32[32,1,160]{2,1,0:T(1,128)}), s32[32,1,160]{2,1,0:T(1,128)S(1)}, u32[]{:S(2)}, u32[]{:S(2)}) async-start(s32[32,1,160]{2,1,0:T(1,128)} %copy.47), calls=%async_computation | async-start | bytes 65536 | tf_op jit(solution)/shard_map/all_to_all | solution.py:235
  340.3 1.8 copy-start.1
  343.8 0.9 copy-start.2
  346.3 11.8 %copy-start.5 = (bf16[128,512]{1,0:T(8,128)(2,1)S(1)}, bf16[128,512]{1,0:T(8,128)(2,1)}, u32[]{:S(2)}) copy-start(bf16[128,512]{1,0:T(8,128)(2,1)} %param.25) | copy-start | bytes 393220
  347.7 34.8 %all-to-all-start.3 = ((bf16[128,40,128]{2,1,0:T(8,128)(2,1)}), bf16[128,40,128]{2,1,0:T(8,128)(2,1)S(1)}, u32[]{:S(2)}, u32[]{:S(2)}) async-start(bf16[128,40,128]{2,1,0:T(8,128)(2,1)} %bitcast.31), calls=%async_computation.3 | async-start | bytes 2621440 | tf_op jit(solution)/shard_map/all_to_all | solution.py:257
  358.2 19.6 %collective-permute-start.6 = (bf16[128,512]{1,0:T(8,128)(2,1)S(1)}, bf16[128,512]{1,0:T(8,128)(2,1)S(1)}, u32[]{:S(2)}, u32[]{:S(2)}) collective-permute-start(bf16[128,512]{1,0:T(8,128)(2,1)S(1)} %copy-done.5), channel_id=1, source_target_pairs={{0,1},{1,2},{2,3},{3,0},{4,5},{5,6},{6,7},{7,4},{8,9},{9,10},{10,1... | collective-permute-start | bytes 393224 | tf_op jit(solution)/shard_map/ppermute | solution.py:202
  359.2 21.4 %collective-permute-start.7 = (bf16[128,512]{1,0:T(8,128)(2,1)S(1)}, bf16[128,512]{1,0:T(8,128)(2,1)S(1)}, u32[]{:S(2)}, u32[]{:S(2)}) collective-permute-start(bf16[128,512]{1,0:T(8,128)(2,1)S(1)} %copy-done.5), channel_id=1, source_target_pairs={{0,2},{1,3},{2,0},{3,1},{4,6},{5,7},{6,4},{7,5},{8,10},{9,11},{10,... | collective-permute-start | bytes 393224 | tf_op jit(solution)/shard_map/ppermute | solution.py:202
  361.9 18.7 %collective-permute-start.8 = (bf16[128,512]{1,0:T(8,128)(2,1)S(1)}, bf16[128,512]{1,0:T(8,128)(2,1)S(1)}, u32[]{:S(2)}, u32[]{:S(2)}) collective-permute-start(bf16[128,512]{1,0:T(8,128)(2,1)S(1)} %copy-done.5), channel_id=1, source_target_pairs={{0,3},{1,0},{2,1},{3,2},{4,7},{5,4},{6,5},{7,6},{8,11},{9,8},{10,9... | collective-permute-start | bytes 393224 | tf_op jit(solution)/shard_map/ppermute | solution.py:202
  383.9 12.3 %copy-start.9 = (f32[128]{0:T(128)S(1)}, f32[128]{0:T(128)}, u32[]{:S(2)}) copy-start(f32[128]{0:T(128)} %param.27) | copy-start | bytes 1540

commit v2 on v1

--- a/solution.py
+++ b/solution.py
@@ -10,73 +10,126 @@
 BLK = 128
 S1 = 10
 LANES = 128
-
-
-def pack_kernel(blocks, counts, cold, out, zeros, sems):
-    zeros[...] = jnp.zeros_like(zeros)
-    total = blocks.shape[0]
-    slots = total // counts.shape[0]
-
-    def start(i, carry):
-        valid = lax.rem(i, slots) < counts[i // slots]
-        rows = pl.ds(pl.multiple_of(i * BLK, BLK), BLK)
-        origin = pl.ds(pl.multiple_of(blocks[i] * BLK, BLK), BLK)
-
-        @pl.when(valid)
-        def _():
-            pltpu.make_async_copy(cold.at[origin], out.at[rows], sems.at[i]).start()
-
-        @pl.when(jnp.logical_not(valid))
-        def _():
-            pltpu.make_async_copy(zeros, out.at[rows], sems.at[i]).start()
-
-        return carry
-
-    def wait(i, carry):
-        rows = pl.ds(pl.multiple_of(i * BLK, BLK), BLK)
-        pltpu.make_async_copy(zeros, out.at[rows], sems.at[i]).wait()
-        return carry
-
-    lax.fori_loop(0, total, start, 0)
-    lax.fori_loop(0, total, wait, 0)
-
-
-def pack_blocks(blocks, counts, cold):
-    total = blocks.shape[0]
+HOT = 16384
+MAIN = 480
+
+
+def mark_kernel(refs, before, need, acc):
+    owner_rows = before.shape[0]
+    hot_rows = HOT
+    acc[...] = jnp.zeros_like(acc)
+    high = lax.broadcasted_iota(jnp.int32, (owner_rows, LANES), 0)
+    low = lax.broadcasted_iota(jnp.int32, (LANES, LANES), 0)
+
+    def count(g, carry):
+        tall, wide = [], []
+        for j in range(2):
+            cold = refs[pl.ds(2 * g + j, 1), :] - hot_rows
+            tall.append(jnp.where(high == cold >> 7, 1.0, 0.0).astype(jnp.bfloat16))
+            wide.append(jnp.where(low == (cold & 127), 1.0, 0.0).astype(jnp.bfloat16))
+        acc[...] += lax.dot_general(
+            jnp.concatenate(tall, axis=1),
+            jnp.concatenate(wide, axis=1),
+            (((1,), (1,)), ((), ())),
+            preferred_element_type=jnp.float32,
+        )
+        return carry
+
+    lax.fori_loop(0, refs.shape[0] // 2, count, 0, unroll=11)
+    needed = jnp.where(acc[...] > 0.0, 1.0, 0.0)
+    upto = jnp.where(
+        lax.broadcasted_iota(jnp.int32, (LANES, LANES), 0)
+        <= lax.broadcasted_iota(jnp.int32, (LANES, LANES), 1),
+        1.0,
+        0.0,
+    )
+    running = jnp.dot(
+        needed.astype(jnp.bfloat16), upto.astype(jnp.bfloat16), preferred_element_type=jnp.float32
+    )
+    totals = jnp.dot(
+        needed.astype(jnp.bfloat16),
+        jnp.ones((LANES, LANES), jnp.bfloat16),
+        preferred_element_type=jnp.float32,
+    )
+    earlier = jnp.dot(before[...], totals.astype(jnp.bfloat16), preferred_element_type=jnp.float32)
+    place = running + earlier - 1.0
+    need[...] = jnp.where(needed > 0.0, place, -1.0).astype(jnp.int32)
+
+
+def mark_rows(refs, slot_count, groups):
+    rows = groups * slot_count
+    at = jnp.arange(rows, dtype=jnp.int32)
+    before = (at[:, None] // slot_count == at[None, :] // slot_count) & (at[None, :] < at[:, None])
+    return pl.pallas_call(
+        mark_kernel,
+        out_shape=jax.ShapeDtypeStruct((rows, LANES), jnp.int32),
+        in_specs=[pl.BlockSpec(memory_space=pltpu.VMEM)] * 2,
+        out_specs=pl.BlockSpec(memory_space=pltpu.VMEM),
+        scratch_shapes=[pltpu.VMEM((rows, LANES), jnp.float32)],
+        name="mark_rows",
+    )(refs.reshape(-1, LANES), before.astype(jnp.bfloat16))
+
+
+def pack_kernel(first, slot_count, blocks, counts, need, cold, out):
+    r = pl.program_id(0)
+    rows = out.shape[1]
+    at = lax.broadcasted_iota(jnp.int32, (rows, BLK), 0) + first
+    total = jnp.zeros((rows, cold.shape[1]), jnp.float32)
+    for k in range(0, slot_count, 2):
+        picks, values = [], []
+        for j in (k, k + 1):
+            place = need[0, j : j + 1, :]
+            place = jnp.where(counts[r] > j, place, -1)
+            picks.append(jnp.where(at == place, 1.0, 0.0).astype(jnp.bfloat16))
+            origin = pl.multiple_of(blocks[r * slot_count + j] * BLK, BLK)
+            values.append(cold[pl.ds(origin, BLK), :])
+        total = total + jnp.dot(
+            jnp.concatenate(picks, axis=1),
+            jnp.concatenate(values, axis=0),
+            preferred_element_type=jnp.float32,
+        )
+    out[0] = total.astype(out.dtype)
+
+
+def pack_needed(blocks, counts, need, cold, first, rows):
+    groups = counts.shape[0]
     cols = cold.shape[1]
     return pl.pallas_call(
-        pack_kernel,
-        out_shape=jax.ShapeDtypeStruct((total * BLK, cols), cold.dtype),
+        functools.partial(pack_kernel, first, blocks.shape[0] // groups),
+        grid=(groups,),
+        out_shape=jax.ShapeDtypeStruct((groups, rows, cols), cold.dtype),
         in_specs=[
             pl.BlockSpec(memory_space=pltpu.SMEM),
             pl.BlockSpec(memory_space=pltpu.SMEM),
+            pl.BlockSpec((1,) + need.shape[1:], lambda r: (r, 0, 0)),
             pl.BlockSpec(memory_space=pltpu.VMEM),
         ],
-        out_specs=pl.BlockSpec(memory_space=pl.ANY),
-        scratch_shapes=[pltpu.VMEM((BLK, cols), cold.dtype), pltpu.SemaphoreType.DMA((total,))],
-        name="pack_blocks",
-    )(blocks, counts, cold)
+        out_specs=pl.BlockSpec((1, rows, cols), lambda r: (r, 0, 0)),
+        name="pack_needed",
+    )(blocks, counts, need, cold)
 
 
 CHUNK = 1024
 DEPTH = 4
 
 
-def gather_kernel(index, dest, hot, fetched, out, table, stage, acc, sems):
-    hot_chunks = hot.shape[0] // CHUNK
-    chunks = hot_chunks + fetched.shape[0] // CHUNK
+def gather_kernel(source_count, index, where, dest, *refs):
+    sources, (out, table, stage, acc, sems) = refs[:source_count], refs[source_count:]
+    chunks = sum(source.shape[0] for source in sources) // CHUNK
     nodes = dest.shape[0]
 
     def copy(c, slot):
-        @pl.when(c < hot_chunks)
-        def _():
-            rows = pl.ds(pl.multiple_of(c * CHUNK, CHUNK), CHUNK)
-            pltpu.make_async_copy(hot.at[rows], stage.at[slot], sems.at[slot]).start()
-
-        @pl.when(c >= hot_chunks)
-        def _():
-            rows = pl.ds(pl.multiple_of((c - hot_chunks) * CHUNK, CHUNK), CHUNK)
-            pltpu.make_async_copy(fetched.at[rows], stage.at[slot], sems.at[slot]).start()
+        begin = 0
+        for source in sources:
+            length = source.shape[0] // CHUNK
+            first = begin
+
+            @pl.when((c >= first) & (c < first + length))
+            def _():
+                rows = pl.ds(pl.multiple_of((c - first) * CHUNK, CHUNK), CHUNK)
+                pltpu.make_async_copy(source.at[rows], stage.at[slot], sems.at[slot]).start()
+
+            begin += length
 
     for c in range(DEPTH):
         copy(c, c)
@@ -89,7 +142,7 @@
 
     def load(c, carry):
         slot = lax.rem(c, DEPTH)
-        pltpu.make_async_copy(hot.at[pl.ds(0, CHUNK)], stage.at[slot], sems.at[slot]).wait()
+        pltpu.make_async_copy(sources[0].at[pl.ds(0, CHUNK)], stage.at[slot], sems.at[slot]).wait()
 
         def widen(g, inner):
             value = stage[slot, pl.ds(pl.multiple_of(g * 16, 16), 16), :].astype(jnp.float32)
@@ -112,9 +165,9 @@
 
     def node(i, carry):
         place = pl.multiple_of(dest[i], 2)
-        acc[pl.ds(place, 2), :] = table[pl.ds(pl.multiple_of(index[i], 2), 2), :]
+        acc[pl.ds(place, 2), :] = table[pl.ds(pl.multiple_of(where[index[i]], 2), 2), :]
         rows = [
-            table[pl.ds(pl.multiple_of(index[(k + 1) * nodes + i], 2), 2), :] for k in range(S1)
+            table[pl.ds(pl.multiple_of(where[index[(k + 1) * nodes + i]], 2), 2), :] for k in range(S1)
         ]
         while len(rows) > 1:
             rows = [a + b for a, b in zip(rows[::2], rows[1::2])] + rows[len(rows) // 2 * 2 :]
@@ -135,18 +188,14 @@
     lax.fori_loop(0, out.shape[0] // 16, finish, 0, unroll=2)
 
 
-def gather_rows(index, dest, hot, fetched, rows):
-    cols = hot.shape[1]
-    table_rows = hot.shape[0] + fetched.shape[0]
+def gather_rows(index, where, dest, sources, rows):
+    cols = sources[0].shape[1]
+    table_rows = sum(source.shape[0] for source in sources)
     return pl.pallas_call(
-        gather_kernel,
+        functools.partial(gather_kernel, len(sources)),
         out_shape=jax.ShapeDtypeStruct((rows, 2 * cols), jnp.bfloat16),
-        in_specs=[
-            pl.BlockSpec(memory_space=pltpu.SMEM),
-            pl.BlockSpec(memory_space=pltpu.SMEM),
-            pl.BlockSpec(memory_space=pl.ANY),
-            pl.BlockSpec(memory_space=pl.ANY),
-        ],
+        in_specs=[pl.BlockSpec(memory_space=pltpu.SMEM)] * 3
+        + [pl.BlockSpec(memory_space=pl.ANY)] * len(sources),
         out_specs=pl.BlockSpec(memory_space=pltpu.VMEM),
         scratch_shapes=[
             pltpu.VMEM((2 * table_rows, LANES), jnp.float32),
@@ -156,7 +205,7 @@
         ],
         compiler_params=pltpu.CompilerParams(vmem_limit_bytes=60 * 1024 * 1024),
         name="gather_rows",
-    )(index, dest, hot, fetched)
+    )(index, where, dest, *sources)
 
 
 def per_device(
@@ -189,10 +238,12 @@
     part_rows = own_part + (routed + (parts - 1) * groups) // parts
     part_rows = (part_rows + 15) // 16 * 16
 
-    outgoing = pack_blocks(send_blocks.reshape(-1), block_counts.reshape(-1), cold_table)
-    outgoing = outgoing.reshape(groups, -1, cold_table.shape[1])
-    fetched = lax.all_to_all(outgoing, "grp", split_axis=0, concat_axis=0, tiled=True)
-    fetched = fetched.reshape(-1, cold_table.shape[1])
+    feat_cols = cold_table.shape[1]
+    slot_count = send_blocks.shape[2]
+    fetch_rows = slot_count * BLK
+    index = jnp.concatenate([self_ref, neigh_ref.T.reshape(-1)])
+    need = mark_rows(index, slot_count, groups).reshape(groups, fetch_rows)
+    spills = (jnp.max(need) >= MAIN).astype(jnp.int32)
 
     w1 = jnp.concatenate([w1_self, w1_neigh], axis=0)
     w1_all, w2s_all, b1_all = [w1], [w2_self], [b1_bias]
@@ -208,10 +259,22 @@
 
     owner = route_owner[:, 0]
     onehot = (owner[:, None] == jnp.arange(groups, dtype=jnp.int32)[None, :]).astype(jnp.int32)
-    ranks = jnp.cumsum(onehot, axis=0)
-    position = jnp.sum((ranks - 1) * onehot, axis=1)
+    spans = routed // LANES
+    upto = jnp.arange(LANES)[:, None] <= jnp.arange(LANES)[None, :]
+    running = jnp.dot(
+        onehot.T.astype(jnp.bfloat16).reshape(groups * spans, LANES),
+        upto.astype(jnp.bfloat16),
+        preferred_element_type=jnp.float32,
+    ).reshape(groups, spans, LANES)
+    span_totals = running[:, :, -1]
+    before = jnp.arange(spans)[:, None] < jnp.arange(spans)[None, :]
+    earlier = jnp.dot(
+        span_totals.astype(jnp.bfloat16), before.astype(jnp.bfloat16), preferred_element_type=jnp.float32
+    )
+    ranks = (running + earlier[:, :, None]).astype(jnp.int32).reshape(groups, routed)
+    position = jnp.sum((ranks - 1) * onehot.T, axis=0)
     quarter, depth = position % parts, position // parts
-    totals = ranks[-1]
+    totals = ranks[:, -1]
     held = (totals[None, :] - jnp.arange(parts)[:, None] + parts - 1) // parts
     base = jnp.cumsum(held, axis=1) - held + own_part
     owner_base = jnp.sum(onehot[:, :, None] * base.T[None, :, :], axis=1)
@@ -221,7 +284,6 @@
     own = jnp.arange(targets, dtype=jnp.int32)
     own_dest = own // own_part * part_rows + own % own_part
     dest = jnp.concatenate([own_dest, routed_dest]) * 2
-    index = jnp.concatenate([self_ref, neigh_ref.T.reshape(-1)]) * 2
 
     column = quarter * slots + depth
     named = (column[:, None] == jnp.arange(capacity, dtype=jnp.int32)[None, :]).astype(jnp.bfloat16)
@@ -232,8 +294,34 @@
         preferred_element_type=jnp.float32,
     )
     send_slots = send_slots.astype(jnp.int32) - 1
-    recv_slots = lax.all_to_all(send_slots, "grp", split_axis=0, concat_axis=0, tiled=True)
-    recv_slots = recv_slots.reshape(groups * capacity)
+    flags = jnp.broadcast_to(spills, (groups, LANES - capacity % LANES))
+    notes = jnp.concatenate([need, send_slots, flags], axis=1)
+    notes = lax.all_to_all(notes, "grp", split_axis=0, concat_axis=0, tiled=True)
+    recv_slots = notes[:, fetch_rows : fetch_rows + capacity].reshape(groups * capacity)
+    spilled = jnp.max(notes[:, fetch_rows + capacity]) > 0
+
+    owner_at = jnp.arange(groups, dtype=jnp.int32)[:, None]
+    spill = fetch_rows - MAIN
+    where = jnp.where(
+        need < MAIN,
+        HOT + owner_at * MAIN + need,
+        HOT + groups * MAIN + owner_at * spill + need - MAIN,
+    )
+    where = jnp.concatenate([jnp.arange(HOT, dtype=jnp.int32), where.reshape(-1)]) * 2
+
+    def exchange(first, rows, prepared):
+        outgoing = pack_needed(
+            send_blocks.reshape(-1),
+            block_counts.reshape(-1),
+            notes.reshape(groups, -1, LANES),
+            cold_table,
+            first,
+            rows,
+        )
+        outgoing, prepared = lax.optimization_barrier((outgoing, prepared))
+        fetched = lax.all_to_all(outgoing, "grp", split_axis=0, concat_axis=0, tiled=True)
+        fetched, prepared = lax.optimization_barrier((fetched, prepared))
+        return fetched.reshape(-1, feat_cols), prepared
 
     my_base = lax.dynamic_index_in_dim(base, me, 0, keepdims=False)
     my_held = lax.dynamic_index_in_dim(held, me, 0, keepdims=False)
@@ -243,7 +331,18 @@
         jnp.bfloat16
     )
 
-    rows = gather_rows(index, dest, hot_table, fetched, parts * part_rows)
+    prepared = (w1_all, w2s_all, b1_all, index, where, dest, recv_slots, spread, spilled)
+    main, prepared = exchange(0, MAIN, prepared)
+    w1_all, w2s_all, b1_all, index, where, dest, recv_slots, spread, spilled = prepared
+
+    def with_spill():
+        extra, _ = exchange(MAIN, spill, ())
+        return gather_rows(index, where, dest, [hot_table, main, extra], parts * part_rows)
+
+    def without_spill():
+        return gather_rows(index, where, dest, [hot_table, main], parts * part_rows)
+
+    rows = lax.cond(spilled, with_spill, without_spill)
     rows = rows.reshape(parts, part_rows, -1)
     rows = lax.all_to_all(rows, "feat", split_axis=0, concat_axis=0, tiled=True)
     pre = b1_all[None, :]

time: 398 us -> 315 us (0.79)
  waiting for transfers between devices: 224 us -> 22.5 us
  blocking collectives: 11.9 us -> 150 us
  starting transfers between devices: 67.2 us -> 26.2 us
  Pallas kernels: 55.5 us -> 81.6 us
  other arithmetic: 16.6 us -> 11 us
    all_to_all x3 -> x1, waiting for transfers between devices: 165 us -> 0.01 us  [per_device(): lax.all_to_all(notes, 'grp', split_axis=0, concat_axis=0, tiled=True)]
    all_to_all x0 -> x2, blocking collectives: none -> 138 us  [the longest x1 97.3 us: exchange(): lax.all_to_all(outgoing, 'grp', split_axis=0, concat_axis=0, tiled=True)]
    ppermute x3, waiting for transfers between devices: 42.9 us -> 3 us  [per_device(): b1_all.append(lax.ppermute(b1_bias, 'feat', ring))]
    all_to_all x3 -> x1, starting transfers between devices: 39.9 us -> 8.46 us  [per_device(): lax.all_to_all(notes, 'grp', split_axis=0, concat_axis=0, tiled=True)]
    pallas_call x2 -> x3, Pallas kernels: 55.5 us -> 81.6 us  [the longest x1 54.7 us: gather_rows(): pl.pallas_call(functools.partial(gather_kernel, len(sources)), out_shape=...]
    all_to_all x1, waiting for transfers between devices: 0.01 us -> 19.5 us  [per_device(): lax.all_to_all(send_rows, ('grp', 'feat'), split_axis=0, concat_axis=0, t...]
    ppermute x3, waiting for transfers between devices: 16.3 us -> 0.01 us  [per_device(): w2s_all.append(lax.ppermute(w2_self, 'feat', ring))]
    another operation x3 -> x0, other arithmetic: 9.53 us -> none
  transfers between devices with their start and end apart: 13 -> 11, of which waited for: 6 -> 2; matrix products, arithmetic and copies ran while one was open for 8% -> 6% of each run, Pallas kernels for 0% -> 9%
where the time goes in v2:
time: 315 us; the launch traced here: 313 us
  blocking collectives  150 us (48%)
  Pallas kernels  81.6 us (26%)
  starting transfers between devices  26.2 us (8%)
  waiting for transfers between devices  22.5 us (7%)
  local copies, waits for them, and re-layouts  12.4 us (4%)
  other arithmetic  11 us (3%)
  matrix products  6.84 us (2%)
    all_to_all x1, blocking collectives, exchange(): lax.all_to_all(outgoing, 'grp', split_axis=0, concat_axis=0, tiled=True)  97.3 us
    pallas_call x1, Pallas kernels, gather_rows(): pl.pallas_call(functools.partial(gather_kernel, len(sources)), out_shape=...  54.7 us
    all_to_all x1, blocking collectives, per_device(): rows = lax.all_to_all(rows, 'feat', split_axis=0, concat_axis=0, tiled=True)  40.4 us
    pallas_call x1, Pallas kernels, pack_needed(): pl.pallas_call(functools.partial(pack_kernel, first, blocks.shape[0] // g...  19.8 us
    all_to_all x1, waiting for transfers between devices, per_device(): lax.all_to_all(send_rows, ('grp', 'feat'), split_axis=0, concat_axis=0, t...  19.5 us
    all_to_all x1, blocking collectives, per_device(): lax.all_to_all(partial_two, 'feat', split_axis=0, concat_axis=0, tiled=True)  12.7 us
    all_to_all x1, starting transfers between devices, per_device(): lax.all_to_all(notes, 'grp', split_axis=0, concat_axis=0, tiled=True)  8.46 us
    pallas_call x1, Pallas kernels, mark_rows(): pl.pallas_call(mark_kernel, out_shape=jax.ShapeDtypeStruct((rows, LANES),...  7.15 us
  transfers between devices with their start and end apart: 11, of which 2 were waited for; matrix products, arithmetic and copies ran while one was open for 6% of the time, Pallas kernels for 9%

profile of v2, /device:TPU:0, one launch (start us, length us, event | category | flops | bytes accessed | tf_op | source)
XLA Modules:
  0.0 312.7 jit_solution(5642796497005627287)
XLA Ops:
  0.0 1.7 collective-permute-start.6
  1.7 1.6 collective-permute-start.8
  3.2 1.0 constant_dynamic-update-slice_fusion.2
  4.2 1.0 constant_dynamic-update-slice_fusion.1
  5.2 1.8 collective-permute-start.2
  7.8 0.9 collective-permute-start
  11.3 7.2 %mark_rows.1 = s32[192,128]{1,0:T(8,128)} custom-call(s32[242,128]{1,0:T(8,128)S(1)} %bitcast.134, bf16[192,192]{1,0:T(8,128)(2,1)} %fusion.31.before), custom_call_target="tpu_custom_call" | custom-call | tf_op jit(solution)/shard_map/mark_rows/pallas_call | solution.py:63
  18.4 0.9 reshape.328
  19.4 1.6 reduce_max.18
  24.1 8.5 %all-to-all-start.1 = ((s32[32,1,1024]{2,1,0:T(1,128)}), s32[32,1,1024]{2,1,0:T(1,128)S(1)}, u32[]{:S(2)}, u32[]{:S(2)}) async-start(s32[32,1,1024]{2,1,0:T(1,128)} %all_to_all.23), calls=%async_computation.1 | async-start | bytes 262144 | tf_op jit(solution)/shard_map/all_to_all | solution.py:299
  33.0 1.7 fusion.1
  34.7 1.9 collective-permute-start.3
  36.6 2.1 collective-permute-start.7
  39.5 3.0 collective-permute-done.7
  43.2 1.7 collective-permute-start.4
  47.1 19.8 %pack_needed.3 = bf16[32,480,256]{2,1,0:T(8,128)(2,1)} custom-call(s32[192]{0:T(256)} %reshape.324.blocks, s32[32]{0:T(128)S(1)} %bitcast.146, s32[32,8,128]{2,1,0:T(8,128)} %bitcast.132, bf16[4096,256]{1,0:T(8,128)(2,1)S(1)} %copy-done.2), custom_call_target="tpu_custom_call" | custom-call | tf_op jit(solution)/shard_map/pack_needed/pallas_call | solution.py:97
  66.8 1.2 pad_maximum_fusion.1
  68.0 1.4 gather_fusion.1
  69.4 1.6 pad_maximum_fusion
  71.0 2.0 gather_fusion
  73.0 97.3 %all_to_all.37 = bf16[32,480,256]{2,1,0:T(8,128)(2,1)} all-to-all(bf16[32,480,256]{2,1,0:T(8,128)(2,1)} %pack_needed.3), channel_id=1, replica_groups=mesh['grp'=32,'feat'=4] {'grp'}, dimensions={0} | all-to-all | bytes 15728640 | tf_op jit(solution)/shard_map/all_to_all | solution.py:322
  170.3 54.7 %conditional.1 = (bf16[2944,512]{1,0:T(8,128)(2,1)S(1)}) conditional(s32[]{:T(128)} %convert_element_type.76, (s32[30976]{0:T(1024)S(1)}, s32[40960]{0:T(1024)S(1)}, s32[2816]{0:T(1024)S(1)}, bf16[16384,256]{1,0:T(8,128)(2,1)}, bf16[15360,256]{1,0:T(8,128)(2,1)}) %tuple.27, (s32[1,32,6]{1,0,2:T(1,128)S(1)}, s32[1,32]{1,0:T(1,128)S(1)}, ...), branch_computations={%region_6.7_spmd, %region_7.8_spmd} | conditional | bytes 9702408 | solution.py:345
  170.3 54.7 %gather_rows.2 = bf16[2944,512]{1,0:T(8,128)(2,1)S(1)} custom-call(s32[30976]{0:T(1024)S(1)} %get-tuple-element.36.index, s32[40960]{0:T(1024)S(1)} %get-tuple-element.37.where, s32[2816]{0:T(1024)S(1)} %get-tuple-element.38.dest, bf16[16384,256]{1,0:T(8,128)(2,1)} %get-tuple-element.39.refs_0_, bf16[15360,256]{1,0:T(8,128)(2,1)} %get-tuple-element.40.refs_1_), custom_call_target="tpu_custom_call" | custom-call | tf_op jit(solution)/shard_map/cond/branch_0_fun/gather_rows/pallas_call | solution.py:194
  225.0 40.4 %all_to_all.38 = bf16[4,736,512]{2,1,0:T(8,128)(2,1)S(1)} all-to-all(bf16[4,736,512]{2,1,0:T(8,128)(2,1)S(1)} %bitcast.129), channel_id=1, replica_groups=mesh['grp'=32,'feat'=4] {'feat'}, dimensions={0} | all-to-all | bytes 6029312 | tf_op jit(solution)/shard_map/all_to_all | solution.py:347
  267.7 0.9 copy-done.7
  268.6 1.2 convolution_convert_fusion
  270.2 1.2 copy.41
  271.4 4.6 %all-to-all-start.4 = ((bf16[128,40,128]{2,1,0:T(8,128)(2,1)}), bf16[128,40,128]{2,1,0:T(8,128)(2,1)S(1)}, u32[]{:S(2)}, u32[]{:S(2)}) async-start(bf16[128,40,128]{2,1,0:T(8,128)(2,1)} %bitcast.38), calls=%async_computation.4 | async-start | bytes 2621440 | tf_op jit(solution)/shard_map/all_to_all | solution.py:356
  276.8 1.0 fusion.39
  278.1 19.5 %all-to-all-done.4 = bf16[128,40,128]{2,1,0:T(8,128)(2,1)S(1)} async-done(((bf16[128,40,128]{2,1,0:T(8,128)(2,1)}), bf16[128,40,128]{2,1,0:T(8,128)(2,1)S(1)}, u32[]{:S(2)}, u32[]{:S(2)}) %all-to-all-start.4) | async-done | bytes 1310752 | tf_op jit(solution)/shard_map/all_to_all | solution.py:356
  297.7 1.1 fusion.9
  299.4 12.7 %all_to_all.39 = f32[4,256,128]{2,1,0:T(8,128)S(1)} all-to-all(f32[4,256,128]{2,1,0:T(8,128)S(1)} %copy.42), channel_id=1, replica_groups=mesh['grp'=32,'feat'=4] {'feat'}, dimensions={0} | all-to-all | bytes 1048576 | tf_op jit(solution)/shard_map/all_to_all | solution.py:368
  (110 shorter events, 14.0 us)
Async XLA Ops:
  0.0 297.7 %copy-start = (bf16[128,512]{1,0:T(8,128)(2,1)S(1)}, bf16[128,512]{1,0:T(8,128)(2,1)}, u32[]{:S(2)}) copy-start(bf16[128,512]{1,0:T(8,128)(2,1)} %param.28) | copy-start | bytes 393220
  0.0 11.2 %copy-start.8 = (s32[2816,10]{0,1:T(8,128)S(1)}, s32[2816,10]{0,1:T(8,128)}, u32[]{:S(2)}) copy-start(s32[2816,10]{0,1:T(8,128)} %param.21) | copy-start | bytes 337924
  0.0 11.2 %copy-start.11 = (s32[2816]{0:T(1024)S(1)}, s32[2816]{0:T(1024)}, u32[]{:S(2)}) copy-start(s32[2816]{0:T(1024)} %param.20) | copy-start | bytes 33796
  0.0 34.7 %collective-permute-start.6 = (f32[128]{0:T(128)}, f32[128]{0:T(128)S(1)}, u32[]{:S(2)}, u32[]{:S(2)}) collective-permute-start(f32[128]{0:T(128)} %param.26), channel_id=1, source_target_pairs={{0,1},{1,2},{2,3},{3,0},{4,5},{5,6},{6,7},{7,4},{8,9},{9,10},{10,1... | collective-permute-start | bytes 1544 | tf_op jit(solution)/shard_map/ppermute | solution.py:254
  1.7 34.9 %collective-permute-start.8 = (f32[128]{0:T(128)}, f32[128]{0:T(128)S(1)}, u32[]{:S(2)}, u32[]{:S(2)}) collective-permute-start(f32[128]{0:T(128)} %param.26), channel_id=1, source_target_pairs={{0,3},{1,0},{2,1},{3,2},{4,7},{5,4},{6,5},{7,6},{8,11},{9,8},{10,9... | collective-permute-start | bytes 1544 | tf_op jit(solution)/shard_map/ppermute | solution.py:254
  4.2 18.2 %copy-start.12 = (s32[2560]{0:T(1024)S(1)}, s32[2560]{0:T(1024)}, u32[]{:S(2)}) copy-start(s32[2560]{0:T(1024)} %param.23) | copy-start | bytes 30724
  5.2 64.2 %collective-permute-start.2 = (bf16[512,512]{1,0:T(8,128)(2,1)S(1)}, bf16[512,512]{1,0:T(8,128)(2,1)}, u32[]{:S(2)}, u32[]{:S(2)}) collective-permute-start(bf16[512,512]{1,0:T(8,128)(2,1)S(1)} %constant_dynamic-update-slice_fusion.1), channel_id=1, source_target_pairs={{0,3},{1,0},{2,1},{3,2},{4,7},{5,4},{6,5},{7,6},{8,11},{9,8},{10,9... | collective-permute-start | bytes 1572872 | tf_op jit(solution)/shard_map/ppermute | solution.py:252
  7.0 62.4 %collective-permute-start.1 = (bf16[512,512]{1,0:T(8,128)(2,1)S(1)}, bf16[512,512]{1,0:T(8,128)(2,1)}, u32[]{:S(2)}, u32[]{:S(2)}) collective-permute-start(bf16[512,512]{1,0:T(8,128)(2,1)S(1)} %constant_dynamic-update-slice_fusion.1), channel_id=1, source_target_pairs={{0,2},{1,3},{2,0},{3,1},{4,6},{5,7},{6,4},{7,5},{8,10},{9,11},{10,... | collective-permute-start | bytes 1572872 | tf_op jit(solution)/shard_map/ppermute | solution.py:252
  7.8 61.6 %collective-permute-start = (bf16[512,512]{1,0:T(8,128)(2,1)S(1)}, bf16[512,512]{1,0:T(8,128)(2,1)}, u32[]{:S(2)}, u32[]{:S(2)}) collective-permute-start(bf16[512,512]{1,0:T(8,128)(2,1)S(1)} %constant_dynamic-update-slice_fusion.1), channel_id=1, source_target_pairs={{0,1},{1,2},{2,3},{3,0},{4,5},{5,6},{6,7},{7,4},{8,9},{9,10},{10,1... | collective-permute-start | bytes 1572872 | tf_op jit(solution)/shard_map/ppermute | solution.py:252
  23.3 11.4 %copy-start.5 = (s32[192,128]{1,0:T(8,128)S(1)}, s32[192,128]{1,0:T(8,128)}, u32[]{:S(2)}) copy-start(s32[192,128]{1,0:T(8,128)} %mark_rows.1) | copy-start | bytes 294916
  23.3 13.3 %copy-start.15 = (f32[128]{0:T(128)S(1)}, f32[128]{0:T(128)}, u32[]{:S(2)}) copy-start(f32[128]{0:T(128)} %param.26) | copy-start | bytes 1540
  23.3 15.4 %copy-start.10 = (s32[1,32,6]{1,0,2:T(1,128)S(1)}, s32[1,32,6]{1,0,2:T(1,128)}, u32[]{:S(2)}) copy-start(s32[1,32,6]{1,0,2:T(1,128)} %param.18) | copy-start | bytes 2308
  24.1 23.0 %copy-start.2 = (bf16[4096,256]{1,0:T(8,128)(2,1)S(1)}, bf16[4096,256]{1,0:T(8,128)(2,1)}, u32[]{:S(2)}) copy-start(bf16[4096,256]{1,0:T(8,128)(2,1)} %cold.1) | copy-start | bytes 6291460
  24.1 23.0 %copy-start.13 = (s32[1,32]{1,0:T(1,128)S(1)}, s32[1,32]{1,0:T(1,128)}, u32[]{:S(2)}) copy-start(s32[1,32]{1,0:T(1,128)} %param.19) | copy-start | bytes 388
  24.1 21.4 %all-to-all-start.1 = ((s32[32,1,1024]{2,1,0:T(1,128)}), s32[32,1,1024]{2,1,0:T(1,128)S(1)}, u32[]{:S(2)}, u32[]{:S(2)}) async-start(s32[32,1,1024]{2,1,0:T(1,128)} %all_to_all.23), calls=%async_computation.1 | async-start | bytes 262144 | tf_op jit(solution)/shard_map/all_to_all | solution.py:299
  34.7 8.5 %collective-permute-start.3 = (bf16[128,512]{1,0:T(8,128)(2,1)}, bf16[128,512]{1,0:T(8,128)(2,1)S(1)}, u32[]{:S(2)}, u32[]{:S(2)}) collective-permute-start(bf16[128,512]{1,0:T(8,128)(2,1)} %param.27), channel_id=1, source_target_pairs={{0,1},{1,2},{2,3},{3,0},{4,5},{5,6},{6,7},{7,4},{8,9},{9,10},{10,1... | collective-permute-start | bytes 393224 | tf_op jit(solution)/shard_map/ppermute | solution.py:253
  36.6 5.8 %collective-permute-start.7 = (f32[128]{0:T(128)S(1)}, f32[128]{0:T(128)S(1)}, u32[]{:S(2)}, u32[]{:S(2)}) collective-permute-start(f32[128]{0:T(128)S(1)} %copy-done.15), channel_id=1, source_target_pairs={{0,2},{1,3},{2,0},{3,1},{4,6},{5,7},{6,4},{7,5},{8,10},{9,11},{10,... | collective-permute-start | bytes 1544 | tf_op jit(solution)/shard_map/ppermute | solution.py:254
  42.5 24.4 %collective-permute-start.5 = (bf16[128,512]{1,0:T(8,128)(2,1)}, bf16[128,512]{1,0:T(8,128)(2,1)}, u32[]{:S(2)}, u32[]{:S(2)}) collective-permute-start(bf16[128,512]{1,0:T(8,128)(2,1)} %param.27), channel_id=1, source_target_pairs={{0,3},{1,0},{2,1},{3,2},{4,7},{5,4},{6,5},{7,6},{8,11},{9,8},{10,9... | collective-permute-start | bytes 393224 | tf_op jit(solution)/shard_map/ppermute | solution.py:253
  43.2 2.3 copy-start.9
  43.2 23.6 %collective-permute-start.4 = (bf16[128,512]{1,0:T(8,128)(2,1)}, bf16[128,512]{1,0:T(8,128)(2,1)}, u32[]{:S(2)}, u32[]{:S(2)}) collective-permute-start(bf16[128,512]{1,0:T(8,128)(2,1)} %param.27), channel_id=1, source_target_pairs={{0,2},{1,3},{2,0},{3,1},{4,6},{5,7},{6,4},{7,5},{8,10},{9,11},{10,... | collective-permute-start | bytes 393224 | tf_op jit(solution)/shard_map/ppermute | solution.py:253
  45.5 1.5 copy-start.6
  225.0 40.4 %copy-start.1 = (bf16[4,512,512]{2,1,0:T(8,128)(2,1)S(1)}, bf16[4,512,512]{2,1,0:T(8,128)(2,1)}, u32[]{:S(2)}) copy-start(bf16[4,512,512]{2,1,0:T(8,128)(2,1)} %gather_fusion) | copy-start | bytes 6291460
  267.0 1.6 copy-start.4
  267.7 0.9 copy-start.7
  270.1 6.7 %copy-start.3 = (bf16[4,128,512]{2,1,0:T(8,128)(2,1)S(1)}, bf16[4,128,512]{2,1,0:T(8,128)(2,1)}, u32[]{:S(2)}) copy-start(bf16[4,128,512]{2,1,0:T(8,128)(2,1)} %gather_fusion.1) | copy-start | bytes 1572868
  271.4 26.3 %all-to-all-start.4 = ((bf16[128,40,128]{2,1,0:T(8,128)(2,1)}), bf16[128,40,128]{2,1,0:T(8,128)(2,1)S(1)}, u32[]{:S(2)}, u32[]{:S(2)}) async-start(bf16[128,40,128]{2,1,0:T(8,128)(2,1)} %bitcast.38), calls=%async_computation.4 | async-start | bytes 2621440 | tf_op jit(solution)/shard_map/all_to_all | solution.py:356
  299.0 13.1 %copy-start.14 = (f32[128]{0:T(128)S(1)}, f32[128]{0:T(128)}, u32[]{:S(2)}) copy-start(f32[128]{0:T(128)} %param.29) | copy-start | bytes 1540

commit v3 on v2

--- a/solution.py
+++ b/solution.py
@@ -12,11 +12,14 @@
 LANES = 128
 HOT = 16384
 MAIN = 480
-
-
-def mark_kernel(refs, before, need, acc):
+PREFIX_AT = 32
+FLAG_AT = 64
+
+
+def mark_kernel(refs, before, owners, extras, notes, look, acc):
     owner_rows = before.shape[0]
-    hot_rows = HOT
+    groups = notes.shape[0]
+    slot_count = owner_rows // groups
     acc[...] = jnp.zeros_like(acc)
     high = lax.broadcasted_iota(jnp.int32, (owner_rows, LANES), 0)
     low = lax.broadcasted_iota(jnp.int32, (LANES, LANES), 0)
@@ -24,7 +27,7 @@
     def count(g, carry):
         tall, wide = [], []
         for j in range(2):
-            cold = refs[pl.ds(2 * g + j, 1), :] - hot_rows
+            cold = refs[pl.ds(2 * g + j, 1), :] - HOT
             tall.append(jnp.where(high == cold >> 7, 1.0, 0.0).astype(jnp.bfloat16))
             wide.append(jnp.where(low == (cold & 127), 1.0, 0.0).astype(jnp.bfloat16))
         acc[...] += lax.dot_general(
@@ -37,12 +40,7 @@
 
     lax.fori_loop(0, refs.shape[0] // 2, count, 0, unroll=11)
     needed = jnp.where(acc[...] > 0.0, 1.0, 0.0)
-    upto = jnp.where(
-        lax.broadcasted_iota(jnp.int32, (LANES, LANES), 0)
-        <= lax.broadcasted_iota(jnp.int32, (LANES, LANES), 1),
-        1.0,
-        0.0,
-    )
+    upto = jnp.where(low <= lax.broadcasted_iota(jnp.int32, (LANES, LANES), 1), 1.0, 0.0)
     running = jnp.dot(
         needed.astype(jnp.bfloat16), upto.astype(jnp.bfloat16), preferred_element_type=jnp.float32
     )
@@ -52,68 +50,200 @@
         preferred_element_type=jnp.float32,
     )
     earlier = jnp.dot(before[...], totals.astype(jnp.bfloat16), preferred_element_type=jnp.float32)
-    place = running + earlier - 1.0
-    need[...] = jnp.where(needed > 0.0, place, -1.0).astype(jnp.int32)
-
-
-def mark_rows(refs, slot_count, groups):
+    local = jnp.where(needed > 0.0, running - 1.0, -1.0)
+    place = jnp.where(needed > 0.0, earlier + running - 1.0, -1.0)
+    spills = jnp.where(jnp.max(place) >= MAIN, 1, 0)
+    place = place.astype(jnp.int32)
+    lane = lax.broadcasted_iota(jnp.int32, (slot_count, LANES), 1)
+    slot_lane = lane - PREFIX_AT == lax.broadcasted_iota(jnp.int32, (slot_count, LANES), 0)
+    row_lane = lax.broadcasted_iota(jnp.int32, (1, LANES), 1)
+    for o in range(groups):
+        span = slice(o * slot_count, (o + 1) * slot_count)
+        notes[o, 0:slot_count, :] = place[span]
+        prefix = jnp.sum(jnp.where(slot_lane, earlier[span], 0.0), axis=0, keepdims=True)
+        last = jnp.where(row_lane < PREFIX_AT, extras[o, 1:2, :], prefix.astype(jnp.int32))
+        notes[o, slot_count : slot_count + 1, :] = extras[o, 0:1, :]
+        notes[o, slot_count + 1 : slot_count + 2, :] = jnp.where(row_lane >= FLAG_AT, spills, last)
+    across = jnp.transpose(earlier)[0:1]
+    eighth = jnp.floor(across * 0.125)
+    rest = jnp.zeros((5, owner_rows), jnp.float32)
+    rows = [jnp.transpose(local), owners[0:1, :], eighth, across - 8.0 * eighth, rest]
+    look[...] = jnp.concatenate(rows, axis=0).astype(jnp.bfloat16)
+
+
+def mark_rows(refs, extras, slot_count, groups):
     rows = groups * slot_count
     at = jnp.arange(rows, dtype=jnp.int32)
     before = (at[:, None] // slot_count == at[None, :] // slot_count) & (at[None, :] < at[:, None])
+    owners = jnp.broadcast_to((at // slot_count).astype(jnp.float32)[None, :], (8, rows))
     return pl.pallas_call(
         mark_kernel,
-        out_shape=jax.ShapeDtypeStruct((rows, LANES), jnp.int32),
-        in_specs=[pl.BlockSpec(memory_space=pltpu.VMEM)] * 2,
-        out_specs=pl.BlockSpec(memory_space=pltpu.VMEM),
+        out_shape=(
+            jax.ShapeDtypeStruct((groups, slot_count + 2, LANES), jnp.int32),
+            jax.ShapeDtypeStruct((LANES + 8, rows), jnp.bfloat16),
+        ),
+        in_specs=[pl.BlockSpec(memory_space=pltpu.VMEM)] * 4,
+        out_specs=(pl.BlockSpec(memory_space=pltpu.VMEM),) * 2,
         scratch_shapes=[pltpu.VMEM((rows, LANES), jnp.float32)],
         name="mark_rows",
-    )(refs.reshape(-1, LANES), before.astype(jnp.bfloat16))
-
-
-def pack_kernel(first, slot_count, blocks, counts, need, cold, out):
+    )(refs, before.astype(jnp.bfloat16), owners, extras)
+
+
+def remap_kernel(spill, groups, refs, look, *outs):
+    owner_rows = look.shape[1]
+    high = lax.broadcasted_iota(jnp.int32, (owner_rows, LANES), 0)
+    low = lax.broadcasted_iota(jnp.int32, (LANES, LANES), 0)
+    rows = outs[0].shape[0]
+    table = look[...]
+    for k, out in enumerate(outs):
+
+        def lookup(g, carry, k=k, out=out):
+            names = [refs[pl.ds(k * rows + 2 * g + j, 1), :] for j in range(2)]
+            tall = [
+                jnp.where(high == (name - HOT) >> 7, 1.0, 0.0).astype(jnp.bfloat16)
+                for name in names
+            ]
+            found = jnp.dot(
+                table, jnp.concatenate(tall, axis=1), preferred_element_type=jnp.float32
+            )
+            for j, name in enumerate(names):
+                part = found[:, j * LANES : (j + 1) * LANES]
+                local = jnp.where(low == ((name - HOT) & 127), part[:LANES], 0.0)
+                local = jnp.sum(local, axis=0, keepdims=True)
+                owner, eighth, unit = (part[LANES + n : LANES + n + 1] for n in range(3))
+                place = 8.0 * eighth + unit + local
+                cold = jnp.where(
+                    place < MAIN,
+                    HOT + owner * MAIN + place,
+                    HOT + groups * MAIN + owner * spill + place - MAIN,
+                ).astype(jnp.int32)
+                out[pl.ds(2 * g + j, 1), :] = jnp.where(name < HOT, name, cold) * 2
+            return carry
+
+        lax.fori_loop(0, rows // 2, lookup, 0, unroll=11)
+
+
+def remap(refs, look, nodes, spill, groups):
+    count = refs.shape[0] * LANES // nodes
+    outs = pl.pallas_call(
+        functools.partial(remap_kernel, spill, groups),
+        out_shape=[jax.ShapeDtypeStruct((nodes // LANES, LANES), jnp.int32)] * count,
+        in_specs=[pl.BlockSpec(memory_space=pltpu.VMEM)] * 2,
+        out_specs=[pl.BlockSpec(memory_space=pltpu.VMEM)] * count,
+        name="remap",
+    )(refs, look)
+    return tuple(out.reshape(nodes) for out in outs)
+
+
+def pack_kernel(first, slot_count, blocks, counts, prefix, need, cold, out, left, right):
     r = pl.program_id(0)
     rows = out.shape[1]
-    at = lax.broadcasted_iota(jnp.int32, (rows, BLK), 0) + first
-    total = jnp.zeros((rows, cold.shape[1]), jnp.float32)
-    for k in range(0, slot_count, 2):
-        picks, values = [], []
-        for j in (k, k + 1):
-            place = need[0, j : j + 1, :]
-            place = jnp.where(counts[r] > j, place, -1)
-            picks.append(jnp.where(at == place, 1.0, 0.0).astype(jnp.bfloat16))
-            origin = pl.multiple_of(blocks[r * slot_count + j] * BLK, BLK)
-            values.append(cold[pl.ds(origin, BLK), :])
-        total = total + jnp.dot(
-            jnp.concatenate(picks, axis=1),
-            jnp.concatenate(values, axis=0),
-            preferred_element_type=jnp.float32,
-        )
-    out[0] = total.astype(out.dtype)
-
-
-def pack_needed(blocks, counts, need, cold, first, rows):
+    at = lax.broadcasted_iota(jnp.int32, (BLK, BLK), 0)
+    for k in range(slot_count):
+        begin = prefix[r * slot_count + k]
+        place = need[0, k : k + 1, :] - begin
+        place = jnp.where(counts[r] > k, place, -1)
+        picks = jnp.where(at == place, 1.0, 0.0).astype(jnp.bfloat16)
+        origin = pl.multiple_of(blocks[r * slot_count + k] * BLK, BLK)
+        value = jnp.dot(picks, cold[pl.ds(origin, BLK), :], preferred_element_type=jnp.float32)
+        left[pl.ds(begin, BLK), :] = value[:, :LANES]
+        right[pl.ds(begin, BLK), :] = value[:, LANES:]
+    out[0, :, :LANES] = left[first : first + rows, :].astype(out.dtype)
+    out[0, :, LANES:] = right[first : first + rows, :].astype(out.dtype)
+
+
+def pack_needed(blocks, counts, prefix, need, cold, first, rows):
     groups = counts.shape[0]
     cols = cold.shape[1]
+    slot_count = blocks.shape[0] // groups
     return pl.pallas_call(
-        functools.partial(pack_kernel, first, blocks.shape[0] // groups),
+        functools.partial(pack_kernel, first, slot_count),
         grid=(groups,),
         out_shape=jax.ShapeDtypeStruct((groups, rows, cols), cold.dtype),
         in_specs=[
+            pl.BlockSpec(memory_space=pltpu.SMEM),
             pl.BlockSpec(memory_space=pltpu.SMEM),
             pl.BlockSpec(memory_space=pltpu.SMEM),
             pl.BlockSpec((1,) + need.shape[1:], lambda r: (r, 0, 0)),
             pl.BlockSpec(memory_space=pltpu.VMEM),
         ],
         out_specs=pl.BlockSpec((1, rows, cols), lambda r: (r, 0, 0)),
+        scratch_shapes=[pltpu.VMEM((slot_count * BLK + BLK, LANES), jnp.float32)] * 2,
         name="pack_needed",
-    )(blocks, counts, need, cold)
+    )(blocks, counts, prefix, need, cold)
+
+
+def layer_one_kernel(me, base, rows, *refs):
+    weights, (out, own_two, hidden, bias) = refs[:-4], refs[-4:]
+    parts = len(weights)
+    depth = rows.shape[2]
+    width = weights[0].shape[1]
+    groups, _, slots, cols = out.shape
+    own_part = own_two.shape[0]
+    total_rows = rows.shape[1]
+    sources = [lax.rem(me[0] - step + parts, parts) for step in range(parts)]
+    for source, weight in zip(sources, weights):
+        tail = weight[depth + cols : depth + cols + 8, :cols].astype(jnp.float32)
+        bias[:, pl.ds(pl.multiple_of(source * cols, cols), cols)] = (
+            tail[0:1] + tail[1:2] + tail[2:3]
+        )
+    chunk = total_rows // 4
+    for c in range(4):
+        span = slice(c * chunk, (c + 1) * chunk)
+        pre = jnp.broadcast_to(bias[...], (chunk, width))
+        for source, weight in zip(sources, weights):
+            pre = pre + jnp.dot(
+                rows[source, span, :], weight[0:depth, :], preferred_element_type=jnp.float32
+            )
+        h1 = jnp.maximum(pre, 0.0).astype(jnp.bfloat16).astype(jnp.float32)
+        for f in range(parts):
+            hidden[f, span, :] = h1[:, f * cols : (f + 1) * cols]
+    for f in range(parts):
+        hidden[f, total_rows:, :] = jnp.zeros((hidden.shape[1] - total_rows, cols), jnp.float32)
+    total = jnp.zeros((own_part, width), jnp.float32)
+    for source, weight in zip(sources, weights):
+        total = total + jnp.dot(
+            hidden[source, 0:own_part, :].astype(jnp.bfloat16),
+            weight[depth : depth + cols, :],
+            preferred_element_type=jnp.float32,
+        )
+    own_two[...] = total
+
+    def send(o, carry):
+        for f in range(parts):
+            out[o, f] = hidden[f, pl.ds(base[o], slots), :].astype(out.dtype)
+        return carry
+
+    lax.fori_loop(0, groups, send, 0)
+
+
+def layer_one(me, base, rows, weights, groups, slots, own_part):
+    parts, total_rows, _ = rows.shape
+    width = weights[0].shape[1]
+    cols = width // parts
+    return pl.pallas_call(
+        layer_one_kernel,
+        out_shape=(
+            jax.ShapeDtypeStruct((groups, parts, slots, cols), jnp.bfloat16),
+            jax.ShapeDtypeStruct((own_part, width), jnp.float32),
+        ),
+        in_specs=[pl.BlockSpec(memory_space=pltpu.SMEM)] * 2
+        + [pl.BlockSpec(memory_space=pltpu.VMEM)] * (1 + len(weights)),
+        out_specs=(pl.BlockSpec(memory_space=pltpu.VMEM),) * 2,
+        scratch_shapes=[
+            pltpu.VMEM((parts, total_rows + slots, cols), jnp.float32),
+            pltpu.VMEM((1, width), jnp.float32),
+        ],
+        name="layer_one",
+    )(me, base, rows, *weights)
 
 
 CHUNK = 1024
 DEPTH = 4
 
 
-def gather_kernel(source_count, index, where, dest, *refs):
+def gather_kernel(source_count, dest, *refs):
+    index, refs = refs[: S1 + 1], refs[S1 + 1 :]
     sources, (out, table, stage, acc, sems) = refs[:source_count], refs[source_count:]
     chunks = sum(source.shape[0] for source in sources) // CHUNK
     nodes = dest.shape[0]
@@ -165,9 +295,9 @@
 
     def node(i, carry):
         place = pl.multiple_of(dest[i], 2)
-        acc[pl.ds(place, 2), :] = table[pl.ds(pl.multiple_of(where[index[i]], 2), 2), :]
+        acc[pl.ds(place, 2), :] = table[pl.ds(pl.multiple_of(index[0][i], 2), 2), :]
         rows = [
-            table[pl.ds(pl.multiple_of(where[index[(k + 1) * nodes + i]], 2), 2), :] for k in range(S1)
+            table[pl.ds(pl.multiple_of(index[k + 1][i], 2), 2), :] for k in range(S1)
         ]
         while len(rows) > 1:
             rows = [a + b for a, b in zip(rows[::2], rows[1::2])] + rows[len(rows) // 2 * 2 :]
@@ -188,13 +318,13 @@
     lax.fori_loop(0, out.shape[0] // 16, finish, 0, unroll=2)
 
 
-def gather_rows(index, where, dest, sources, rows):
+def gather_rows(index, dest, sources, rows):
     cols = sources[0].shape[1]
     table_rows = sum(source.shape[0] for source in sources)
     return pl.pallas_call(
         functools.partial(gather_kernel, len(sources)),
         out_shape=jax.ShapeDtypeStruct((rows, 2 * cols), jnp.bfloat16),
-        in_specs=[pl.BlockSpec(memory_space=pltpu.SMEM)] * 3
+        in_specs=[pl.BlockSpec(memory_space=pltpu.SMEM)] * (1 + len(index))
         + [pl.BlockSpec(memory_space=pl.ANY)] * len(sources),
         out_specs=pl.BlockSpec(memory_space=pltpu.VMEM),
         scratch_shapes=[
@@ -205,7 +335,7 @@
         ],
         compiler_params=pltpu.CompilerParams(vmem_limit_bytes=60 * 1024 * 1024),
         name="gather_rows",
-    )(index, where, dest, *sources)
+    )(dest, *index, *sources)
 
 
 def per_device(
@@ -241,21 +371,18 @@
     feat_cols = cold_table.shape[1]
     slot_count = send_blocks.shape[2]
     fetch_rows = slot_count * BLK
-    index = jnp.concatenate([self_ref, neigh_ref.T.reshape(-1)])
-    need = mark_rows(index, slot_count, groups).reshape(groups, fetch_rows)
-    spills = (jnp.max(need) >= MAIN).astype(jnp.int32)
-
-    w1 = jnp.concatenate([w1_self, w1_neigh], axis=0)
-    w1_all, w2s_all, b1_all = [w1], [w2_self], [b1_bias]
+    refs = jnp.concatenate([self_ref, neigh_ref.T.reshape(-1)]).reshape(-1, LANES)
+
+    coarse = lax.reduce_precision(b1_bias, 8, 7)
+    middle = lax.reduce_precision(b1_bias - coarse, 8, 7)
+    fine = b1_bias - coarse - middle
+    bias_rows = jnp.stack([coarse, middle, fine]).astype(jnp.bfloat16)
+    bias_rows = jnp.pad(bias_rows, ((0, 16 - 3), (0, hidden - hidden_part)))
+    weight = jnp.concatenate([w1_self, w1_neigh, w2_self, bias_rows], axis=0)
+    weights = [weight]
     for step in range(1, parts):
         ring = [(s, (s + step) % parts) for s in range(parts)]
-        w1_all.append(lax.ppermute(w1, "feat", ring))
-        w2s_all.append(lax.ppermute(w2_self, "feat", ring))
-        b1_all.append(lax.ppermute(b1_bias, "feat", ring))
-    order = lax.rem(me - jnp.arange(parts) + parts, parts)
-    w1_all = jnp.stack(w1_all)[order]
-    w2s_all = jnp.stack(w2s_all)[order].reshape(hidden, hidden)
-    b1_all = jnp.stack(b1_all)[order].reshape(hidden)
+        weights.append(lax.ppermute(weight, "feat", ring))
 
     owner = route_owner[:, 0]
     onehot = (owner[:, None] == jnp.arange(groups, dtype=jnp.int32)[None, :]).astype(jnp.int32)
@@ -294,26 +421,22 @@
         preferred_element_type=jnp.float32,
     )
     send_slots = send_slots.astype(jnp.int32) - 1
-    flags = jnp.broadcast_to(spills, (groups, LANES - capacity % LANES))
-    notes = jnp.concatenate([need, send_slots, flags], axis=1)
+    extras = jnp.pad(send_slots, ((0, 0), (0, 2 * LANES - capacity))).reshape(groups, 2, LANES)
+    notes, look = mark_rows(refs, extras, slot_count, groups)
     notes = lax.all_to_all(notes, "grp", split_axis=0, concat_axis=0, tiled=True)
-    recv_slots = notes[:, fetch_rows : fetch_rows + capacity].reshape(groups * capacity)
-    spilled = jnp.max(notes[:, fetch_rows + capacity]) > 0
-
-    owner_at = jnp.arange(groups, dtype=jnp.int32)[:, None]
     spill = fetch_rows - MAIN
-    where = jnp.where(
-        need < MAIN,
-        HOT + owner_at * MAIN + need,
-        HOT + groups * MAIN + owner_at * spill + need - MAIN,
-    )
-    where = jnp.concatenate([jnp.arange(HOT, dtype=jnp.int32), where.reshape(-1)]) * 2
+    index = remap(refs, look, nodes, spill, groups)
+    recv_slots = notes[:, slot_count:, :].reshape(groups, -1)[:, :capacity]
+    recv_slots = recv_slots.reshape(groups * capacity)
+    spilled = jnp.max(notes[:, slot_count + 1, FLAG_AT]) > 0
+    prefix = notes[:, slot_count + 1, PREFIX_AT : PREFIX_AT + slot_count].reshape(-1)
 
     def exchange(first, rows, prepared):
         outgoing = pack_needed(
             send_blocks.reshape(-1),
             block_counts.reshape(-1),
-            notes.reshape(groups, -1, LANES),
+            prefix,
+            notes,
             cold_table,
             first,
             rows,
@@ -324,39 +447,28 @@
         return fetched.reshape(-1, feat_cols), prepared
 
     my_base = lax.dynamic_index_in_dim(base, me, 0, keepdims=False)
-    my_held = lax.dynamic_index_in_dim(held, me, 0, keepdims=False)
-    place = jnp.arange(slots, dtype=jnp.int32)[None, :]
-    source = jnp.where(place < my_held[:, None], my_base[:, None] + place, -1).reshape(-1)
-    spread = (source[:, None] == jnp.arange(part_rows, dtype=jnp.int32)[None, :]).astype(
-        jnp.bfloat16
-    )
-
-    prepared = (w1_all, w2s_all, b1_all, index, where, dest, recv_slots, spread, spilled)
+
+    prepared = (weights, index, dest, recv_slots, my_base, spilled)
     main, prepared = exchange(0, MAIN, prepared)
-    w1_all, w2s_all, b1_all, index, where, dest, recv_slots, spread, spilled = prepared
+    weights, index, dest, recv_slots, my_base, spilled = prepared
 
     def with_spill():
         extra, _ = exchange(MAIN, spill, ())
-        return gather_rows(index, where, dest, [hot_table, main, extra], parts * part_rows)
+        return gather_rows(index, dest, [hot_table, main, extra], parts * part_rows)
 
     def without_spill():
-        return gather_rows(index, where, dest, [hot_table, main], parts * part_rows)
+        return gather_rows(index, dest, [hot_table, main], parts * part_rows)
 
     rows = lax.cond(spilled, with_spill, without_spill)
     rows = rows.reshape(parts, part_rows, -1)
     rows = lax.all_to_all(rows, "feat", split_axis=0, concat_axis=0, tiled=True)
-    pre = b1_all[None, :]
-    for s in range(parts):
-        pre = pre + jnp.dot(rows[s], w1_all[s], preferred_element_type=jnp.float32)
-    h1 = jnp.maximum(pre, 0.0).astype(jnp.bfloat16)
-
-    send_rows = jnp.dot(spread, h1, preferred_element_type=jnp.float32).astype(jnp.bfloat16)
-    send_rows = send_rows.reshape(groups, slots, parts, hidden_part).transpose(0, 2, 1, 3)
+    send_rows, own_two = layer_one(
+        me.reshape(1), my_base, rows, weights, groups, slots, own_part
+    )
     send_rows = send_rows.reshape(groups * parts, slots, hidden_part)
     recv_rows = lax.all_to_all(send_rows, ("grp", "feat"), split_axis=0, concat_axis=0, tiled=True)
     recv_rows = recv_rows.reshape(groups * capacity, hidden_part)
 
-    own_two = jnp.dot(h1[:own_part], w2s_all, preferred_element_type=jnp.float32)
     member = jnp.arange(targets, dtype=jnp.int32)[:, None] == recv_slots[None, :]
     total = jnp.dot(member.astype(jnp.bfloat16), recv_rows, preferred_element_type=jnp.float32)
     count = jnp.sum(member.astype(jnp.float32), axis=1)

time: 315 us -> 278 us (0.88)
  local copies, waits for them, and re-layouts: 12.4 us -> 3.93 us
  Pallas kernels: 81.6 us -> 73.5 us
  starting transfers between devices: 26.2 us -> 18.9 us
  matrix products: 6.84 us -> 2.35 us
  other arithmetic: 11 us -> 6.71 us
    pallas_call x1, Pallas kernels: 54.7 us -> 36.4 us  [gather_rows(): pl.pallas_call(functools.partial(gather_kernel, len(sources)), out_shape=...]
    pallas_call x2 -> x4, Pallas kernels: 26.9 us -> 37 us  [the longest x1 17.3 us: pack_needed(): pl.pallas_call(functools.partial(pack_kernel, first, slot_count), grid=(g...]
    ppermute x9 -> x3, starting transfers between devices: 13.1 us -> 5.84 us  [per_device(): weights.append(lax.ppermute(weight, 'feat', ring))]
    dot_general x6 -> x0, matrix products: 4.49 us -> none  [the longest x4 2.27 us: per_device(): pre = pre + jnp.dot(rows[s], w1_all[s], preferred_element_type=jnp.float32)]
    gather x3 -> x0, local copies, waits for them, and re-layouts: 3.95 us -> none  [the longest x1 2.03 us: per_device(): w1_all = jnp.stack(w1_all)[order]]
  transfers between devices with their start and end apart: 11 -> 5, of which waited for: 2 -> 1; matrix products, arithmetic and copies ran while one was open for 6% -> 3% of each run, Pallas kernels for 9% -> 11%
where the time goes in v3:
time: 278 us
  blocking collectives  151 us (54%)
  Pallas kernels  73.5 us (26%)
  waiting for transfers between devices  20.6 us (7%)
  starting transfers between devices  18.9 us (7%)
  other arithmetic  6.71 us (2%)
  local copies, waits for them, and re-layouts  3.93 us (1%)
    all_to_all x1, blocking collectives, exchange(): lax.all_to_all(outgoing, 'grp', split_axis=0, concat_axis=0, tiled=True)  97.2 us
    all_to_all x1, blocking collectives, per_device(): rows = lax.all_to_all(rows, 'feat', split_axis=0, concat_axis=0, tiled=True)  40.7 us
    pallas_call x1, Pallas kernels, gather_rows(): pl.pallas_call(functools.partial(gather_kernel, len(sources)), out_shape=...  36.4 us
    all_to_all x1, waiting for transfers between devices, per_device(): lax.all_to_all(send_rows, ('grp', 'feat'), split_axis=0, concat_axis=0, t...  20.6 us
    pallas_call x1, Pallas kernels, pack_needed(): pl.pallas_call(functools.partial(pack_kernel, first, slot_count), grid=(g...  17.3 us
    all_to_all x1, blocking collectives, per_device(): lax.all_to_all(partial_two, 'feat', split_axis=0, concat_axis=0, tiled=True)  12.7 us
    all_to_all x1, starting transfers between devices, per_device(): lax.all_to_all(notes, 'grp', split_axis=0, concat_axis=0, tiled=True)  8.32 us
    pallas_call x1, Pallas kernels, mark_rows(): pl.pallas_call(mark_kernel, out_shape=(jax.ShapeDtypeStruct((groups, slot...  7.35 us
  transfers between devices with their start and end apart: 5, of which 1 were waited for; matrix products, arithmetic and copies ran while one was open for 3% of the time, Pallas kernels for 11%

profile of v3, /device:TPU:0, one launch (start us, length us, event | category | flops | bytes accessed | tf_op | source)
XLA Modules:
  0.0 277.6 jit_solution(3621165188580671817)
XLA Ops:
  0.0 0.7 fusion.53
  0.7 1.1 pad_maximum_fusion.refs_0_
  1.9 1.7 collective-permute-start
  3.6 2.7 collective-permute-start.1
  6.3 1.4 collective-permute-start.2
  8.0 0.3 fusion.21
  9.0 0.2 reduce_window_sum.13
  9.3 0.2 multiply_reduce_fusion
  9.7 0.9 fusion.12
  10.6 0.6 reshape.259.extras
  11.2 0.7 fusion.19.before
  12.0 0.7 add_bitcast_fusion.1.refs
  12.6 0.6 broadcast_in_dim.25.owners
  13.2 7.3 %mark_rows.1 = (s32[32,8,128]{2,1,0:T(8,128)}, bf16[136,192]{1,0:T(8,128)(2,1)}) custom-call(s32[242,128]{1,0:T(8,128)} %add_bitcast_fusion.1.refs, bf16[192,192]{1,0:T(8,128)(2,1)} %fusion.19.before, f32[8,192]{1,0:T(8,128)} %broadcast_in_dim.25.owners, s32[32,2,128]{2,1,0:T(2,128)} %reshape.259.extras), custom_call_target="tpu_custom_call" | custom-call | tf_op jit(solution)/shard_map/mark_rows/pallas_call | solution.py:79
  20.6 8.3 %all-to-all-start.1 = ((s32[32,8,128]{2,1,0:T(8,128)}), s32[32,8,128]{2,1,0:T(8,128)S(1)}, u32[]{:S(2)}, u32[]{:S(2)}) async-start(s32[32,8,128]{2,1,0:T(8,128)} %get-tuple-element.162), calls=%async_computation.1 | async-start | bytes 262144 | tf_op jit(solution)/shard_map/all_to_all | solution.py:426
  28.9 0.5 dynamic-slice_bitcast_fusion.base
  29.5 0.7 reshape.255.blocks
  30.2 6.5 %remap.1 = (s32[22,128]{1,0:T(8,128)S(1)}, s32[22,128]{1,0:T(8,128)S(1)}, s32[22,128]{1,0:T(8,128)S(1)}, s32[22,128]{1,0:T(8,128)S(1)}, s32[22,128]{1,0:T(8,128)...) custom-call(s32[242,128]{1,0:T(8,128)} %add_bitcast_fusion.1.refs, ...), custom_call_target="tpu_custom_call" | custom-call | tf_op jit(solution)/shard_map/remap/pallas_call | solution.py:128
  37.1 0.8 slice_reduce_fusion
  38.6 17.3 %pack_needed.3 = bf16[32,480,256]{2,1,0:T(8,128)(2,1)} custom-call(s32[192]{0:T(256)} %reshape.255.blocks, s32[32]{0:T(128)S(1)} %bitcast.118, s32[192]{0:T(256)S(1)} %reshape_squeeze.3.prefix, s32[32,8,128]{2,1,0:T(8,128)S(1)} %all-to-all-done.1.need, bf16[4096,256]{1,0:T(8,128)(2,1)S(1)} %copy-done.1), custom_call_target="tpu_custom_call" | custom-call | tf_op jit(solution)/shard_map/pack_needed/pallas_call | solution.py:159
  55.9 97.2 %all_to_all.30 = bf16[32,480,256]{2,1,0:T(8,128)(2,1)} all-to-all(bf16[32,480,256]{2,1,0:T(8,128)(2,1)} %pack_needed.3), channel_id=1, replica_groups=mesh['grp'=32,'feat'=4] {'grp'}, dimensions={0} | all-to-all | bytes 15728640 | tf_op jit(solution)/shard_map/all_to_all | solution.py:445
  153.1 36.4 %conditional.1 = (bf16[2944,512]{1,0:T(8,128)(2,1)S(1)}) conditional(s32[]{:T(128)} %convert_element_type.73, (s32[2816]{0:T(1024)S(1)}, s32[2816]{0:T(1024)S(1)}, s32[2816]{0:T(1024)S(1)}, s32[2816]{0:T(1024)S(1)}, s32[2816]{0:T(1024)S(1)}, /*index=5*/s32[2816]{0:T(1024)S(1)}, s32[2816]{0:T(1024)S(1)}, s32[2816]{0:T(1024)S(1)}, s32[2816]{0:T(1024)S(1)}, ...), branch_computations={%region_5.6_spmd, %region_6.7_spmd} | conditional | bytes 9440264 | solution.py:462
  153.1 36.4 %gather_rows.2 = bf16[2944,512]{1,0:T(8,128)(2,1)S(1)} custom-call(s32[2816]{0:T(1024)S(1)} %get-tuple-element.74.dest, s32[2816]{0:T(1024)S(1)} %get-tuple-element.75.refs_0_, s32[2816]{0:T(1024)S(1)} %get-tuple-element.76.refs_1_, s32[2816]{0:T(1024)S(1)} %get-tuple-element.77.refs_2_, s32[2816]{0:T(1024)S(1)} %get-tuple-element.78.refs_3_, ...), custom_call_target="tpu_custom_call" | custom-call | tf_op jit(solution)/shard_map/cond/branch_0_fun/gather_rows/pallas_call | solution.py:324
  189.6 40.7 %all_to_all.31.rows = bf16[4,736,512]{2,1,0:T(8,128)(2,1)} all-to-all(bf16[4,736,512]{2,1,0:T(8,128)(2,1)S(1)} %bitcast.88), channel_id=1, replica_groups=mesh['grp'=32,'feat'=4] {'feat'}, dimensions={0} | all-to-all | bytes 6029312 | tf_op jit(solution)/shard_map/all_to_all | solution.py:464
  230.2 5.9 %layer_one.1 = (bf16[32,4,40,128]{3,2,1,0:T(8,128)(2,1)}, f32[64,512]{1,0:T(8,128)}) custom-call(s32[1]{0:T(128)} %bitcast.23.me, s32[32]{0:T(128)} %dynamic-slice_bitcast_fusion.base, bf16[4,736,512]{2,1,0:T(8,128)(2,1)} %all_to_all.31.rows, bf16[656,512]{1,0:T(8,128)(2,1)} %copy-done.2, bf16[656,512]{1,0:T(8,128)(2,1)} %collective-permute-done.refs_1_, ...), custom_call_target="tpu_custom_call" | custom-call | tf_op jit(solution)/shard_map/layer_one/pallas_call | solution.py:224
  236.2 4.8 %all-to-all-start.4 = ((bf16[128,40,128]{2,1,0:T(8,128)(2,1)}), bf16[128,40,128]{2,1,0:T(8,128)(2,1)S(1)}, u32[]{:S(2)}, u32[]{:S(2)}) async-start(bf16[128,40,128]{2,1,0:T(8,128)(2,1)} %bitcast.89), calls=%async_computation.4 | async-start | bytes 2621440 | tf_op jit(solution)/shard_map/all_to_all | solution.py:469
  241.1 0.6 convert_reduce_fusion
  242.0 20.6 %all-to-all-done.4 = bf16[128,40,128]{2,1,0:T(8,128)(2,1)S(1)} async-done(((bf16[128,40,128]{2,1,0:T(8,128)(2,1)}), bf16[128,40,128]{2,1,0:T(8,128)(2,1)S(1)}, u32[]{:S(2)}, u32[]{:S(2)}) %all-to-all-start.4) | async-done | bytes 1310752 | tf_op jit(solution)/shard_map/all_to_all | solution.py:469
  262.6 1.1 fusion.8
  263.9 0.3 add_bitcast_fusion
  264.3 12.7 %all_to_all.32 = f32[4,256,128]{2,1,0:T(8,128)S(1)} all-to-all(f32[4,256,128]{2,1,0:T(8,128)S(1)} %copy.37), channel_id=1, replica_groups=mesh['grp'=32,'feat'=4] {'feat'}, dimensions={0} | all-to-all | bytes 1048576 | tf_op jit(solution)/shard_map/all_to_all | solution.py:480
  277.0 0.6 add_convert_fusion
  (61 shorter events, 2.3 us)
Async XLA Ops:
  0.0 262.6 %copy-start = (bf16[128,512]{1,0:T(8,128)(2,1)S(1)}, bf16[128,512]{1,0:T(8,128)(2,1)}, u32[]{:S(2)}) copy-start(bf16[128,512]{1,0:T(8,128)(2,1)} %param.28) | copy-start | bytes 393220
  0.0 7.7 %copy-start.8 = (s32[2560,1]{0,1:T(1,128)S(1)}, s32[2560,1]{0,1:T(1,128)}, u32[]{:S(2)}) copy-start(s32[2560,1]{0,1:T(1,128)} %param.22) | copy-start | bytes 30724
  1.9 8.7 %copy-start.2 = (bf16[656,512]{1,0:T(8,128)(2,1)}, bf16[656,512]{1,0:T(8,128)(2,1)S(1)}, u32[]{:S(2)}) copy-start(bf16[656,512]{1,0:T(8,128)(2,1)S(1)} %pad_maximum_fusion.refs_0_) | copy-start | bytes 2015236
  1.9 7.7 %copy-start.7 = (s32[2560]{0:T(1024)S(1)}, s32[2560]{0:T(1024)}, u32[]{:S(2)}) copy-start(s32[2560]{0:T(1024)} %param.23) | copy-start | bytes 30724
  1.9 54.0 %collective-permute-start = (bf16[656,512]{1,0:T(8,128)(2,1)S(1)}, bf16[656,512]{1,0:T(8,128)(2,1)}, u32[]{:S(2)}, u32[]{:S(2)}) collective-permute-start(bf16[656,512]{1,0:T(8,128)(2,1)S(1)} %pad_maximum_fusion.refs_0_), channel_id=1, source_target_pairs={{0,1},{1,2},{2,3},{3,0},{4,5},{5,6},{6,7},{7,4},{8,9},{9,10},{10,1... | collective-permute-start | bytes 2015240 | tf_op jit(solution)/shard_map/ppermute | solution.py:385
  3.6 52.3 %collective-permute-start.1 = (bf16[656,512]{1,0:T(8,128)(2,1)S(1)}, bf16[656,512]{1,0:T(8,128)(2,1)}, u32[]{:S(2)}, u32[]{:S(2)}) collective-permute-start(bf16[656,512]{1,0:T(8,128)(2,1)S(1)} %pad_maximum_fusion.refs_0_), channel_id=1, source_target_pairs={{0,2},{1,3},{2,0},{3,1},{4,6},{5,7},{6,4},{7,5},{8,10},{9,11},{10,... | collective-permute-start | bytes 2015240 | tf_op jit(solution)/shard_map/ppermute | solution.py:385
  6.3 49.6 %collective-permute-start.2 = (bf16[656,512]{1,0:T(8,128)(2,1)S(1)}, bf16[656,512]{1,0:T(8,128)(2,1)}, u32[]{:S(2)}, u32[]{:S(2)}) collective-permute-start(bf16[656,512]{1,0:T(8,128)(2,1)S(1)} %pad_maximum_fusion.refs_0_), channel_id=1, source_target_pairs={{0,3},{1,0},{2,1},{3,2},{4,7},{5,4},{6,5},{7,6},{8,11},{9,8},{10,9... | collective-permute-start | bytes 2015240 | tf_op jit(solution)/shard_map/ppermute | solution.py:385
  9.5 1.7 copy-start.3
  9.6 2.3 copy-start.5
  9.6 19.8 %copy-start.6 = (s32[1,32,6]{1,0,2:T(1,128)S(1)}, s32[1,32,6]{1,0,2:T(1,128)}, u32[]{:S(2)}) copy-start(s32[1,32,6]{1,0,2:T(1,128)} %param.18) | copy-start | bytes 2308
  9.7 29.0 %copy-start.1 = (bf16[4096,256]{1,0:T(8,128)(2,1)S(1)}, bf16[4096,256]{1,0:T(8,128)(2,1)}, u32[]{:S(2)}) copy-start(bf16[4096,256]{1,0:T(8,128)(2,1)} %cold.1) | copy-start | bytes 6291460
  10.6 28.1 %copy-start.9 = (s32[1,32]{1,0:T(1,128)S(1)}, s32[1,32]{1,0:T(1,128)}, u32[]{:S(2)}) copy-start(s32[1,32]{1,0:T(1,128)} %param.19) | copy-start | bytes 388
  20.6 16.2 %all-to-all-start.1 = ((s32[32,8,128]{2,1,0:T(8,128)}), s32[32,8,128]{2,1,0:T(8,128)S(1)}, u32[]{:S(2)}, u32[]{:S(2)}) async-start(s32[32,8,128]{2,1,0:T(8,128)} %get-tuple-element.162), calls=%async_computation.1 | async-start | bytes 262144 | tf_op jit(solution)/shard_map/all_to_all | solution.py:426
  236.2 5.6 %copy-start.4 = (f32[64,512]{1,0:T(8,128)S(1)}, f32[64,512]{1,0:T(8,128)}, u32[]{:S(2)}) copy-start(f32[64,512]{1,0:T(8,128)} %get-tuple-element.216) | copy-start | bytes 393220
  236.2 26.4 %all-to-all-start.4 = ((bf16[128,40,128]{2,1,0:T(8,128)(2,1)}), bf16[128,40,128]{2,1,0:T(8,128)(2,1)S(1)}, u32[]{:S(2)}, u32[]{:S(2)}) async-start(bf16[128,40,128]{2,1,0:T(8,128)(2,1)} %bitcast.89), calls=%async_computation.4 | async-start | bytes 2621440 | tf_op jit(solution)/shard_map/all_to_all | solution.py:469
  264.2 12.8 %copy-start.10 = (f32[128]{0:T(128)S(1)}, f32[128]{0:T(128)}, u32[]{:S(2)}) copy-start(f32[128]{0:T(128)} %param.29) | copy-start | bytes 1540

commit v4 on v3

--- a/solution.py
+++ b/solution.py
@@ -7,8 +7,8 @@
 from jax.experimental.pallas import tpu as pltpu
 from jax.sharding import PartitionSpec as P
 
+
 BLK = 128
-S1 = 10
 LANES = 128
 HOT = 16384
 MAIN = 480
@@ -173,14 +173,15 @@
     )(blocks, counts, prefix, need, cold)
 
 
-def layer_one_kernel(me, base, rows, *refs):
-    weights, (out, own_two, hidden, bias) = refs[:-4], refs[-4:]
-    parts = len(weights)
-    depth = rows.shape[2]
+def layer_one_kernel(parts, me, base, *refs):
+    own, mean, weights = (refs[n * parts : (n + 1) * parts] for n in range(3))
+    out, own_two, hidden, bias, product = refs[3 * parts :]
+    half = own[0].shape[1]
+    depth = 2 * half
     width = weights[0].shape[1]
     groups, _, slots, cols = out.shape
     own_part = own_two.shape[0]
-    total_rows = rows.shape[1]
+    total_rows = own[0].shape[0]
     sources = [lax.rem(me[0] - step + parts, parts) for step in range(parts)]
     for source, weight in zip(sources, weights):
         tail = weight[depth + cols : depth + cols + 8, :cols].astype(jnp.float32)
@@ -191,9 +192,12 @@
     for c in range(4):
         span = slice(c * chunk, (c + 1) * chunk)
         pre = jnp.broadcast_to(bias[...], (chunk, width))
-        for source, weight in zip(sources, weights):
+        for self_x, neigh_x, weight in zip(own, mean, weights):
             pre = pre + jnp.dot(
-                rows[source, span, :], weight[0:depth, :], preferred_element_type=jnp.float32
+                self_x[span, :], weight[0:half, :], preferred_element_type=jnp.float32
+            )
+            pre = pre + jnp.dot(
+                neigh_x[span, :], weight[half:depth, :], preferred_element_type=jnp.float32
             )
         h1 = jnp.maximum(pre, 0.0).astype(jnp.bfloat16).astype(jnp.float32)
         for f in range(parts):
@@ -207,7 +211,10 @@
             weight[depth : depth + cols, :],
             preferred_element_type=jnp.float32,
         )
-    own_two[...] = total
+    product[...] = total
+    for step in range(parts):
+        column = pl.multiple_of(lax.rem(me[0] + step, parts) * cols, cols)
+        own_two[:, step * cols : (step + 1) * cols] = product[:, pl.ds(column, cols)]
 
     def send(o, carry):
         for f in range(parts):
@@ -217,35 +224,38 @@
     lax.fori_loop(0, groups, send, 0)
 
 
-def layer_one(me, base, rows, weights, groups, slots, own_part):
-    parts, total_rows, _ = rows.shape
+def layer_one(me, base, own, mean, weights, groups, slots, own_part):
+    parts = len(weights)
+    total_rows = own[0].shape[0]
     width = weights[0].shape[1]
     cols = width // parts
     return pl.pallas_call(
-        layer_one_kernel,
+        functools.partial(layer_one_kernel, parts),
         out_shape=(
             jax.ShapeDtypeStruct((groups, parts, slots, cols), jnp.bfloat16),
             jax.ShapeDtypeStruct((own_part, width), jnp.float32),
         ),
         in_specs=[pl.BlockSpec(memory_space=pltpu.SMEM)] * 2
-        + [pl.BlockSpec(memory_space=pltpu.VMEM)] * (1 + len(weights)),
+        + [pl.BlockSpec(memory_space=pltpu.VMEM)] * (3 * parts),
         out_specs=(pl.BlockSpec(memory_space=pltpu.VMEM),) * 2,
         scratch_shapes=[
             pltpu.VMEM((parts, total_rows + slots, cols), jnp.float32),
             pltpu.VMEM((1, width), jnp.float32),
+            pltpu.VMEM((own_part, width), jnp.float32),
         ],
         name="layer_one",
-    )(me, base, rows, *weights)
+    )(me, base, *own, *mean, *weights)
 
 
 CHUNK = 1024
 DEPTH = 4
 
 
-def gather_kernel(source_count, dest, *refs):
-    index, refs = refs[: S1 + 1], refs[S1 + 1 :]
-    sources, (out, table, stage, acc, sems) = refs[:source_count], refs[source_count:]
-    chunks = sum(source.shape[0] for source in sources) // CHUNK
+def gather_kernel(columns, source_count, dest, extent, *refs):
+    index, refs = refs[:columns], refs[columns:]
+    sources, refs = refs[:source_count], refs[source_count:]
+    outs, (table, stage, acc, sems) = refs[:-4], refs[-4:]
+    chunks = extent[0]
     nodes = dest.shape[0]
 
     def copy(c, slot):
@@ -291,51 +301,71 @@
 
     lax.fori_loop(0, chunks, load, 0)
 
-    total = acc.shape[0] // 2
-
     def node(i, carry):
-        place = pl.multiple_of(dest[i], 2)
-        acc[pl.ds(place, 2), :] = table[pl.ds(pl.multiple_of(index[0][i], 2), 2), :]
-        rows = [
-            table[pl.ds(pl.multiple_of(index[k + 1][i], 2), 2), :] for k in range(S1)
-        ]
+        rows = [table[pl.ds(pl.multiple_of(column[i], 2), 2), :] for column in index]
         while len(rows) > 1:
             rows = [a + b for a, b in zip(rows[::2], rows[1::2])] + rows[len(rows) // 2 * 2 :]
-        acc[pl.ds(total + place, 2), :] = rows[0]
+        acc[pl.ds(pl.multiple_of(dest[i], 2), 2), :] = rows[0]
         return carry
 
     lax.fori_loop(0, nodes, node, 0, unroll=8)
 
-    def finish(g, carry):
-        row = pl.multiple_of(g * 32, 32)
-        own = [acc[pl.ds(row + j, 16, stride=2), :] for j in range(2)]
-        mean = [acc[pl.ds(total + row + j, 16, stride=2), :] / S1 for j in range(2)]
-        out[pl.ds(pl.multiple_of(g * 16, 16), 16), :] = jnp.concatenate(own + mean, axis=1).astype(
-            jnp.bfloat16
-        )
-        return carry
-
-    lax.fori_loop(0, out.shape[0] // 16, finish, 0, unroll=2)
-
-
-def gather_rows(index, dest, sources, rows):
+    for f, out in enumerate(outs):
+        first = 2 * f * out.shape[0]
+
+        def finish(g, carry, first=first, out=out):
+            row = pl.multiple_of(first + g * 32, 32)
+            halves = [acc[pl.ds(row + j, 16, stride=2), :] for j in range(2)]
+            if columns > 1:
+                halves = [half / columns for half in halves]
+            out[pl.ds(pl.multiple_of(g * 16, 16), 16), :] = jnp.concatenate(halves, axis=1).astype(
+                jnp.bfloat16
+            )
+            return carry
+
+        lax.fori_loop(0, out.shape[0] // 16, finish, 0, unroll=2)
+
+
+def gather_rows(index, dest, extent, sources, parts, rows):
     cols = sources[0].shape[1]
     table_rows = sum(source.shape[0] for source in sources)
     return pl.pallas_call(
-        functools.partial(gather_kernel, len(sources)),
-        out_shape=jax.ShapeDtypeStruct((rows, 2 * cols), jnp.bfloat16),
-        in_specs=[pl.BlockSpec(memory_space=pltpu.SMEM)] * (1 + len(index))
+        functools.partial(gather_kernel, len(index), len(sources)),
+        out_shape=[jax.ShapeDtypeStruct((rows, cols), jnp.bfloat16)] * parts,
+        in_specs=[pl.BlockSpec(memory_space=pltpu.SMEM)] * (2 + len(index))
         + [pl.BlockSpec(memory_space=pl.ANY)] * len(sources),
-        out_specs=pl.BlockSpec(memory_space=pltpu.VMEM),
+        out_specs=[pl.BlockSpec(memory_space=pltpu.VMEM)] * parts,
         scratch_shapes=[
             pltpu.VMEM((2 * table_rows, LANES), jnp.float32),
             pltpu.VMEM((DEPTH, CHUNK, cols), jnp.bfloat16),
-            pltpu.VMEM((4 * rows, LANES), jnp.float32),
+            pltpu.VMEM((2 * parts * rows, LANES), jnp.float32),
             pltpu.SemaphoreType.DMA((DEPTH,)),
         ],
         compiler_params=pltpu.CompilerParams(vmem_limit_bytes=60 * 1024 * 1024),
-        name="gather_rows",
-    )(dest, *index, *sources)
+    )(dest, extent, *index, *sources)
+
+
+def unused_kernel(out):
+    out[...] = jnp.zeros_like(out)
+
+
+def unused_rows(rows, cols, dtype):
+    return pl.pallas_call(
+        unused_kernel,
+        grid=(1,),
+        out_shape=jax.ShapeDtypeStruct((rows, cols), dtype),
+        out_specs=pl.BlockSpec((16, cols), lambda i: (0, 0)),
+        name="unused_rows",
+    )()
+
+
+def send_round(chunks):
+    parts = len(chunks)
+    received = [chunks[0]]
+    for step in range(1, parts):
+        ring = [(s, (s + step) % parts) for s in range(parts)]
+        received.append(lax.ppermute(chunks[step], "feat", ring))
+    return received
 
 
 def per_device(
@@ -407,9 +437,9 @@
     owner_base = jnp.sum(onehot[:, :, None] * base.T[None, :, :], axis=1)
     mine = quarter[:, None] == jnp.arange(parts)[None, :]
     row_base = jnp.sum(jnp.where(mine, owner_base, 0), axis=1)
-    routed_dest = quarter * part_rows + row_base + depth
+    routed_dest = (quarter - me + parts) % parts * part_rows + row_base + depth
     own = jnp.arange(targets, dtype=jnp.int32)
-    own_dest = own // own_part * part_rows + own % own_part
+    own_dest = (own // own_part - me + parts) % parts * part_rows + own % own_part
     dest = jnp.concatenate([own_dest, routed_dest]) * 2
 
     column = quarter * slots + depth
@@ -448,22 +478,32 @@
 
     my_base = lax.dynamic_index_in_dim(base, me, 0, keepdims=False)
 
-    prepared = (weights, index, dest, recv_slots, my_base, spilled)
+    turned = lax.dynamic_slice_in_dim(
+        jnp.concatenate([w2_neigh, w2_neigh], axis=1), me * hidden_part, hidden, 1
+    )
+    prepared = (weights, index, dest, recv_slots, my_base, spilled, turned)
     main, prepared = exchange(0, MAIN, prepared)
-    weights, index, dest, recv_slots, my_base, spilled = prepared
-
-    def with_spill():
-        extra, _ = exchange(MAIN, spill, ())
-        return gather_rows(index, dest, [hot_table, main, extra], parts * part_rows)
-
-    def without_spill():
-        return gather_rows(index, dest, [hot_table, main], parts * part_rows)
-
-    rows = lax.cond(spilled, with_spill, without_spill)
-    rows = rows.reshape(parts, part_rows, -1)
-    rows = lax.all_to_all(rows, "feat", split_axis=0, concat_axis=0, tiled=True)
+    weights, index, dest, recv_slots, my_base, spilled, turned = prepared
+
+    extent = (HOT + groups * MAIN + jnp.where(spilled, groups * spill, 0)) // CHUNK
+    extent = extent.astype(jnp.int32).reshape(1)
+
+    def gather_own(extra):
+        own = gather_rows(index[:1], dest, extent, [hot_table, main, extra], parts, part_rows)
+        return own, extra
+
+    own_rows, extra = lax.cond(
+        spilled,
+        lambda: gather_own(exchange(MAIN, spill, ())[0]),
+        lambda: gather_own(unused_rows(groups * spill, feat_cols, cold_table.dtype)),
+    )
+    sources = [hot_table, main, extra]
+    own_rows, others = lax.optimization_barrier((own_rows, index[1:]))
+    own_rows = send_round(own_rows)
+    mean_rows = gather_rows(others, dest, extent, sources, parts, part_rows)
+    mean_rows = send_round(mean_rows)
     send_rows, own_two = layer_one(
-        me.reshape(1), my_base, rows, weights, groups, slots, own_part
+        me.reshape(1), my_base, own_rows, mean_rows, weights, groups, slots, own_part
     )
     send_rows = send_rows.reshape(groups * parts, slots, hidden_part)
     recv_rows = lax.all_to_all(send_rows, ("grp", "feat"), split_axis=0, concat_axis=0, tiled=True)
@@ -473,12 +513,12 @@
     total = jnp.dot(member.astype(jnp.bfloat16), recv_rows, preferred_element_type=jnp.float32)
     count = jnp.sum(member.astype(jnp.float32), axis=1)
     neigh_h = (total / jnp.maximum(count, 1.0)[:, None]).astype(jnp.bfloat16)
-    partial_two = jnp.dot(neigh_h, w2_neigh, preferred_element_type=jnp.float32)
+    partial_two = jnp.dot(neigh_h, turned, preferred_element_type=jnp.float32)
     holds = (jnp.arange(parts) == me)[:, None, None]
     partial_two = partial_two.reshape(parts, own_part, hidden) + jnp.where(holds, own_two[None], 0.0)
-    partial_two = partial_two.reshape(targets, parts, hidden_part).transpose(1, 0, 2)
-    shared = lax.all_to_all(partial_two, "feat", split_axis=0, concat_axis=0, tiled=True)
-    return (jnp.sum(shared, axis=0) + b2_bias).astype(jnp.bfloat16)
+    partial_two = partial_two.reshape(targets, hidden)
+    shared = send_round(jnp.split(partial_two, parts, axis=1))
+    return (sum(shared[1:], shared[0]) + b2_bias).astype(jnp.bfloat16)
 
 
 def solution(mesh):

time: 278 us -> 294 us (1.058)
  blocking collectives: 151 us -> 97.3 us
  waiting for transfers between devices: 20.6 us -> 59.3 us
  Pallas kernels: 73.5 us -> 92.5 us
  starting transfers between devices: 18.9 us -> 29.8 us
    all_to_all x2 -> x0, blocking collectives: 53.4 us -> none  [the longest x1 40.7 us: per_device(): rows = lax.all_to_all(rows, 'feat', split_axis=0, concat_axis=0, tiled=True)]
    ppermute x0 -> x9, waiting for transfers between devices: none -> 38.5 us  [send_round(): received.append(lax.ppermute(chunks[step], 'feat', ring))]
    pallas_call x2 -> x4, Pallas kernels: 42.4 us -> 60.8 us  [the longest x2 54.3 us: gather_rows(): pl.pallas_call(functools.partial(gather_kernel, len(index), len(sources))...]
    ppermute x0 -> x9, starting transfers between devices: none -> 9.75 us  [send_round(): received.append(lax.ppermute(chunks[step], 'feat', ring))]
  transfers between devices with their start and end apart: 5 -> 14, of which waited for: 1 -> 8; matrix products, arithmetic and copies ran while one was open for 3% -> 3% of each run, Pallas kernels for 11% -> 11%
where the time goes in v4:
time: 294 us; the launch traced here: 293 us
  blocking collectives  97.3 us (33%)
  Pallas kernels  92.5 us (31%)
  waiting for transfers between devices  59.3 us (20%)
  starting transfers between devices  29.8 us (10%)
  other arithmetic  6.28 us (2%)
  local copies, waits for them, and re-layouts  4.39 us (1%)
    all_to_all x1, blocking collectives, exchange(): lax.all_to_all(outgoing, 'grp', split_axis=0, concat_axis=0, tiled=True)  97.3 us
    pallas_call x2, Pallas kernels, gather_rows(): pl.pallas_call(functools.partial(gather_kernel, len(index), len(sources))...  54.3 us
    ppermute x9, waiting for transfers between devices, send_round(): received.append(lax.ppermute(chunks[step], 'feat', ring))  38.5 us
    all_to_all x1, waiting for transfers between devices, per_device(): lax.all_to_all(send_rows, ('grp', 'feat'), split_axis=0, concat_axis=0, t...  20.8 us
    pallas_call x1, Pallas kernels, pack_needed(): pl.pallas_call(functools.partial(pack_kernel, first, slot_count), grid=(g...  17.2 us
    ppermute x9, starting transfers between devices, send_round(): received.append(lax.ppermute(chunks[step], 'feat', ring))  9.75 us
    all_to_all x1, starting transfers between devices, per_device(): lax.all_to_all(notes, 'grp', split_axis=0, concat_axis=0, tiled=True)  8.34 us
    pallas_call x1, Pallas kernels, mark_rows(): pl.pallas_call(mark_kernel, out_shape=(jax.ShapeDtypeStruct((groups, slot...  7.35 us
  transfers between devices with their start and end apart: 14, of which 8 were waited for; matrix products, arithmetic and copies ran while one was open for 3% of the time, Pallas kernels for 11%

profile of v4, /device:TPU:0, one launch (start us, length us, event | category | flops | bytes accessed | tf_op | source)
XLA Modules:
  0.0 292.8 jit_solution(14021498441409120982)
XLA Ops:
  0.7 1.1 pad_maximum_fusion.refs_8_
  1.9 1.7 collective-permute-start
  3.5 2.7 collective-permute-start.1
  6.3 1.4 collective-permute-start.2
  9.6 0.9 fusion.12
  11.2 0.7 fusion.20.before
  13.2 7.4 %mark_rows.1 = (s32[32,8,128]{2,1,0:T(8,128)}, bf16[136,192]{1,0:T(8,128)(2,1)}) custom-call(s32[242,128]{1,0:T(8,128)} %add_bitcast_fusion.refs, bf16[192,192]{1,0:T(8,128)(2,1)} %fusion.20.before, f32[8,192]{1,0:T(8,128)} %broadcast_in_dim.25.owners, s32[32,2,128]{2,1,0:T(2,128)} %reshape.256.extras), custom_call_target="tpu_custom_call" | custom-call | tf_op jit(solution)/shard_map/mark_rows/pallas_call | solution.py:79
  20.5 8.3 %all-to-all-start.1 = ((s32[32,8,128]{2,1,0:T(8,128)}), s32[32,8,128]{2,1,0:T(8,128)S(1)}, u32[]{:S(2)}, u32[]{:S(2)}) async-start(s32[32,8,128]{2,1,0:T(8,128)} %get-tuple-element.138), calls=%async_computation.1 | async-start | bytes 262144 | tf_op jit(solution)/shard_map/all_to_all | solution.py:456
  29.6 0.7 reshape.252.blocks
  30.3 7.1 %remap.1 = (s32[22,128]{1,0:T(8,128)S(1)}, s32[22,128]{1,0:T(8,128)}, s32[22,128]{1,0:T(8,128)}, s32[22,128]{1,0:T(8,128)}, s32[22,128]{1,0:T(8,128)}, /*index=5...) custom-call(s32[242,128]{1,0:T(8,128)} %add_bitcast_fusion.refs, ...), custom_call_target="tpu_custom_call" | custom-call | tf_op jit(solution)/shard_map/remap/pallas_call | solution.py:128
  37.8 0.7 slice_reduce_fusion
  39.1 17.2 %pack_needed.3 = bf16[32,480,256]{2,1,0:T(8,128)(2,1)} custom-call(s32[192]{0:T(256)} %reshape.252.blocks, s32[32]{0:T(128)S(1)} %bitcast.111, s32[192]{0:T(256)S(1)} %reshape_squeeze.3.prefix, s32[32,8,128]{2,1,0:T(8,128)S(1)} %all-to-all-done.1.need, bf16[4096,256]{1,0:T(8,128)(2,1)S(1)} %copy-done), custom_call_target="tpu_custom_call" | custom-call | tf_op jit(solution)/shard_map/pack_needed/pallas_call | solution.py:159
  56.4 97.3 %all_to_all.20 = bf16[32,480,256]{2,1,0:T(8,128)(2,1)} all-to-all(bf16[32,480,256]{2,1,0:T(8,128)(2,1)} %pack_needed.3), channel_id=1, replica_groups=mesh['grp'=32,'feat'=4] {'grp'}, dimensions={0} | all-to-all | bytes 15728640 | tf_op jit(solution)/shard_map/all_to_all | solution.py:475
  153.6 19.4 %conditional.1 = (bf16[736,256]{1,0:T(8,128)(2,1)S(1)}, bf16[736,256]{1,0:T(8,128)(2,1)S(1)}, bf16[736,256]{1,0:T(8,128)(2,1)}, bf16[736,256]{1,0:T(8,128)(2,1)}, bf16[9216,256]{1,0:T(8,128)(2,1)}) conditional(s32[]{:T(128)} %convert_element_type.73, (s32[2816]{0:T(1024)S(1)}, s32[1]{0:T(128)}, s32[2816]{0:T(1024)S(1)}, bf16[16384,256]{1,0:T(8,128)(2,1)}, ...), branch_computations={%region_5.6_spmd, %region_6.7_spmd} | conditional | bytes 9440296 | solution.py:495
  154.2 18.8 %branch_0_fun.1 = (bf16[736,256]{1,0:T(8,128)(2,1)S(1)}, bf16[736,256]{1,0:T(8,128)(2,1)S(1)}, bf16[736,256]{1,0:T(8,128)(2,1)}, bf16[736,256]{1,0:T(8,128)(2,1)}) custom-call(s32[2816]{0:T(1024)S(1)} %get-tuple-element.35.dest, s32[1]{0:T(128)} %get-tuple-element.36.extent, s32[2816]{0:T(1024)S(1)} %get-tuple-element.37.refs_0_, ...), custom_call_target="tpu_custom_call" | custom-call | tf_op jit(solution)/shard_map/cond/branch_0_fun/pallas_call | solution.py:332
  173.1 35.5 %shard_map.136 = (bf16[736,256]{1,0:T(8,128)(2,1)}, bf16[736,256]{1,0:T(8,128)(2,1)}, bf16[736,256]{1,0:T(8,128)(2,1)}, bf16[736,256]{1,0:T(8,128)(2,1)}) custom-call(s32[2816]{0:T(1024)S(1)} %add_multiply_fusion.dest, s32[1]{0:T(128)} %bitcast.24.extent, s32[2816]{0:T(1024)} %bitcast.101, s32[2816]{0:T(1024)} %bitcast.102, s32[2816]{0:T(1024)} %bitcast.103, ...), custom_call_target="tpu_custom_call" | custom-call | tf_op jit(solution)/shard_map/pallas_call | solution.py:332
  208.6 0.8 collective-permute-start.6
  209.4 0.9 collective-permute-start.7
  210.3 1.9 collective-permute-start.8
  212.2 0.8 collective-permute-start.3
  213.0 2.1 collective-permute-start.4
  215.0 15.0 %collective-permute-done.6.refs_5_ = bf16[736,256]{1,0:T(8,128)(2,1)S(1)} collective-permute-done((bf16[736,256]{1,0:T(8,128)(2,1)}, bf16[736,256]{1,0:T(8,128)(2,1)S(1)}, u32[]{:S(2)}, u32[]{:S(2)}) %collective-permute-start.6) | collective-permute-done | bytes 376864 | tf_op jit(solution)/shard_map/ppermute | solution.py:367
  230.0 0.9 collective-permute-done.8.refs_7_
  230.9 15.0 %collective-permute-done.3.refs_1_ = bf16[736,256]{1,0:T(8,128)(2,1)S(1)} collective-permute-done((bf16[736,256]{1,0:T(8,128)(2,1)S(1)}, bf16[736,256]{1,0:T(8,128)(2,1)S(1)}, u32[]{:S(2)}, u32[]{:S(2)}) %collective-permute-start.3) | collective-permute-done | bytes 376864 | tf_op jit(solution)/shard_map/ppermute | solution.py:367
  247.4 5.8 %layer_one.1 = (bf16[32,4,40,128]{3,2,1,0:T(8,128)(2,1)}, f32[64,512]{1,0:T(8,128)}) custom-call(s32[1]{0:T(128)} %bitcast.23.me, s32[32]{0:T(128)} %fusion.70.base, bf16[736,256]{1,0:T(8,128)(2,1)S(1)} %get-tuple-element.192.refs_0_, bf16[736,256]{1,0:T(8,128)(2,1)} %copy-done.5, bf16[736,256]{1,0:T(8,128)(2,1)} %copy-done.6, bf16[736,256]{1,0:T(8,128)(2,1)} %copy-done.7, ...), custom_call_target="tpu_custom_call" | custom-call | tf_op jit(solution)/shard_map/layer_one/pallas_call | solution.py:232
  253.2 5.9 %all-to-all-start.3 = ((bf16[128,40,128]{2,1,0:T(8,128)(2,1)}), bf16[128,40,128]{2,1,0:T(8,128)(2,1)S(1)}, u32[]{:S(2)}, u32[]{:S(2)}) async-start(bf16[128,40,128]{2,1,0:T(8,128)(2,1)} %bitcast.93), calls=%async_computation.3 | async-start | bytes 2621440 | tf_op jit(solution)/shard_map/all_to_all | solution.py:509
  259.9 20.8 %all-to-all-done.3 = bf16[128,40,128]{2,1,0:T(8,128)(2,1)S(1)} async-done(((bf16[128,40,128]{2,1,0:T(8,128)(2,1)}), bf16[128,40,128]{2,1,0:T(8,128)(2,1)S(1)}, u32[]{:S(2)}, u32[]{:S(2)}) %all-to-all-start.3) | async-done | bytes 1310752 | tf_op jit(solution)/shard_map/all_to_all | solution.py:509
  280.7 1.1 fusion.17
  281.9 1.2 collective-permute-start.10
  283.0 2.2 collective-permute-start.11
  285.2 4.6 %collective-permute-done.10 = f32[256,128]{1,0:T(8,128)S(1)} collective-permute-done((f32[256,128]{1,0:T(8,128)S(1)}, f32[256,128]{1,0:T(8,128)S(1)}, u32[]{:S(2)}, u32[]{:S(2)}) %collective-permute-start.10) | collective-permute-done | bytes 131104 | tf_op jit(solution)/shard_map/ppermute | solution.py:367
  290.2 1.9 collective-permute-done.9
  (88 shorter events, 9.5 us)
Async XLA Ops:
  0.0 7.7 %copy-start.14 = (s32[2560,1]{0,1:T(1,128)S(1)}, s32[2560,1]{0,1:T(1,128)}, u32[]{:S(2)}) copy-start(s32[2560,1]{0,1:T(1,128)} %param.22) | copy-start | bytes 30724
  1.8 8.7 %copy-start.1 = (bf16[656,512]{1,0:T(8,128)(2,1)}, bf16[656,512]{1,0:T(8,128)(2,1)S(1)}, u32[]{:S(2)}) copy-start(bf16[656,512]{1,0:T(8,128)(2,1)S(1)} %pad_maximum_fusion.refs_8_) | copy-start | bytes 2015236
  1.9 7.7 %copy-start.13 = (s32[2560]{0:T(1024)S(1)}, s32[2560]{0:T(1024)}, u32[]{:S(2)}) copy-start(s32[2560]{0:T(1024)} %param.23) | copy-start | bytes 30724
  1.9 54.5 %collective-permute-start = (bf16[656,512]{1,0:T(8,128)(2,1)S(1)}, bf16[656,512]{1,0:T(8,128)(2,1)}, u32[]{:S(2)}, u32[]{:S(2)}) collective-permute-start(bf16[656,512]{1,0:T(8,128)(2,1)S(1)} %pad_maximum_fusion.refs_8_), channel_id=1, source_target_pairs={{0,1},{1,2},{2,3},{3,0},{4,5},{5,6},{6,7},{7,4},{8,9},{9,10},{10,1... | collective-permute-start | bytes 2015240 | tf_op jit(solution)/shard_map/ppermute | solution.py:415
  3.5 52.8 %collective-permute-start.1 = (bf16[656,512]{1,0:T(8,128)(2,1)S(1)}, bf16[656,512]{1,0:T(8,128)(2,1)}, u32[]{:S(2)}, u32[]{:S(2)}) collective-permute-start(bf16[656,512]{1,0:T(8,128)(2,1)S(1)} %pad_maximum_fusion.refs_8_), channel_id=1, source_target_pairs={{0,2},{1,3},{2,0},{3,1},{4,6},{5,7},{6,4},{7,5},{8,10},{9,11},{10,... | collective-permute-start | bytes 2015240 | tf_op jit(solution)/shard_map/ppermute | solution.py:415
  6.3 50.1 %collective-permute-start.2 = (bf16[656,512]{1,0:T(8,128)(2,1)S(1)}, bf16[656,512]{1,0:T(8,128)(2,1)}, u32[]{:S(2)}, u32[]{:S(2)}) collective-permute-start(bf16[656,512]{1,0:T(8,128)(2,1)S(1)} %pad_maximum_fusion.refs_8_), channel_id=1, source_target_pairs={{0,3},{1,0},{2,1},{3,2},{4,7},{5,4},{6,5},{7,6},{8,11},{9,8},{10,9... | collective-permute-start | bytes 2015240 | tf_op jit(solution)/shard_map/ppermute | solution.py:415
  9.5 1.7 copy-start.8
  9.6 2.3 copy-start.11
  9.6 19.9 %copy-start.12 = (s32[1,32,6]{1,0,2:T(1,128)S(1)}, s32[1,32,6]{1,0,2:T(1,128)}, u32[]{:S(2)}) copy-start(s32[1,32,6]{1,0,2:T(1,128)} %param.18) | copy-start | bytes 2308
  9.6 27.8 %copy-start.10 = (bf16[128,512]{1,0:T(8,128)(2,1)S(1)}, bf16[128,512]{1,0:T(8,128)(2,1)}, u32[]{:S(2)}) copy-start(bf16[128,512]{1,0:T(8,128)(2,1)} %param.28) | copy-start | bytes 393220
  10.5 28.6 %copy-start = (bf16[4096,256]{1,0:T(8,128)(2,1)S(1)}, bf16[4096,256]{1,0:T(8,128)(2,1)}, u32[]{:S(2)}) copy-start(bf16[4096,256]{1,0:T(8,128)(2,1)} %cold.1) | copy-start | bytes 6291460
  10.5 28.6 %copy-start.15 = (s32[1,32]{1,0:T(1,128)S(1)}, s32[1,32]{1,0:T(1,128)}, u32[]{:S(2)}) copy-start(s32[1,32]{1,0:T(1,128)} %param.19) | copy-start | bytes 388
  20.5 16.9 %all-to-all-start.1 = ((s32[32,8,128]{2,1,0:T(8,128)}), s32[32,8,128]{2,1,0:T(8,128)S(1)}, u32[]{:S(2)}, u32[]{:S(2)}) async-start(s32[32,8,128]{2,1,0:T(8,128)} %get-tuple-element.138), calls=%async_computation.1 | async-start | bytes 262144 | tf_op jit(solution)/shard_map/all_to_all | solution.py:456
  173.1 39.9 %copy-start.17 = (bf16[736,256]{1,0:T(8,128)(2,1)S(1)}, bf16[736,256]{1,0:T(8,128)(2,1)}, u32[]{:S(2)}) copy-start(bf16[736,256]{1,0:T(8,128)(2,1)} %get-tuple-element.194) | copy-start | bytes 1130500
  208.6 21.4 %collective-permute-start.6 = (bf16[736,256]{1,0:T(8,128)(2,1)}, bf16[736,256]{1,0:T(8,128)(2,1)S(1)}, u32[]{:S(2)}, u32[]{:S(2)}) collective-permute-start(bf16[736,256]{1,0:T(8,128)(2,1)} %get-tuple-element.208), channel_id=1, source_target_pairs={{0,1},{1,2},{2,3},{3,0},{4,5},{5,6},{6,7},{7,4},{8,9},{9,10},{10,1... | collective-permute-start | bytes 1130504 | tf_op jit(solution)/shard_map/ppermute | solution.py:367
  209.4 20.6 %collective-permute-start.7 = (bf16[736,256]{1,0:T(8,128)(2,1)}, bf16[736,256]{1,0:T(8,128)(2,1)S(1)}, u32[]{:S(2)}, u32[]{:S(2)}) collective-permute-start(bf16[736,256]{1,0:T(8,128)(2,1)} %get-tuple-element.209), channel_id=1, source_target_pairs={{0,2},{1,3},{2,0},{3,1},{4,6},{5,7},{6,4},{7,5},{8,10},{9,11},{10,... | collective-permute-start | bytes 1130504 | tf_op jit(solution)/shard_map/ppermute | solution.py:367
  210.3 20.6 %collective-permute-start.8 = (bf16[736,256]{1,0:T(8,128)(2,1)}, bf16[736,256]{1,0:T(8,128)(2,1)S(1)}, u32[]{:S(2)}, u32[]{:S(2)}) collective-permute-start(bf16[736,256]{1,0:T(8,128)(2,1)} %get-tuple-element.210), channel_id=1, source_target_pairs={{0,3},{1,0},{2,1},{3,2},{4,7},{5,4},{6,5},{7,6},{8,11},{9,8},{10,9... | collective-permute-start | bytes 1130504 | tf_op jit(solution)/shard_map/ppermute | solution.py:367
  212.2 33.7 %collective-permute-start.3 = (bf16[736,256]{1,0:T(8,128)(2,1)S(1)}, bf16[736,256]{1,0:T(8,128)(2,1)S(1)}, u32[]{:S(2)}, u32[]{:S(2)}) collective-permute-start(bf16[736,256]{1,0:T(8,128)(2,1)S(1)} %get-tuple-element.193), channel_id=1, source_target_pairs={{0,1},{1,2},{2,3},{3,0},{4,5},{5,6},{6,7},{7,4},{8,9},{9,10},{10,1... | collective-permute-start | bytes 1130504 | tf_op jit(solution)/shard_map/ppermute | solution.py:367
  213.0 33.0 %collective-permute-start.4 = (bf16[736,256]{1,0:T(8,128)(2,1)S(1)}, bf16[736,256]{1,0:T(8,128)(2,1)S(1)}, u32[]{:S(2)}, u32[]{:S(2)}) collective-permute-start(bf16[736,256]{1,0:T(8,128)(2,1)S(1)} %copy-done.17), channel_id=1, source_target_pairs={{0,2},{1,3},{2,0},{3,1},{4,6},{5,7},{6,4},{7,5},{8,10},{9,11},{10,... | collective-permute-start | bytes 1130504 | tf_op jit(solution)/shard_map/ppermute | solution.py:367
  230.0 16.6 %copy-start.2 = (bf16[736,256]{1,0:T(8,128)(2,1)}, bf16[736,256]{1,0:T(8,128)(2,1)S(1)}, u32[]{:S(2)}) copy-start(bf16[736,256]{1,0:T(8,128)(2,1)S(1)} %collective-permute-done.6.refs_5_) | copy-start | bytes 1130500
  230.0 16.6 %collective-permute-start.5 = (bf16[736,256]{1,0:T(8,128)(2,1)}, bf16[736,256]{1,0:T(8,128)(2,1)S(1)}, u32[]{:S(2)}, u32[]{:S(2)}) collective-permute-start(bf16[736,256]{1,0:T(8,128)(2,1)} %get-tuple-element.195), channel_id=1, source_target_pairs={{0,3},{1,0},{2,1},{3,2},{4,7},{5,4},{6,5},{7,6},{8,11},{9,8},{10,9... | collective-permute-start | bytes 1130504 | tf_op jit(solution)/shard_map/ppermute | solution.py:367
  230.0 16.6 %copy-start.3 = (bf16[736,256]{1,0:T(8,128)(2,1)}, bf16[736,256]{1,0:T(8,128)(2,1)S(1)}, u32[]{:S(2)}) copy-start(bf16[736,256]{1,0:T(8,128)(2,1)S(1)} %collective-permute-done.7.refs_6_) | copy-start | bytes 1130500
  230.9 15.7 %copy-start.4 = (bf16[736,256]{1,0:T(8,128)(2,1)}, bf16[736,256]{1,0:T(8,128)(2,1)S(1)}, u32[]{:S(2)}) copy-start(bf16[736,256]{1,0:T(8,128)(2,1)S(1)} %collective-permute-done.8.refs_7_) | copy-start | bytes 1130500
  245.9 0.8 copy-start.5
  245.9 0.9 copy-start.6
  246.6 0.8 copy-start.7
  253.2 27.5 %copy-start.9 = (f32[64,512]{1,0:T(8,128)S(1)}, f32[64,512]{1,0:T(8,128)}, u32[]{:S(2)}) copy-start(f32[64,512]{1,0:T(8,128)} %get-tuple-element.217) | copy-start | bytes 393220
  253.2 27.5 %all-to-all-start.3 = ((bf16[128,40,128]{2,1,0:T(8,128)(2,1)}), bf16[128,40,128]{2,1,0:T(8,128)(2,1)S(1)}, u32[]{:S(2)}, u32[]{:S(2)}) async-start(bf16[128,40,128]{2,1,0:T(8,128)(2,1)} %bitcast.93), calls=%async_computation.3 | async-start | bytes 2621440 | tf_op jit(solution)/shard_map/all_to_all | solution.py:509
  280.7 11.4 %copy-start.16 = (f32[128]{0:T(128)S(1)}, f32[128]{0:T(128)}, u32[]{:S(2)}) copy-start(f32[128]{0:T(128)} %param.29) | copy-start | bytes 1540
  281.9 8.0 %collective-permute-start.10 = (f32[256,128]{1,0:T(8,128)S(1)}, f32[256,128]{1,0:T(8,128)S(1)}, u32[]{:S(2)}, u32[]{:S(2)}) collective-permute-start(f32[256,128]{1,0:T(8,128)S(1)} %get-tuple-element.250), channel_id=1, source_target_pairs={{0,2},{1,3},{2,0},{3,1},{4,6},{5,7},{6,4},{7,5},{8,10},{9,11},{10,... | collective-permute-start | bytes 393224 | tf_op jit(solution)/shard_map/ppermute | solution.py:367
  283.0 7.2 %collective-permute-start.11 = (f32[256,128]{1,0:T(8,128)S(1)}, f32[256,128]{1,0:T(8,128)S(1)}, u32[]{:S(2)}, u32[]{:S(2)}) collective-permute-start(f32[256,128]{1,0:T(8,128)S(1)} %get-tuple-element.249), channel_id=1, source_target_pairs={{0,3},{1,0},{2,1},{3,2},{4,7},{5,4},{6,5},{7,6},{8,11},{9,8},{10,9... | collective-permute-start | bytes 393224 | tf_op jit(solution)/shard_map/ppermute | solution.py:367
  285.2 6.9 %collective-permute-start.9 = (f32[256,128]{1,0:T(8,128)S(1)}, f32[256,128]{1,0:T(8,128)S(1)}, u32[]{:S(2)}, u32[]{:S(2)}) collective-permute-start(f32[256,128]{1,0:T(8,128)S(1)} %get-tuple-element.248), channel_id=1, source_target_pairs={{0,1},{1,2},{2,3},{3,0},{4,5},{5,6},{6,7},{7,4},{8,9},{9,10},{10,1... | collective-permute-start | bytes 393224 | tf_op jit(solution)/shard_map/ppermute | solution.py:367

commit v5 on v4

--- a/solution.py
+++ b/solution.py
@@ -135,21 +135,26 @@
     return tuple(out.reshape(nodes) for out in outs)
 
 
+TOGETHER = 4
+
+
 def pack_kernel(first, slot_count, blocks, counts, prefix, need, cold, out, left, right):
-    r = pl.program_id(0)
     rows = out.shape[1]
     at = lax.broadcasted_iota(jnp.int32, (BLK, BLK), 0)
-    for k in range(slot_count):
-        begin = prefix[r * slot_count + k]
-        place = need[0, k : k + 1, :] - begin
-        place = jnp.where(counts[r] > k, place, -1)
-        picks = jnp.where(at == place, 1.0, 0.0).astype(jnp.bfloat16)
-        origin = pl.multiple_of(blocks[r * slot_count + k] * BLK, BLK)
-        value = jnp.dot(picks, cold[pl.ds(origin, BLK), :], preferred_element_type=jnp.float32)
-        left[pl.ds(begin, BLK), :] = value[:, :LANES]
-        right[pl.ds(begin, BLK), :] = value[:, LANES:]
-    out[0, :, :LANES] = left[first : first + rows, :].astype(out.dtype)
-    out[0, :, LANES:] = right[first : first + rows, :].astype(out.dtype)
+    for n in range(TOGETHER):
+        r = pl.program_id(0) * TOGETHER + n
+        for k in range(slot_count):
+            begin = prefix[r * slot_count + k]
+            place = need[n, k : k + 1, :] - begin
+            place = jnp.where(counts[r] > k, place, -1)
+            picks = jnp.where(at == place, 1.0, 0.0).astype(jnp.bfloat16)
+            origin = pl.multiple_of(blocks[r * slot_count + k] * BLK, BLK)
+            value = jnp.dot(picks, cold[pl.ds(origin, BLK), :], preferred_element_type=jnp.float32)
+            left[n, pl.ds(begin, BLK), :] = value[:, :LANES]
+            right[n, pl.ds(begin, BLK), :] = value[:, LANES:]
+    for n in range(TOGETHER):
+        out[n, :, :LANES] = left[n, first : first + rows, :].astype(out.dtype)
+        out[n, :, LANES:] = right[n, first : first + rows, :].astype(out.dtype)
 
 
 def pack_needed(blocks, counts, prefix, need, cold, first, rows):
@@ -158,17 +163,17 @@
     slot_count = blocks.shape[0] // groups
     return pl.pallas_call(
         functools.partial(pack_kernel, first, slot_count),
-        grid=(groups,),
+        grid=(groups // TOGETHER,),
         out_shape=jax.ShapeDtypeStruct((groups, rows, cols), cold.dtype),
         in_specs=[
             pl.BlockSpec(memory_space=pltpu.SMEM),
             pl.BlockSpec(memory_space=pltpu.SMEM),
             pl.BlockSpec(memory_space=pltpu.SMEM),
-            pl.BlockSpec((1,) + need.shape[1:], lambda r: (r, 0, 0)),
+            pl.BlockSpec((TOGETHER,) + need.shape[1:], lambda r: (r, 0, 0)),
             pl.BlockSpec(memory_space=pltpu.VMEM),
         ],
-        out_specs=pl.BlockSpec((1, rows, cols), lambda r: (r, 0, 0)),
-        scratch_shapes=[pltpu.VMEM((slot_count * BLK + BLK, LANES), jnp.float32)] * 2,
+        out_specs=pl.BlockSpec((TOGETHER, rows, cols), lambda r: (r, 0, 0)),
+        scratch_shapes=[pltpu.VMEM((TOGETHER, slot_count * BLK + BLK, LANES), jnp.float32)] * 2,
         name="pack_needed",
     )(blocks, counts, prefix, need, cold)
 
@@ -248,7 +253,7 @@
 
 
 CHUNK = 1024
-DEPTH = 4
+DEPTH = 12
 
 
 def gather_kernel(columns, source_count, dest, extent, *refs):
@@ -291,7 +296,7 @@
             table[pl.ds(row + 1, 16, stride=2), :] = value[:, LANES:]
             return inner
 
-        lax.fori_loop(0, CHUNK // 16, widen, 0, unroll=4)
+        lax.fori_loop(0, CHUNK // 16, widen, 0, unroll=8)
 
         @pl.when(c + DEPTH < chunks)
         def _():

time: 294 us -> 276 us (0.939)
  Pallas kernels: 92.5 us -> 75 us
    pallas_call x1, Pallas kernels: 17.2 us -> 8.27 us  [pack_needed(): pl.pallas_call(functools.partial(pack_kernel, first, slot_count), grid=(g...]
    pallas_call x2, Pallas kernels: 54.3 us -> 45.8 us  [gather_rows(): pl.pallas_call(functools.partial(gather_kernel, len(index), len(sources))...]
  transfers between devices with their start and end apart: 14 -> 14, of which waited for: 8 -> 8; matrix products, arithmetic and copies ran while one was open for 3% -> 3% of each run, Pallas kernels for 11% -> 8%
where the time goes in v5:
time: 276 us; the launch traced here: 275 us
  blocking collectives  97.3 us (35%)
  Pallas kernels  75 us (27%)
  waiting for transfers between devices  59.3 us (21%)
  starting transfers between devices  29.7 us (11%)
  other arithmetic  6.28 us (2%)
  local copies, waits for them, and re-layouts  4.39 us (2%)
    all_to_all x1, blocking collectives, exchange(): lax.all_to_all(outgoing, 'grp', split_axis=0, concat_axis=0, tiled=True)  97.3 us
    pallas_call x2, Pallas kernels, gather_rows(): pl.pallas_call(functools.partial(gather_kernel, len(index), len(sources))...  45.8 us
    ppermute x9, waiting for transfers between devices, send_round(): received.append(lax.ppermute(chunks[step], 'feat', ring))  38.5 us
    all_to_all x1, waiting for transfers between devices, per_device(): lax.all_to_all(send_rows, ('grp', 'feat'), split_axis=0, concat_axis=0, t...  20.8 us
    ppermute x9, starting transfers between devices, send_round(): received.append(lax.ppermute(chunks[step], 'feat', ring))  9.57 us
    all_to_all x1, starting transfers between devices, per_device(): lax.all_to_all(notes, 'grp', split_axis=0, concat_axis=0, tiled=True)  8.34 us
    pallas_call x1, Pallas kernels, pack_needed(): pl.pallas_call(functools.partial(pack_kernel, first, slot_count), grid=(g...  8.27 us
    pallas_call x1, Pallas kernels, mark_rows(): pl.pallas_call(mark_kernel, out_shape=(jax.ShapeDtypeStruct((groups, slot...  7.35 us
  transfers between devices with their start and end apart: 14, of which 8 were waited for; matrix products, arithmetic and copies ran while one was open for 3% of the time, Pallas kernels for 8%

profile of v5, /device:TPU:0, one launch (start us, length us, event | category | flops | bytes accessed | tf_op | source)
XLA Modules:
  0.0 275.3 jit_solution(10428935987851224066)
XLA Ops:
  0.0 0.7 fusion.66
  0.7 1.1 pad_maximum_fusion.refs_8_
  1.9 1.7 collective-permute-start
  3.5 2.7 collective-permute-start.1
  6.3 1.4 collective-permute-start.2
  9.6 0.9 fusion.12
  11.2 0.7 fusion.20.before
  13.2 7.4 %mark_rows.1 = (s32[32,8,128]{2,1,0:T(8,128)}, bf16[136,192]{1,0:T(8,128)(2,1)}) custom-call(s32[242,128]{1,0:T(8,128)} %add_bitcast_fusion.refs, bf16[192,192]{1,0:T(8,128)(2,1)} %fusion.20.before, f32[8,192]{1,0:T(8,128)} %broadcast_in_dim.25.owners, s32[32,2,128]{2,1,0:T(2,128)} %reshape.256.extras), custom_call_target="tpu_custom_call" | custom-call | tf_op jit(solution)/shard_map/mark_rows/pallas_call | solution.py:79
  20.5 8.3 %all-to-all-start.1 = ((s32[32,8,128]{2,1,0:T(8,128)}), s32[32,8,128]{2,1,0:T(8,128)S(1)}, u32[]{:S(2)}, u32[]{:S(2)}) async-start(s32[32,8,128]{2,1,0:T(8,128)} %get-tuple-element.138), calls=%async_computation.1 | async-start | bytes 262144 | tf_op jit(solution)/shard_map/all_to_all | solution.py:461
  29.6 0.7 reshape.252.blocks
  30.3 7.1 %remap.1 = (s32[22,128]{1,0:T(8,128)S(1)}, s32[22,128]{1,0:T(8,128)}, s32[22,128]{1,0:T(8,128)}, s32[22,128]{1,0:T(8,128)}, s32[22,128]{1,0:T(8,128)}, /*index=5...) custom-call(s32[242,128]{1,0:T(8,128)} %add_bitcast_fusion.refs, ...), custom_call_target="tpu_custom_call" | custom-call | tf_op jit(solution)/shard_map/remap/pallas_call | solution.py:128
  37.8 0.7 slice_reduce_fusion
  39.1 8.3 %pack_needed.3 = bf16[32,480,256]{2,1,0:T(8,128)(2,1)} custom-call(s32[192]{0:T(256)} %reshape.252.blocks, s32[32]{0:T(128)S(1)} %bitcast.111, s32[192]{0:T(256)S(1)} %reshape_squeeze.3.prefix, s32[32,8,128]{2,1,0:T(8,128)S(1)} %all-to-all-done.1.need, bf16[4096,256]{1,0:T(8,128)(2,1)S(1)} %copy-done), custom_call_target="tpu_custom_call" | custom-call | tf_op jit(solution)/shard_map/pack_needed/pallas_call | solution.py:164
  47.4 97.3 %all_to_all.20 = bf16[32,480,256]{2,1,0:T(8,128)(2,1)} all-to-all(bf16[32,480,256]{2,1,0:T(8,128)(2,1)} %pack_needed.3), channel_id=1, replica_groups=mesh['grp'=32,'feat'=4] {'grp'}, dimensions={0} | all-to-all | bytes 15728640 | tf_op jit(solution)/shard_map/all_to_all | solution.py:480
  144.7 15.4 %conditional.1 = (bf16[736,256]{1,0:T(8,128)(2,1)S(1)}, bf16[736,256]{1,0:T(8,128)(2,1)S(1)}, bf16[736,256]{1,0:T(8,128)(2,1)}, bf16[736,256]{1,0:T(8,128)(2,1)}, bf16[9216,256]{1,0:T(8,128)(2,1)}) conditional(s32[]{:T(128)} %convert_element_type.73, (s32[2816]{0:T(1024)S(1)}, s32[1]{0:T(128)}, s32[2816]{0:T(1024)S(1)}, bf16[16384,256]{1,0:T(8,128)(2,1)}, ...), branch_computations={%region_5.6_spmd, %region_6.7_spmd} | conditional | bytes 9440296 | solution.py:500
  145.3 14.6 %branch_0_fun.1 = (bf16[736,256]{1,0:T(8,128)(2,1)S(1)}, bf16[736,256]{1,0:T(8,128)(2,1)S(1)}, bf16[736,256]{1,0:T(8,128)(2,1)}, bf16[736,256]{1,0:T(8,128)(2,1)}) custom-call(s32[2816]{0:T(1024)S(1)} %get-tuple-element.35.dest, s32[1]{0:T(128)} %get-tuple-element.36.extent, s32[2816]{0:T(1024)S(1)} %get-tuple-element.37.refs_0_, ...), custom_call_target="tpu_custom_call" | custom-call | tf_op jit(solution)/shard_map/cond/branch_0_fun/pallas_call | solution.py:337
  160.0 31.3 %shard_map.136 = (bf16[736,256]{1,0:T(8,128)(2,1)}, bf16[736,256]{1,0:T(8,128)(2,1)}, bf16[736,256]{1,0:T(8,128)(2,1)}, bf16[736,256]{1,0:T(8,128)(2,1)}) custom-call(s32[2816]{0:T(1024)S(1)} %add_multiply_fusion.dest, s32[1]{0:T(128)} %bitcast.24.extent, s32[2816]{0:T(1024)} %bitcast.101, s32[2816]{0:T(1024)} %bitcast.102, s32[2816]{0:T(1024)} %bitcast.103, ...), custom_call_target="tpu_custom_call" | custom-call | tf_op jit(solution)/shard_map/pallas_call | solution.py:337
  192.0 0.9 collective-permute-start.7
  192.8 1.9 collective-permute-start.8
  194.7 0.8 collective-permute-start.3
  195.5 2.1 collective-permute-start.4
  197.6 15.0 %collective-permute-done.6.refs_5_ = bf16[736,256]{1,0:T(8,128)(2,1)S(1)} collective-permute-done((bf16[736,256]{1,0:T(8,128)(2,1)}, bf16[736,256]{1,0:T(8,128)(2,1)S(1)}, u32[]{:S(2)}, u32[]{:S(2)}) %collective-permute-start.6) | collective-permute-done | bytes 376864 | tf_op jit(solution)/shard_map/ppermute | solution.py:372
  212.5 0.9 collective-permute-done.8.refs_7_
  213.4 15.0 %collective-permute-done.3.refs_1_ = bf16[736,256]{1,0:T(8,128)(2,1)S(1)} collective-permute-done((bf16[736,256]{1,0:T(8,128)(2,1)S(1)}, bf16[736,256]{1,0:T(8,128)(2,1)S(1)}, u32[]{:S(2)}, u32[]{:S(2)}) %collective-permute-start.3) | collective-permute-done | bytes 376864 | tf_op jit(solution)/shard_map/ppermute | solution.py:372
  229.9 5.8 %layer_one.1 = (bf16[32,4,40,128]{3,2,1,0:T(8,128)(2,1)}, f32[64,512]{1,0:T(8,128)}) custom-call(s32[1]{0:T(128)} %bitcast.23.me, s32[32]{0:T(128)} %fusion.70.base, bf16[736,256]{1,0:T(8,128)(2,1)S(1)} %get-tuple-element.192.refs_0_, bf16[736,256]{1,0:T(8,128)(2,1)} %copy-done.5, bf16[736,256]{1,0:T(8,128)(2,1)} %copy-done.6, bf16[736,256]{1,0:T(8,128)(2,1)} %copy-done.7, ...), custom_call_target="tpu_custom_call" | custom-call | tf_op jit(solution)/shard_map/layer_one/pallas_call | solution.py:237
  235.7 5.9 %all-to-all-start.3 = ((bf16[128,40,128]{2,1,0:T(8,128)(2,1)}), bf16[128,40,128]{2,1,0:T(8,128)(2,1)S(1)}, u32[]{:S(2)}, u32[]{:S(2)}) async-start(bf16[128,40,128]{2,1,0:T(8,128)(2,1)} %bitcast.93), calls=%async_computation.3 | async-start | bytes 2621440 | tf_op jit(solution)/shard_map/all_to_all | solution.py:514
  242.4 20.8 %all-to-all-done.3 = bf16[128,40,128]{2,1,0:T(8,128)(2,1)S(1)} async-done(((bf16[128,40,128]{2,1,0:T(8,128)(2,1)}), bf16[128,40,128]{2,1,0:T(8,128)(2,1)S(1)}, u32[]{:S(2)}, u32[]{:S(2)}) %all-to-all-start.3) | async-done | bytes 1310752 | tf_op jit(solution)/shard_map/all_to_all | solution.py:514
  263.2 1.1 fusion.17
  264.4 1.2 collective-permute-start.10
  265.6 2.2 collective-permute-start.11
  267.7 4.6 %collective-permute-done.10 = f32[256,128]{1,0:T(8,128)S(1)} collective-permute-done((f32[256,128]{1,0:T(8,128)S(1)}, f32[256,128]{1,0:T(8,128)S(1)}, u32[]{:S(2)}, u32[]{:S(2)}) %collective-permute-start.10) | collective-permute-done | bytes 131104 | tf_op jit(solution)/shard_map/ppermute | solution.py:372
  272.7 1.9 collective-permute-done.9
  (88 shorter events, 9.4 us)
Async XLA Ops:
  0.0 7.7 %copy-start.14 = (s32[2560,1]{0,1:T(1,128)S(1)}, s32[2560,1]{0,1:T(1,128)}, u32[]{:S(2)}) copy-start(s32[2560,1]{0,1:T(1,128)} %param.22) | copy-start | bytes 30724
  1.8 8.7 %copy-start.1 = (bf16[656,512]{1,0:T(8,128)(2,1)}, bf16[656,512]{1,0:T(8,128)(2,1)S(1)}, u32[]{:S(2)}) copy-start(bf16[656,512]{1,0:T(8,128)(2,1)S(1)} %pad_maximum_fusion.refs_8_) | copy-start | bytes 2015236
  1.9 7.7 %copy-start.13 = (s32[2560]{0:T(1024)S(1)}, s32[2560]{0:T(1024)}, u32[]{:S(2)}) copy-start(s32[2560]{0:T(1024)} %param.23) | copy-start | bytes 30724
  1.9 45.5 %collective-permute-start = (bf16[656,512]{1,0:T(8,128)(2,1)S(1)}, bf16[656,512]{1,0:T(8,128)(2,1)}, u32[]{:S(2)}, u32[]{:S(2)}) collective-permute-start(bf16[656,512]{1,0:T(8,128)(2,1)S(1)} %pad_maximum_fusion.refs_8_), channel_id=1, source_target_pairs={{0,1},{1,2},{2,3},{3,0},{4,5},{5,6},{6,7},{7,4},{8,9},{9,10},{10,1... | collective-permute-start | bytes 2015240 | tf_op jit(solution)/shard_map/ppermute | solution.py:420
  3.5 43.8 %collective-permute-start.1 = (bf16[656,512]{1,0:T(8,128)(2,1)S(1)}, bf16[656,512]{1,0:T(8,128)(2,1)}, u32[]{:S(2)}, u32[]{:S(2)}) collective-permute-start(bf16[656,512]{1,0:T(8,128)(2,1)S(1)} %pad_maximum_fusion.refs_8_), channel_id=1, source_target_pairs={{0,2},{1,3},{2,0},{3,1},{4,6},{5,7},{6,4},{7,5},{8,10},{9,11},{10,... | collective-permute-start | bytes 2015240 | tf_op jit(solution)/shard_map/ppermute | solution.py:420
  6.3 41.1 %collective-permute-start.2 = (bf16[656,512]{1,0:T(8,128)(2,1)S(1)}, bf16[656,512]{1,0:T(8,128)(2,1)}, u32[]{:S(2)}, u32[]{:S(2)}) collective-permute-start(bf16[656,512]{1,0:T(8,128)(2,1)S(1)} %pad_maximum_fusion.refs_8_), channel_id=1, source_target_pairs={{0,3},{1,0},{2,1},{3,2},{4,7},{5,4},{6,5},{7,6},{8,11},{9,8},{10,9... | collective-permute-start | bytes 2015240 | tf_op jit(solution)/shard_map/ppermute | solution.py:420
  9.5 1.7 copy-start.8
  9.6 2.3 copy-start.11
  9.6 19.9 %copy-start.12 = (s32[1,32,6]{1,0,2:T(1,128)S(1)}, s32[1,32,6]{1,0,2:T(1,128)}, u32[]{:S(2)}) copy-start(s32[1,32,6]{1,0,2:T(1,128)} %param.18) | copy-start | bytes 2308
  9.6 27.8 %copy-start.10 = (bf16[128,512]{1,0:T(8,128)(2,1)S(1)}, bf16[128,512]{1,0:T(8,128)(2,1)}, u32[]{:S(2)}) copy-start(bf16[128,512]{1,0:T(8,128)(2,1)} %param.28) | copy-start | bytes 393220
  10.5 28.6 %copy-start = (bf16[4096,256]{1,0:T(8,128)(2,1)S(1)}, bf16[4096,256]{1,0:T(8,128)(2,1)}, u32[]{:S(2)}) copy-start(bf16[4096,256]{1,0:T(8,128)(2,1)} %cold.1) | copy-start | bytes 6291460
  10.5 28.6 %copy-start.15 = (s32[1,32]{1,0:T(1,128)S(1)}, s32[1,32]{1,0:T(1,128)}, u32[]{:S(2)}) copy-start(s32[1,32]{1,0:T(1,128)} %param.19) | copy-start | bytes 388
  20.5 16.9 %all-to-all-start.1 = ((s32[32,8,128]{2,1,0:T(8,128)}), s32[32,8,128]{2,1,0:T(8,128)S(1)}, u32[]{:S(2)}, u32[]{:S(2)}) async-start(s32[32,8,128]{2,1,0:T(8,128)} %get-tuple-element.138), calls=%async_computation.1 | async-start | bytes 262144 | tf_op jit(solution)/shard_map/all_to_all | solution.py:461
  160.0 35.5 %copy-start.17 = (bf16[736,256]{1,0:T(8,128)(2,1)S(1)}, bf16[736,256]{1,0:T(8,128)(2,1)}, u32[]{:S(2)}) copy-start(bf16[736,256]{1,0:T(8,128)(2,1)} %get-tuple-element.194) | copy-start | bytes 1130500
  191.3 21.2 %collective-permute-start.6 = (bf16[736,256]{1,0:T(8,128)(2,1)}, bf16[736,256]{1,0:T(8,128)(2,1)S(1)}, u32[]{:S(2)}, u32[]{:S(2)}) collective-permute-start(bf16[736,256]{1,0:T(8,128)(2,1)} %get-tuple-element.208), channel_id=1, source_target_pairs={{0,1},{1,2},{2,3},{3,0},{4,5},{5,6},{6,7},{7,4},{8,9},{9,10},{10,1... | collective-permute-start | bytes 1130504 | tf_op jit(solution)/shard_map/ppermute | solution.py:372
  192.0 20.6 %collective-permute-start.7 = (bf16[736,256]{1,0:T(8,128)(2,1)}, bf16[736,256]{1,0:T(8,128)(2,1)S(1)}, u32[]{:S(2)}, u32[]{:S(2)}) collective-permute-start(bf16[736,256]{1,0:T(8,128)(2,1)} %get-tuple-element.209), channel_id=1, source_target_pairs={{0,2},{1,3},{2,0},{3,1},{4,6},{5,7},{6,4},{7,5},{8,10},{9,11},{10,... | collective-permute-start | bytes 1130504 | tf_op jit(solution)/shard_map/ppermute | solution.py:372
  192.8 20.6 %collective-permute-start.8 = (bf16[736,256]{1,0:T(8,128)(2,1)}, bf16[736,256]{1,0:T(8,128)(2,1)S(1)}, u32[]{:S(2)}, u32[]{:S(2)}) collective-permute-start(bf16[736,256]{1,0:T(8,128)(2,1)} %get-tuple-element.210), channel_id=1, source_target_pairs={{0,3},{1,0},{2,1},{3,2},{4,7},{5,4},{6,5},{7,6},{8,11},{9,8},{10,9... | collective-permute-start | bytes 1130504 | tf_op jit(solution)/shard_map/ppermute | solution.py:372
  194.7 33.7 %collective-permute-start.3 = (bf16[736,256]{1,0:T(8,128)(2,1)S(1)}, bf16[736,256]{1,0:T(8,128)(2,1)S(1)}, u32[]{:S(2)}, u32[]{:S(2)}) collective-permute-start(bf16[736,256]{1,0:T(8,128)(2,1)S(1)} %get-tuple-element.193), channel_id=1, source_target_pairs={{0,1},{1,2},{2,3},{3,0},{4,5},{5,6},{6,7},{7,4},{8,9},{9,10},{10,1... | collective-permute-start | bytes 1130504 | tf_op jit(solution)/shard_map/ppermute | solution.py:372
  195.5 33.0 %collective-permute-start.4 = (bf16[736,256]{1,0:T(8,128)(2,1)S(1)}, bf16[736,256]{1,0:T(8,128)(2,1)S(1)}, u32[]{:S(2)}, u32[]{:S(2)}) collective-permute-start(bf16[736,256]{1,0:T(8,128)(2,1)S(1)} %copy-done.17), channel_id=1, source_target_pairs={{0,2},{1,3},{2,0},{3,1},{4,6},{5,7},{6,4},{7,5},{8,10},{9,11},{10,... | collective-permute-start | bytes 1130504 | tf_op jit(solution)/shard_map/ppermute | solution.py:372
  212.5 16.6 %copy-start.2 = (bf16[736,256]{1,0:T(8,128)(2,1)}, bf16[736,256]{1,0:T(8,128)(2,1)S(1)}, u32[]{:S(2)}) copy-start(bf16[736,256]{1,0:T(8,128)(2,1)S(1)} %collective-permute-done.6.refs_5_) | copy-start | bytes 1130500
  212.5 16.6 %collective-permute-start.5 = (bf16[736,256]{1,0:T(8,128)(2,1)}, bf16[736,256]{1,0:T(8,128)(2,1)S(1)}, u32[]{:S(2)}, u32[]{:S(2)}) collective-permute-start(bf16[736,256]{1,0:T(8,128)(2,1)} %get-tuple-element.195), channel_id=1, source_target_pairs={{0,3},{1,0},{2,1},{3,2},{4,7},{5,4},{6,5},{7,6},{8,11},{9,8},{10,9... | collective-permute-start | bytes 1130504 | tf_op jit(solution)/shard_map/ppermute | solution.py:372
  212.5 16.6 %copy-start.3 = (bf16[736,256]{1,0:T(8,128)(2,1)}, bf16[736,256]{1,0:T(8,128)(2,1)S(1)}, u32[]{:S(2)}) copy-start(bf16[736,256]{1,0:T(8,128)(2,1)S(1)} %collective-permute-done.7.refs_6_) | copy-start | bytes 1130500
  213.4 15.7 %copy-start.4 = (bf16[736,256]{1,0:T(8,128)(2,1)}, bf16[736,256]{1,0:T(8,128)(2,1)S(1)}, u32[]{:S(2)}) copy-start(bf16[736,256]{1,0:T(8,128)(2,1)S(1)} %collective-permute-done.8.refs_7_) | copy-start | bytes 1130500
  228.5 0.8 copy-start.5
  228.5 0.9 copy-start.6
  229.1 0.8 copy-start.7
  235.7 27.5 %copy-start.9 = (f32[64,512]{1,0:T(8,128)S(1)}, f32[64,512]{1,0:T(8,128)}, u32[]{:S(2)}) copy-start(f32[64,512]{1,0:T(8,128)} %get-tuple-element.217) | copy-start | bytes 393220
  235.7 27.5 %all-to-all-start.3 = ((bf16[128,40,128]{2,1,0:T(8,128)(2,1)}), bf16[128,40,128]{2,1,0:T(8,128)(2,1)S(1)}, u32[]{:S(2)}, u32[]{:S(2)}) async-start(bf16[128,40,128]{2,1,0:T(8,128)(2,1)} %bitcast.93), calls=%async_computation.3 | async-start | bytes 2621440 | tf_op jit(solution)/shard_map/all_to_all | solution.py:514
  263.2 11.4 %copy-start.16 = (f32[128]{0:T(128)S(1)}, f32[128]{0:T(128)}, u32[]{:S(2)}) copy-start(f32[128]{0:T(128)} %param.29) | copy-start | bytes 1540
  264.4 8.0 %collective-permute-start.10 = (f32[256,128]{1,0:T(8,128)S(1)}, f32[256,128]{1,0:T(8,128)S(1)}, u32[]{:S(2)}, u32[]{:S(2)}) collective-permute-start(f32[256,128]{1,0:T(8,128)S(1)} %get-tuple-element.250), channel_id=1, source_target_pairs={{0,2},{1,3},{2,0},{3,1},{4,6},{5,7},{6,4},{7,5},{8,10},{9,11},{10,... | collective-permute-start | bytes 393224 | tf_op jit(solution)/shard_map/ppermute | solution.py:372
  265.6 7.2 %collective-permute-start.11 = (f32[256,128]{1,0:T(8,128)S(1)}, f32[256,128]{1,0:T(8,128)S(1)}, u32[]{:S(2)}, u32[]{:S(2)}) collective-permute-start(f32[256,128]{1,0:T(8,128)S(1)} %get-tuple-element.249), channel_id=1, source_target_pairs={{0,3},{1,0},{2,1},{3,2},{4,7},{5,4},{6,5},{7,6},{8,11},{9,8},{10,9... | collective-permute-start | bytes 393224 | tf_op jit(solution)/shard_map/ppermute | solution.py:372
  267.7 6.9 %collective-permute-start.9 = (f32[256,128]{1,0:T(8,128)S(1)}, f32[256,128]{1,0:T(8,128)S(1)}, u32[]{:S(2)}, u32[]{:S(2)}) collective-permute-start(f32[256,128]{1,0:T(8,128)S(1)} %get-tuple-element.248), channel_id=1, source_target_pairs={{0,1},{1,2},{2,3},{3,0},{4,5},{5,6},{6,7},{7,4},{8,9},{9,10},{10,1... | collective-permute-start | bytes 393224 | tf_op jit(solution)/shard_map/ppermute | solution.py:372

commit v6 on v5

--- a/solution.py
+++ b/solution.py
@@ -2,6 +2,7 @@
 
 import jax
 import jax.numpy as jnp
+import numpy as np
 from jax import lax
 from jax.experimental import pallas as pl
 from jax.experimental.pallas import tpu as pltpu
@@ -21,15 +22,17 @@
     groups = notes.shape[0]
     slot_count = owner_rows // groups
     acc[...] = jnp.zeros_like(acc)
-    high = lax.broadcasted_iota(jnp.int32, (owner_rows, LANES), 0)
+    high = lax.broadcasted_iota(jnp.int32, (owner_rows, LANES), 0).astype(jnp.bfloat16)
     low = lax.broadcasted_iota(jnp.int32, (LANES, LANES), 0)
+    low_half = low.astype(jnp.bfloat16)
+    one, zero = jnp.bfloat16(1.0), jnp.bfloat16(0.0)
 
     def count(g, carry):
         tall, wide = [], []
         for j in range(2):
             cold = refs[pl.ds(2 * g + j, 1), :] - HOT
-            tall.append(jnp.where(high == cold >> 7, 1.0, 0.0).astype(jnp.bfloat16))
-            wide.append(jnp.where(low == (cold & 127), 1.0, 0.0).astype(jnp.bfloat16))
+            tall.append(jnp.where(high == (cold >> 7).astype(jnp.bfloat16), one, zero))
+            wide.append(jnp.where(low_half == (cold & 127).astype(jnp.bfloat16), one, zero))
         acc[...] += lax.dot_general(
             jnp.concatenate(tall, axis=1),
             jnp.concatenate(wide, axis=1),
@@ -73,9 +76,10 @@
 
 def mark_rows(refs, extras, slot_count, groups):
     rows = groups * slot_count
-    at = jnp.arange(rows, dtype=jnp.int32)
+    at = np.arange(rows)
     before = (at[:, None] // slot_count == at[None, :] // slot_count) & (at[None, :] < at[:, None])
-    owners = jnp.broadcast_to((at // slot_count).astype(jnp.float32)[None, :], (8, rows))
+    before = jnp.asarray(before.astype(np.float32), jnp.bfloat16)
+    owners = jnp.asarray(np.broadcast_to((at // slot_count)[None, :], (8, rows)), jnp.float32)
     return pl.pallas_call(
         mark_kernel,
         out_shape=(
@@ -86,13 +90,14 @@
         out_specs=(pl.BlockSpec(memory_space=pltpu.VMEM),) * 2,
         scratch_shapes=[pltpu.VMEM((rows, LANES), jnp.float32)],
         name="mark_rows",
-    )(refs, before.astype(jnp.bfloat16), owners, extras)
+    )(refs, before, owners, extras)
 
 
 def remap_kernel(spill, groups, refs, look, *outs):
     owner_rows = look.shape[1]
-    high = lax.broadcasted_iota(jnp.int32, (owner_rows, LANES), 0)
+    high = lax.broadcasted_iota(jnp.int32, (owner_rows, LANES), 0).astype(jnp.bfloat16)
     low = lax.broadcasted_iota(jnp.int32, (LANES, LANES), 0)
+    one, zero = jnp.bfloat16(1.0), jnp.bfloat16(0.0)
     rows = outs[0].shape[0]
     table = look[...]
     for k, out in enumerate(outs):
@@ -100,7 +105,7 @@
         def lookup(g, carry, k=k, out=out):
             names = [refs[pl.ds(k * rows + 2 * g + j, 1), :] for j in range(2)]
             tall = [
-                jnp.where(high == (name - HOT) >> 7, 1.0, 0.0).astype(jnp.bfloat16)
+                jnp.where(high == ((name - HOT) >> 7).astype(jnp.bfloat16), one, zero)
                 for name in names
             ]
             found = jnp.dot(
@@ -226,7 +231,7 @@
             out[o, f] = hidden[f, pl.ds(base[o], slots), :].astype(out.dtype)
         return carry
 
-    lax.fori_loop(0, groups, send, 0)
+    lax.fori_loop(0, groups, send, 0, unroll=4)
 
 
 def layer_one(me, base, own, mean, weights, groups, slots, own_part):
@@ -313,7 +318,7 @@
         acc[pl.ds(pl.multiple_of(dest[i], 2), 2), :] = rows[0]
         return carry
 
-    lax.fori_loop(0, nodes, node, 0, unroll=8)
+    lax.fori_loop(0, nodes, node, 0, unroll=16)
 
     for f, out in enumerate(outs):
         first = 2 * f * out.shape[0]

time: 276 us -> 272 us (0.986)
  Pallas kernels: 75 us -> 72.1 us
where the time goes in v6:
time: 272 us; the launch traced here: 271 us
  blocking collectives  97.2 us (36%)
  Pallas kernels  72.1 us (27%)
  waiting for transfers between devices  59.3 us (22%)
  starting transfers between devices  29.8 us (11%)
  other arithmetic  5.54 us (2%)
  local copies, waits for them, and re-layouts  3.66 us (1%)
    all_to_all x1, blocking collectives, exchange(): lax.all_to_all(outgoing, 'grp', split_axis=0, concat_axis=0, tiled=True)  97.2 us
    pallas_call x2, Pallas kernels, gather_rows(): pl.pallas_call(functools.partial(gather_kernel, len(index), len(sources))...  43.9 us
    ppermute x9, waiting for transfers between devices, send_round(): received.append(lax.ppermute(chunks[step], 'feat', ring))  38.5 us
    all_to_all x1, waiting for transfers between devices, per_device(): lax.all_to_all(send_rows, ('grp', 'feat'), split_axis=0, concat_axis=0, t...  20.8 us
    ppermute x9, starting transfers between devices, send_round(): received.append(lax.ppermute(chunks[step], 'feat', ring))  9.75 us
    all_to_all x1, starting transfers between devices, per_device(): lax.all_to_all(notes, 'grp', split_axis=0, concat_axis=0, tiled=True)  8.33 us
    pallas_call x1, Pallas kernels, pack_needed(): pl.pallas_call(functools.partial(pack_kernel, first, slot_count), grid=(g...  8.27 us
    pallas_call x1, Pallas kernels, mark_rows(): pl.pallas_call(mark_kernel, out_shape=(jax.ShapeDtypeStruct((groups, slot...  7.1 us
  transfers between devices with their start and end apart: 14, of which 8 were waited for; matrix products, arithmetic and copies ran while one was open for 3% of the time, Pallas kernels for 8%

profile of v6, /device:TPU:0, one launch (start us, length us, event | category | flops | bytes accessed | tf_op | source)
XLA Modules:
  0.0 271.0 jit_solution(7612458532618833906)
XLA Ops:
  0.0 0.7 fusion.64
  0.7 1.1 pad_maximum_fusion.refs_8_
  1.9 1.7 collective-permute-start
  3.5 2.7 %collective-permute-start.1 = (bf16[656,512]{1,0:T(8,128)(2,1)S(1)}, bf16[656,512]{1,0:T(8,128)(2,1)}, u32[]{:S(2)}, u32[]{:S(2)}) collective-permute-start(bf16[656,512]{1,0:T(8,128)(2,1)S(1)} %pad_maximum_fusion.refs_8_), channel_id=1, source_target_pairs={{0,2},{1,3},{2,0},{3,1},{4,6},{5,7},{6,4},{7,5},{8,10},{9,11},{10,... | collective-permute-start | bytes 2015240 | tf_op jit(solution)/shard_map/ppermute | solution.py:425
  6.3 1.4 collective-permute-start.2
  9.6 0.9 fusion.12
  11.9 7.1 %mark_rows.1 = (s32[32,8,128]{2,1,0:T(8,128)}, bf16[136,192]{1,0:T(8,128)(2,1)}) custom-call(s32[242,128]{1,0:T(8,128)} %add_bitcast_fusion.refs, bf16[192,192]{1,0:T(8,128)(2,1)} %constant.142.clone.before, f32[8,192]{1,0:T(8,128)} %constant.143.clone.owners, s32[32,2,128]{2,1,0:T(2,128)} %reshape.207.extras), custom_call_target="tpu_custom_call" | custom-call | tf_op jit(solution)/shard_map/mark_rows/pallas_call | solution.py:83
  19.0 8.3 %all-to-all-start.1 = ((s32[32,8,128]{2,1,0:T(8,128)}), s32[32,8,128]{2,1,0:T(8,128)S(1)}, u32[]{:S(2)}, u32[]{:S(2)}) async-start(s32[32,8,128]{2,1,0:T(8,128)} %get-tuple-element.138), calls=%async_computation.1 | async-start | bytes 262144 | tf_op jit(solution)/shard_map/all_to_all | solution.py:466
  28.6 6.5 %remap.1 = (s32[22,128]{1,0:T(8,128)S(1)}, s32[22,128]{1,0:T(8,128)}, s32[22,128]{1,0:T(8,128)}, s32[22,128]{1,0:T(8,128)}, s32[22,128]{1,0:T(8,128)}, /*index=5...) custom-call(s32[242,128]{1,0:T(8,128)} %add_bitcast_fusion.refs, ...), custom_call_target="tpu_custom_call" | custom-call | tf_op jit(solution)/shard_map/remap/pallas_call | solution.py:133
  35.6 0.7 slice_reduce_fusion
  36.8 8.3 %pack_needed.3 = bf16[32,480,256]{2,1,0:T(8,128)(2,1)} custom-call(s32[192]{0:T(256)} %reshape.203.blocks, s32[32]{0:T(128)S(1)} %bitcast.111, s32[192]{0:T(256)S(1)} %reshape_squeeze.3.prefix, s32[32,8,128]{2,1,0:T(8,128)S(1)} %all-to-all-done.1.need, bf16[4096,256]{1,0:T(8,128)(2,1)S(1)} %copy-done), custom_call_target="tpu_custom_call" | custom-call | tf_op jit(solution)/shard_map/pack_needed/pallas_call | solution.py:169
  45.1 97.2 %all_to_all.20 = bf16[32,480,256]{2,1,0:T(8,128)(2,1)} all-to-all(bf16[32,480,256]{2,1,0:T(8,128)(2,1)} %pack_needed.3), channel_id=1, replica_groups=mesh['grp'=32,'feat'=4] {'grp'}, dimensions={0} | all-to-all | bytes 15728640 | tf_op jit(solution)/shard_map/all_to_all | solution.py:485
  142.4 14.4 %conditional.1 = (bf16[736,256]{1,0:T(8,128)(2,1)S(1)}, bf16[736,256]{1,0:T(8,128)(2,1)S(1)}, bf16[736,256]{1,0:T(8,128)(2,1)}, bf16[736,256]{1,0:T(8,128)(2,1)}, bf16[9216,256]{1,0:T(8,128)(2,1)}) conditional(s32[]{:T(128)} %convert_element_type.61, (s32[2816]{0:T(1024)S(1)}, s32[1]{0:T(128)}, s32[2816]{0:T(1024)S(1)}, bf16[16384,256]{1,0:T(8,128)(2,1)}, ...), branch_computations={%region_5.6_spmd, %region_6.7_spmd} | conditional | bytes 9440296 | solution.py:505
  143.0 13.8 %branch_0_fun.1 = (bf16[736,256]{1,0:T(8,128)(2,1)S(1)}, bf16[736,256]{1,0:T(8,128)(2,1)S(1)}, bf16[736,256]{1,0:T(8,128)(2,1)}, bf16[736,256]{1,0:T(8,128)(2,1)}) custom-call(s32[2816]{0:T(1024)S(1)} %get-tuple-element.35.dest, s32[1]{0:T(128)} %get-tuple-element.36.extent, s32[2816]{0:T(1024)S(1)} %get-tuple-element.37.refs_0_, ...), custom_call_target="tpu_custom_call" | custom-call | tf_op jit(solution)/shard_map/cond/branch_0_fun/pallas_call | solution.py:342
  156.8 30.1 %shard_map.154 = (bf16[736,256]{1,0:T(8,128)(2,1)}, bf16[736,256]{1,0:T(8,128)(2,1)}, bf16[736,256]{1,0:T(8,128)(2,1)}, bf16[736,256]{1,0:T(8,128)(2,1)}) custom-call(s32[2816]{0:T(1024)S(1)} %add_multiply_fusion.dest, s32[1]{0:T(128)} %bitcast.24.extent, s32[2816]{0:T(1024)} %bitcast.101, s32[2816]{0:T(1024)} %bitcast.102, s32[2816]{0:T(1024)} %bitcast.103, ...), custom_call_target="tpu_custom_call" | custom-call | tf_op jit(solution)/shard_map/pallas_call | solution.py:342
  186.9 0.8 collective-permute-start.6
  187.7 0.9 collective-permute-start.7
  188.6 1.9 collective-permute-start.8
  190.5 0.7 collective-permute-start.3
  191.2 2.1 collective-permute-start.4
  193.3 15.0 %collective-permute-done.6.refs_5_ = bf16[736,256]{1,0:T(8,128)(2,1)S(1)} collective-permute-done((bf16[736,256]{1,0:T(8,128)(2,1)}, bf16[736,256]{1,0:T(8,128)(2,1)S(1)}, u32[]{:S(2)}, u32[]{:S(2)}) %collective-permute-start.6) | collective-permute-done | bytes 376864 | tf_op jit(solution)/shard_map/ppermute | solution.py:377
  208.3 0.9 collective-permute-done.8.refs_7_
  209.2 15.0 %collective-permute-done.3.refs_1_ = bf16[736,256]{1,0:T(8,128)(2,1)S(1)} collective-permute-done((bf16[736,256]{1,0:T(8,128)(2,1)S(1)}, bf16[736,256]{1,0:T(8,128)(2,1)S(1)}, u32[]{:S(2)}, u32[]{:S(2)}) %collective-permute-start.3) | collective-permute-done | bytes 376864 | tf_op jit(solution)/shard_map/ppermute | solution.py:377
  225.6 5.7 %layer_one.1 = (bf16[32,4,40,128]{3,2,1,0:T(8,128)(2,1)}, f32[64,512]{1,0:T(8,128)}) custom-call(s32[1]{0:T(128)} %bitcast.23.me, s32[32]{0:T(128)} %fusion.68.base, bf16[736,256]{1,0:T(8,128)(2,1)S(1)} %get-tuple-element.192.refs_0_, bf16[736,256]{1,0:T(8,128)(2,1)} %copy-done.5, bf16[736,256]{1,0:T(8,128)(2,1)} %copy-done.6, bf16[736,256]{1,0:T(8,128)(2,1)} %copy-done.7, ...), custom_call_target="tpu_custom_call" | custom-call | tf_op jit(solution)/shard_map/layer_one/pallas_call | solution.py:242
  231.3 5.9 %all-to-all-start.3 = ((bf16[128,40,128]{2,1,0:T(8,128)(2,1)}), bf16[128,40,128]{2,1,0:T(8,128)(2,1)S(1)}, u32[]{:S(2)}, u32[]{:S(2)}) async-start(bf16[128,40,128]{2,1,0:T(8,128)(2,1)} %bitcast.93), calls=%async_computation.3 | async-start | bytes 2621440 | tf_op jit(solution)/shard_map/all_to_all | solution.py:519
  238.0 20.8 %all-to-all-done.3 = bf16[128,40,128]{2,1,0:T(8,128)(2,1)S(1)} async-done(((bf16[128,40,128]{2,1,0:T(8,128)(2,1)}), bf16[128,40,128]{2,1,0:T(8,128)(2,1)S(1)}, u32[]{:S(2)}, u32[]{:S(2)}) %all-to-all-start.3) | async-done | bytes 1310752 | tf_op jit(solution)/shard_map/all_to_all | solution.py:519
  258.9 1.1 fusion.17
  260.0 1.2 collective-permute-start.10
  261.2 2.2 collective-permute-start.11
  263.4 4.6 %collective-permute-done.10 = f32[256,128]{1,0:T(8,128)S(1)} collective-permute-done((f32[256,128]{1,0:T(8,128)S(1)}, f32[256,128]{1,0:T(8,128)S(1)}, u32[]{:S(2)}, u32[]{:S(2)}) %collective-permute-start.10) | collective-permute-done | bytes 131104 | tf_op jit(solution)/shard_map/ppermute | solution.py:377
  268.4 1.9 collective-permute-done.9
  270.3 0.7 fusion.27
  (85 shorter events, 8.1 us)
Async XLA Ops:
  0.0 7.7 %copy-start.14 = (s32[2560,1]{0,1:T(1,128)S(1)}, s32[2560,1]{0,1:T(1,128)}, u32[]{:S(2)}) copy-start(s32[2560,1]{0,1:T(1,128)} %param.24) | copy-start | bytes 30724
  1.8 8.7 %copy-start.1 = (bf16[656,512]{1,0:T(8,128)(2,1)}, bf16[656,512]{1,0:T(8,128)(2,1)S(1)}, u32[]{:S(2)}) copy-start(bf16[656,512]{1,0:T(8,128)(2,1)S(1)} %pad_maximum_fusion.refs_8_) | copy-start | bytes 2015236
  1.9 7.7 %copy-start.13 = (s32[2560]{0:T(1024)S(1)}, s32[2560]{0:T(1024)}, u32[]{:S(2)}) copy-start(s32[2560]{0:T(1024)} %param.25) | copy-start | bytes 30724
  1.9 43.3 %collective-permute-start = (bf16[656,512]{1,0:T(8,128)(2,1)S(1)}, bf16[656,512]{1,0:T(8,128)(2,1)}, u32[]{:S(2)}, u32[]{:S(2)}) collective-permute-start(bf16[656,512]{1,0:T(8,128)(2,1)S(1)} %pad_maximum_fusion.refs_8_), channel_id=1, source_target_pairs={{0,1},{1,2},{2,3},{3,0},{4,5},{5,6},{6,7},{7,4},{8,9},{9,10},{10,1... | collective-permute-start | bytes 2015240 | tf_op jit(solution)/shard_map/ppermute | solution.py:425
  3.5 41.6 %collective-permute-start.1 = (bf16[656,512]{1,0:T(8,128)(2,1)S(1)}, bf16[656,512]{1,0:T(8,128)(2,1)}, u32[]{:S(2)}, u32[]{:S(2)}) collective-permute-start(bf16[656,512]{1,0:T(8,128)(2,1)S(1)} %pad_maximum_fusion.refs_8_), channel_id=1, source_target_pairs={{0,2},{1,3},{2,0},{3,1},{4,6},{5,7},{6,4},{7,5},{8,10},{9,11},{10,... | collective-permute-start | bytes 2015240 | tf_op jit(solution)/shard_map/ppermute | solution.py:425
  6.3 38.9 %collective-permute-start.2 = (bf16[656,512]{1,0:T(8,128)(2,1)S(1)}, bf16[656,512]{1,0:T(8,128)(2,1)}, u32[]{:S(2)}, u32[]{:S(2)}) collective-permute-start(bf16[656,512]{1,0:T(8,128)(2,1)S(1)} %pad_maximum_fusion.refs_8_), channel_id=1, source_target_pairs={{0,3},{1,0},{2,1},{3,2},{4,7},{5,4},{6,5},{7,6},{8,11},{9,8},{10,9... | collective-permute-start | bytes 2015240 | tf_op jit(solution)/shard_map/ppermute | solution.py:425
  9.5 1.7 copy-start.8
  9.6 1.6 copy-start.11
  9.6 18.3 %copy-start.12 = (s32[1,32,6]{1,0,2:T(1,128)S(1)}, s32[1,32,6]{1,0,2:T(1,128)}, u32[]{:S(2)}) copy-start(s32[1,32,6]{1,0,2:T(1,128)} %param.20) | copy-start | bytes 2308
  9.6 27.2 %copy-start = (bf16[4096,256]{1,0:T(8,128)(2,1)S(1)}, bf16[4096,256]{1,0:T(8,128)(2,1)}, u32[]{:S(2)}) copy-start(bf16[4096,256]{1,0:T(8,128)(2,1)} %cold.1) | copy-start | bytes 6291460
  10.5 24.6 %copy-start.10 = (bf16[128,512]{1,0:T(8,128)(2,1)S(1)}, bf16[128,512]{1,0:T(8,128)(2,1)}, u32[]{:S(2)}) copy-start(bf16[128,512]{1,0:T(8,128)(2,1)} %param.30) | copy-start | bytes 393220
  10.5 26.3 %copy-start.15 = (s32[1,32]{1,0:T(1,128)S(1)}, s32[1,32]{1,0:T(1,128)}, u32[]{:S(2)}) copy-start(s32[1,32]{1,0:T(1,128)} %param.21) | copy-start | bytes 388
  19.0 16.2 %all-to-all-start.1 = ((s32[32,8,128]{2,1,0:T(8,128)}), s32[32,8,128]{2,1,0:T(8,128)S(1)}, u32[]{:S(2)}, u32[]{:S(2)}) async-start(s32[32,8,128]{2,1,0:T(8,128)} %get-tuple-element.138), calls=%async_computation.1 | async-start | bytes 262144 | tf_op jit(solution)/shard_map/all_to_all | solution.py:466
  156.8 34.4 %copy-start.17 = (bf16[736,256]{1,0:T(8,128)(2,1)S(1)}, bf16[736,256]{1,0:T(8,128)(2,1)}, u32[]{:S(2)}) copy-start(bf16[736,256]{1,0:T(8,128)(2,1)} %get-tuple-element.194) | copy-start | bytes 1130500
  186.9 21.4 %collective-permute-start.6 = (bf16[736,256]{1,0:T(8,128)(2,1)}, bf16[736,256]{1,0:T(8,128)(2,1)S(1)}, u32[]{:S(2)}, u32[]{:S(2)}) collective-permute-start(bf16[736,256]{1,0:T(8,128)(2,1)} %get-tuple-element.208), channel_id=1, source_target_pairs={{0,1},{1,2},{2,3},{3,0},{4,5},{5,6},{6,7},{7,4},{8,9},{9,10},{10,1... | collective-permute-start | bytes 1130504 | tf_op jit(solution)/shard_map/ppermute | solution.py:377
  187.7 20.6 %collective-permute-start.7 = (bf16[736,256]{1,0:T(8,128)(2,1)}, bf16[736,256]{1,0:T(8,128)(2,1)S(1)}, u32[]{:S(2)}, u32[]{:S(2)}) collective-permute-start(bf16[736,256]{1,0:T(8,128)(2,1)} %get-tuple-element.209), channel_id=1, source_target_pairs={{0,2},{1,3},{2,0},{3,1},{4,6},{5,7},{6,4},{7,5},{8,10},{9,11},{10,... | collective-permute-start | bytes 1130504 | tf_op jit(solution)/shard_map/ppermute | solution.py:377
  188.6 20.6 %collective-permute-start.8 = (bf16[736,256]{1,0:T(8,128)(2,1)}, bf16[736,256]{1,0:T(8,128)(2,1)S(1)}, u32[]{:S(2)}, u32[]{:S(2)}) collective-permute-start(bf16[736,256]{1,0:T(8,128)(2,1)} %get-tuple-element.210), channel_id=1, source_target_pairs={{0,3},{1,0},{2,1},{3,2},{4,7},{5,4},{6,5},{7,6},{8,11},{9,8},{10,9... | collective-permute-start | bytes 1130504 | tf_op jit(solution)/shard_map/ppermute | solution.py:377
  190.5 33.7 %collective-permute-start.3 = (bf16[736,256]{1,0:T(8,128)(2,1)S(1)}, bf16[736,256]{1,0:T(8,128)(2,1)S(1)}, u32[]{:S(2)}, u32[]{:S(2)}) collective-permute-start(bf16[736,256]{1,0:T(8,128)(2,1)S(1)} %get-tuple-element.193), channel_id=1, source_target_pairs={{0,1},{1,2},{2,3},{3,0},{4,5},{5,6},{6,7},{7,4},{8,9},{9,10},{10,1... | collective-permute-start | bytes 1130504 | tf_op jit(solution)/shard_map/ppermute | solution.py:377
  191.2 33.0 %collective-permute-start.4 = (bf16[736,256]{1,0:T(8,128)(2,1)S(1)}, bf16[736,256]{1,0:T(8,128)(2,1)S(1)}, u32[]{:S(2)}, u32[]{:S(2)}) collective-permute-start(bf16[736,256]{1,0:T(8,128)(2,1)S(1)} %copy-done.17), channel_id=1, source_target_pairs={{0,2},{1,3},{2,0},{3,1},{4,6},{5,7},{6,4},{7,5},{8,10},{9,11},{10,... | collective-permute-start | bytes 1130504 | tf_op jit(solution)/shard_map/ppermute | solution.py:377
  208.3 16.6 %copy-start.2 = (bf16[736,256]{1,0:T(8,128)(2,1)}, bf16[736,256]{1,0:T(8,128)(2,1)S(1)}, u32[]{:S(2)}) copy-start(bf16[736,256]{1,0:T(8,128)(2,1)S(1)} %collective-permute-done.6.refs_5_) | copy-start | bytes 1130500
  208.3 16.6 %collective-permute-start.5 = (bf16[736,256]{1,0:T(8,128)(2,1)}, bf16[736,256]{1,0:T(8,128)(2,1)S(1)}, u32[]{:S(2)}, u32[]{:S(2)}) collective-permute-start(bf16[736,256]{1,0:T(8,128)(2,1)} %get-tuple-element.195), channel_id=1, source_target_pairs={{0,3},{1,0},{2,1},{3,2},{4,7},{5,4},{6,5},{7,6},{8,11},{9,8},{10,9... | collective-permute-start | bytes 1130504 | tf_op jit(solution)/shard_map/ppermute | solution.py:377
  208.3 16.6 %copy-start.3 = (bf16[736,256]{1,0:T(8,128)(2,1)}, bf16[736,256]{1,0:T(8,128)(2,1)S(1)}, u32[]{:S(2)}) copy-start(bf16[736,256]{1,0:T(8,128)(2,1)S(1)} %collective-permute-done.7.refs_6_) | copy-start | bytes 1130500
  209.2 15.7 %copy-start.4 = (bf16[736,256]{1,0:T(8,128)(2,1)}, bf16[736,256]{1,0:T(8,128)(2,1)S(1)}, u32[]{:S(2)}) copy-start(bf16[736,256]{1,0:T(8,128)(2,1)S(1)} %collective-permute-done.8.refs_7_) | copy-start | bytes 1130500
  224.2 0.8 copy-start.5
  224.2 0.9 copy-start.6
  224.9 0.8 copy-start.7
  231.3 27.5 %copy-start.9 = (f32[64,512]{1,0:T(8,128)S(1)}, f32[64,512]{1,0:T(8,128)}, u32[]{:S(2)}) copy-start(f32[64,512]{1,0:T(8,128)} %get-tuple-element.217) | copy-start | bytes 393220
  231.3 27.5 %all-to-all-start.3 = ((bf16[128,40,128]{2,1,0:T(8,128)(2,1)}), bf16[128,40,128]{2,1,0:T(8,128)(2,1)S(1)}, u32[]{:S(2)}, u32[]{:S(2)}) async-start(bf16[128,40,128]{2,1,0:T(8,128)(2,1)} %bitcast.93), calls=%async_computation.3 | async-start | bytes 2621440 | tf_op jit(solution)/shard_map/all_to_all | solution.py:519
  258.9 11.4 %copy-start.16 = (f32[128]{0:T(128)S(1)}, f32[128]{0:T(128)}, u32[]{:S(2)}) copy-start(f32[128]{0:T(128)} %param.31) | copy-start | bytes 1540
  260.0 8.0 %collective-permute-start.10 = (f32[256,128]{1,0:T(8,128)S(1)}, f32[256,128]{1,0:T(8,128)S(1)}, u32[]{:S(2)}, u32[]{:S(2)}) collective-permute-start(f32[256,128]{1,0:T(8,128)S(1)} %get-tuple-element.250), channel_id=1, source_target_pairs={{0,2},{1,3},{2,0},{3,1},{4,6},{5,7},{6,4},{7,5},{8,10},{9,11},{10,... | collective-permute-start | bytes 393224 | tf_op jit(solution)/shard_map/ppermute | solution.py:377
  261.2 7.2 %collective-permute-start.11 = (f32[256,128]{1,0:T(8,128)S(1)}, f32[256,128]{1,0:T(8,128)S(1)}, u32[]{:S(2)}, u32[]{:S(2)}) collective-permute-start(f32[256,128]{1,0:T(8,128)S(1)} %get-tuple-element.249), channel_id=1, source_target_pairs={{0,3},{1,0},{2,1},{3,2},{4,7},{5,4},{6,5},{7,6},{8,11},{9,8},{10,9... | collective-permute-start | bytes 393224 | tf_op jit(solution)/shard_map/ppermute | solution.py:377
  263.4 6.9 %collective-permute-start.9 = (f32[256,128]{1,0:T(8,128)S(1)}, f32[256,128]{1,0:T(8,128)S(1)}, u32[]{:S(2)}, u32[]{:S(2)}) collective-permute-start(f32[256,128]{1,0:T(8,128)S(1)} %get-tuple-element.248), channel_id=1, source_target_pairs={{0,1},{1,2},{2,3},{3,0},{4,5},{5,6},{6,7},{7,4},{8,9},{9,10},{10,1... | collective-permute-start | bytes 393224 | tf_op jit(solution)/shard_map/ppermute | solution.py:377
